TPU v7x, 768 devices: a whole 4x8x12 slice. The times are simulated.
768 devices in a mesh: dp: 24 (over x_hi, z), fsdp: 16 (over y, core), query: 2 (over x_lo).
Axes of the slice: x: 4 (x_hi: 2, x_lo: 2; x = x_hi * 2 + x_lo), y: 8, z: 12, core: 2. Of those that a mesh axis runs over, the one named last changes fastest.
Arguments:
- queries: bfloat16 [16, 6144, 1024], P('fsdp', ('dp', 'query')), may hold values from -40 to 40
- passages: bfloat16 [16, 12288, 1024], P('fsdp', ('dp', 'query')), may hold values from -6 to 6
- head_weight: bfloat16 [1024, 1024], P('fsdp'), may hold values from -0.1875 to 0.1875
- positives: int32 [16, 6144], P('fsdp', ('dp', 'query')), may hold values from 0 to 12287
- negative_ids: int32 [16, 48, 12], P('fsdp', ('dp', 'query')), may hold values from 0 to 95, as said below
- negative_count: int32 [16, 48], P('fsdp', ('dp', 'query')), may hold values from 4 to 12, as said below
Outputs:
- query_loss: float32 [16, 6144], P('fsdp', ('dp', 'query'))
Inputs may be any that keep to these rules, and one draw needn't show every extreme that they name: `negative_ids`: the 12 entries of a query block are distinct passage blocks of its index shard; only the first negative_count of them are live. `negative_count`: in every aligned run of 8 query blocks one has exactly 12 live entries.
All inputs are finite; a program needn't handle non-finite values.
Results may differ from a plain program's by a relative error of at most 0.0048.
Values may be sent and summed in bfloat16 or wider, within the bound.
No kernel may reach another device: no remote copies, remote signals or barrier semaphores. Data moves between devices by JAX's collectives and lax.ppermute only.
A program may use at most 64 MiB of HBM per device.

v0:
```python
import jax
import jax.numpy as jnp
from jax import lax
from jax.sharding import PartitionSpec as P

BLOCK = 128


masked_floor = -1e30


def joined(part, axis, combine):
    gathered = jax.tree.map(lambda a: lax.all_gather(a, axis), part)

    def take(source):
        return jax.tree.map(lambda a: lax.dynamic_index_in_dim(a, source, 0, False), gathered)

    return lax.fori_loop(
        1, lax.axis_size(axis), lambda source, state: combine(state, take(source)), take(0)
    )


def combine_stats(first, second):
    top = jnp.maximum(first[0], second[0])
    total = first[1] * jnp.exp(first[0] - top) + second[1] * jnp.exp(second[0] - top)
    return (top, total, first[2] + second[2])


def local(queries, passages, head_weight, positives, negative_ids, negative_count):
    query_rows = queries[0]
    passage_rows = passages[0]
    feature_width = query_rows.shape[1]
    scale_factor = feature_width ** (-0.5)
    query_count = query_rows.shape[0]
    shard_rows = lax.all_gather(head_weight, "fsdp", axis=0, tiled=True)
    query_sum = jnp.dot(query_rows, shard_rows, preferred_element_type=jnp.float32)
    passage_sum = jnp.dot(passage_rows, shard_rows, preferred_element_type=jnp.float32)
    query_proj = query_sum.astype(jnp.bfloat16)
    passage_proj = passage_sum.astype(jnp.bfloat16)
    paired = lax.all_gather(passage_proj, "query", axis=0, tiled=True)
    pair_count = paired.shape[0]
    pair_first = lax.axis_index("dp") * pair_count
    tile_count = pair_count // BLOCK
    tile_ids = pair_first // BLOCK + lax.iota(jnp.int32, tile_count)
    listed_ids = negative_ids[0]
    live_slot = lax.broadcasted_iota(jnp.int32, listed_ids.shape, 1) < negative_count[0][:, None]
    listed_ids = jnp.where(live_slot, listed_ids, -1)
    row_lists = jnp.repeat(listed_ids, BLOCK, axis=0)
    targets = positives[0]
    query_piece = lax.all_gather(query_proj, "dp", axis=0, tiled=True)
    list_piece = lax.all_gather(row_lists, "dp", axis=0, tiled=True)
    target_piece = lax.all_gather(targets, "dp", axis=0, tiled=True)
    local_target = target_piece - pair_first
    has_target = (local_target >= 0) & (local_target < pair_count)
    target_rows = jnp.take(paired, jnp.clip(local_target, 0, pair_count - 1), axis=0)
    target_logit = (
        jnp.sum(query_piece.astype(jnp.float32) * target_rows.astype(jnp.float32), axis=1)
        * scale_factor
    )
    target_listed = jnp.any(list_piece == (target_piece // BLOCK)[:, None], axis=1)
    extra = has_target & jnp.logical_not(target_listed)
    block_used = jnp.any(list_piece[:, :, None] == tile_ids[None, None, :], axis=1)
    logits = (
        jnp.einsum("qe,pe->qp", query_piece, paired, preferred_element_type=jnp.float32)
        * scale_factor
    )
    chosen = jnp.repeat(block_used, BLOCK, axis=1)
    masked = jnp.where(chosen, logits, masked_floor)
    part_max = jnp.max(masked, axis=1)
    part_sum = jnp.sum(jnp.where(chosen, jnp.exp(logits - part_max[:, None]), 0.0), axis=1)
    extra_logit = jnp.where(extra, target_logit, masked_floor)
    full_max = jnp.maximum(part_max, extra_logit)
    full_sum = part_sum * jnp.exp(part_max - full_max) + jnp.where(
        extra, jnp.exp(target_logit - full_max), 0.0
    )
    kept_target = jnp.where(has_target, target_logit, 0.0)
    partial_stats = (full_max, full_sum, kept_target)
    own_first = lax.axis_index("dp") * query_count
    merged = joined(partial_stats, "dp", combine_stats)
    own_max = lax.dynamic_slice_in_dim(merged[0], own_first, query_count, 0)
    own_sum = lax.dynamic_slice_in_dim(merged[1], own_first, query_count, 0)
    own_target = lax.dynamic_slice_in_dim(merged[2], own_first, query_count, 0)
    query_loss = own_max + jnp.log(own_sum) - own_target
    return query_loss[None, :]


def solution(mesh):
    in_specs = (
        P("fsdp", ("dp", "query"), None),
        P("fsdp", ("dp", "query"), None),
        P("fsdp", None),
        P("fsdp", ("dp", "query")),
        P("fsdp", ("dp", "query"), None),
        P("fsdp", ("dp", "query")),
    )
    out_specs = P("fsdp", ("dp", "query"))
    return jax.shard_map(local, mesh=mesh, in_specs=in_specs, out_specs=out_specs, check_vma=False)
```

profile of v0, /device:TPU:6, one launch (start us, length us, event | category | flops | bytes accessed | tf_op | source)
XLA Modules:
  0.0 443.0 jit_solution(17594762869970588404)
XLA Ops:
  6.5 0.7 all-gather.8.cloned.1.call-update
  7.3 0.0 all-gather.12.cloned.1.call-start
  7.3 53.8 %all-gather.8.cloned.1.call-done = bf16[1024,1024]{1,0:T(8,128)(2,1)} async-done(((bf16[64,1024]{1,0:T(8,128)(2,1)}), bf16[1024,1024]{1,0:T(8,128)(2,1)}) %all-gather.8.cloned.1.call-update) | async-done | bytes 2097168 | tf_op jit(solution)/shard_map/all_gather | solution.py:35
  61.1 3.1 convolution_convert_fusion
  64.3 0.0 all-gather.10.cloned.1.call-start
  64.3 2.8 convolution_convert_fusion.1
  67.9 58.2 %all-gather = s32[1,3072]{1,0:T(1,128)S(1)} all-gather(s32[1,128]{1,0:T(1,128)S(1)} %copy-done.3), channel_id=2, replica_groups=mesh['dp'=24,'fsdp'=16,'query'=2] {'dp'}, dimensions={1}, use_global_device_ids=true | all-gather | bytes 12800 | tf_op jit(solution)/shard_map/all_gather | solution.py:52
  126.1 0.1 reshape.28
  126.2 54.2 %all_gather.33 = s32[3072,12]{0,1:T(8,128)S(1)} all-gather(s32[128,12]{0,1:T(8,128)S(1)} %reshape.28), channel_id=1, replica_groups=mesh['dp'=24,'fsdp'=16,'query'=2] {'dp'}, dimensions={0}, use_global_device_ids=true | all-gather | bytes 153600 | tf_op jit(solution)/shard_map/all_gather | solution.py:51
  180.4 0.1 compare_reduce_fusion.1
  180.5 0.2 compare_reduce_fusion
  180.8 17.3 %gather_fusion = bf16[3072,1024]{1,0:T(8,128)(2,1)} fusion(bf16[512,1024]{1,0:T(8,128)(2,1)} %all-gather.12.cloned.1.call-done, s32[3072]{0:T(1024)S(1)} %get-tuple-element.209), kind=kCustom, calls=%fused_computation | custom fusion | bytes 12595200 | tf_op jit(solution)/shard_map/jit(_take)/gather | solution.py:55
  198.1 54.6 %all-gather.10.cloned.1.call-done = bf16[3072,1024]{1,0:T(8,128)(2,1)} async-done(((bf16[128,1024]{1,0:T(8,128)(2,1)}), bf16[3072,1024]{1,0:T(8,128)(2,1)}) %all-gather.10.cloned.1.call-update) | async-done | bytes 6291472 | tf_op jit(solution)/shard_map/all_gather | solution.py:50
  252.7 6.7 %multiply_reduce_fusion = f32[3072]{0:T(1024)S(1)} fusion(bf16[3072,1024]{1,0:T(8,128)(2,1)} %all-gather.10.cloned.1.call-done, bf16[3072,1024]{1,0:T(8,128)(2,1)} %gather_fusion, pred[3072]{0:T(1024)(128)(4,1)S(1)} %compare_and_fusion), kind=kLoop, calls=%fused_computation.5 | loop fusion | flops 15725568 | bytes 12598272 | tf_op jit(solution)/shard_map/reduce_sum | solution.py:57
  259.4 3.6 fusion
  263.0 1.3 fusion.1
  264.3 57.5 %all-gather.2 = f32[73728]{0:T(1024)S(1)} all-gather(f32[3072]{0:T(1024)S(1)} %get-tuple-element.206), channel_id=4, replica_groups=mesh['dp'=24,'fsdp'=16,'query'=2] {'dp'}, dimensions={0}, use_global_device_ids=true | all-gather | bytes 307200 | tf_op jit(solution)/shard_map/all_gather | solution.py:13
  321.8 0.1 reshape.40
  321.9 54.7 %all-gather.3 = f32[73728]{0:T(1024)S(1)} all-gather(f32[3072]{0:T(1024)S(1)} %get-tuple-element.202), channel_id=5, replica_groups=mesh['dp'=24,'fsdp'=16,'query'=2] {'dp'}, dimensions={0}, use_global_device_ids=true | all-gather | bytes 307200 | tf_op jit(solution)/shard_map/all_gather | solution.py:13
  376.5 0.1 reshape.41
  376.6 56.5 %all-gather.1 = f32[73728]{0:T(1024)S(1)} all-gather(f32[3072]{0:T(1024)S(1)} %get-tuple-element.207), channel_id=3, replica_groups=mesh['dp'=24,'fsdp'=16,'query'=2] {'dp'}, dimensions={0}, use_global_device_ids=true | all-gather | bytes 307200 | tf_op jit(solution)/shard_map/all_gather | solution.py:13
  433.1 0.1 reshape.39
  433.2 2.7 while.19
  435.9 0.6 subtract_bitcast_fusion
  (115 shorter events, 1.7 us)
Async XLA Ops:
  6.5 54.6 %copy-start = (bf16[1,256,1024]{2,1,0:T(8,128)(2,1)S(1)}, bf16[1,256,1024]{2,1,0:T(8,128)(2,1)}, u32[]{:S(2)}) copy-start(bf16[1,256,1024]{2,1,0:T(8,128)(2,1)} %param.9) | copy-start | bytes 1572868
  6.5 61.3 %copy-start.3 = (s32[1,128]{1,0:T(1,128)S(1)}, s32[1,128]{1,0:T(1,128)}, u32[]{:S(2)}) copy-start(s32[1,128]{1,0:T(1,128)} %param.11) | copy-start | bytes 1540
  6.5 119.6 %copy-start.4 = (s32[1,1,12]{2,1,0:T(1,128)S(1)}, s32[1,1,12]{2,1,0:T(1,128)}, u32[]{:S(2)}) copy-start(s32[1,1,12]{2,1,0:T(1,128)} %param.12) | copy-start | bytes 148
  6.5 54.6 %all-gather.8.cloned.1.call-start = ((), (), s32[]{:S(2)}) async-start(), calls=%async_computation | async-start | bytes 2228224 | tf_op jit(solution)/shard_map/all_gather | solution.py:35
  7.3 173.5 %all-gather.12.cloned.1.call-start = ((), (), s32[]{:S(2)}) async-start(), calls=%async_computation.2 | async-start | bytes 1572864 | tf_op jit(solution)/shard_map/all_gather | solution.py:40
  64.3 188.4 %all-gather.10.cloned.1.call-start = ((), (), s32[]{:S(2)}) async-start(), calls=%async_computation.1 | async-start | bytes 6553600 | tf_op jit(solution)/shard_map/all_gather | solution.py:50
  198.1 61.3 %copy-start.1 = (bf16[512,1024]{1,0:T(8,128)(2,1)S(1)}, bf16[512,1024]{1,0:T(8,128)(2,1)}, u32[]{:S(2)}) copy-start(bf16[512,1024]{1,0:T(8,128)(2,1)} %all-gather.12.cloned.1.call-done) | copy-start | bytes 3145732
  252.7 6.7 %copy-start.2 = (bf16[3072,1024]{1,0:T(8,128)(2,1)S(1)}, bf16[3072,1024]{1,0:T(8,128)(2,1)}, u32[]{:S(2)}) copy-start(bf16[3072,1024]{1,0:T(8,128)(2,1)} %all-gather.10.cloned.1.call-done) | copy-start | bytes 18874372
Sparse Core Ops, SparseCore 0:
  9.8 51.2 all-gather.7
  64.4 30.2 all-gather.11
  98.3 154.3 all-gather.9
where the time goes:
time: 443 us
  blocking collectives  281 us (63%)
  waiting for transfers between devices  109 us (25%)
  local copies, waits for them, and re-layouts  18.6 us (4%)
  between operations  13.9 us (3%)
  matrix products  9.51 us (2%)
  other arithmetic  9.42 us (2%)
    all_gather x3, blocking collectives, joined(): gathered = jax.tree.map(lambda a: lax.all_gather(a, axis), part)  169 us
    all_gather x1, blocking collectives, local(): target_piece = lax.all_gather(targets, 'dp', axis=0, tiled=True)  58.2 us
    all_gather x1, waiting for transfers between devices, local(): query_piece = lax.all_gather(query_proj, 'dp', axis=0, tiled=True)  54.6 us
    all_gather x1, blocking collectives, local(): list_piece = lax.all_gather(row_lists, 'dp', axis=0, tiled=True)  54.2 us
    all_gather x1, waiting for transfers between devices, local(): shard_rows = lax.all_gather(head_weight, 'fsdp', axis=0, tiled=True)  53.8 us
    gather x1, local copies, waits for them, and re-layouts, local(): jnp.take(paired, jnp.clip(local_target, 0, pair_count - 1), axis=0)  17.3 us
  transfers between devices with their start and end apart: 3, of which 2 were waited for; matrix products, arithmetic and copies ran while one was open for 5% of the time, Pallas kernels for 0%

commit v1 on v0

v1 whole, which is shorter than its diff:
```python
import functools

import jax
import jax.numpy as jnp
from jax import lax
from jax.experimental import pallas as pl
from jax.experimental.pallas import tpu as pltpu
from jax.sharding import Mesh
from jax.sharding import PartitionSpec as P

BLOCK = 128
FLOOR = -1e30
ROW = ("xh", "xl")
NT = (((1,), (1,)), ((), ()))
VMEM_BYTES = 48 * 1024 * 1024


def passage_kernel(passages, head, proj, full):
    cores, steps, depth, _ = head.shape
    for y in range(steps):
        for c in range(cores):
            full[pl.ds((y * cores + c) * depth, depth), :] = head[c, y]
    shards, rows, _ = passages.shape
    for s in range(shards):
        proj[pl.ds(s * rows, rows), :] = jnp.dot(
            passages[s], full[...], preferred_element_type=jnp.float32
        ).astype(proj.dtype)


def query_kernel(scale, used, queries, full, proj, target, out, logits):
    step = pl.program_id(0)
    query_rows = queries.shape[0]
    count = query_rows // BLOCK
    tiles = proj.shape[0] // BLOCK
    query_proj = jnp.dot(
        queries[...], full[...], preferred_element_type=jnp.float32
    ).astype(jnp.bfloat16)
    logits[...] = lax.dot_general(proj[...], query_proj, NT, preferred_element_type=jnp.float32)
    sub = lax.broadcasted_iota(jnp.int32, (BLOCK, BLOCK), 0)
    for b in range(count):
        lanes = pl.ds(b * BLOCK, BLOCK)
        wanted = target[b]
        found = jnp.zeros((BLOCK, BLOCK), jnp.float32)
        for j in range(tiles):
            tile = logits[pl.ds(j * BLOCK, BLOCK), lanes]
            found = found + jnp.where(sub == wanted - j * BLOCK, tile, 0.0)
        found = jnp.sum(found, axis=0, keepdims=True) * scale

        def peak(j, top):
            def live(top):
                tile = logits[pl.ds(pl.multiple_of(j * BLOCK, BLOCK), BLOCK), lanes]
                return jnp.maximum(top, jnp.max(tile.reshape(BLOCK // 8, 8, BLOCK), axis=0))

            return lax.cond(used[step * count + b, j] > 0, live, lambda t: t, top)

        top = lax.fori_loop(0, tiles, peak, jnp.full((8, BLOCK), FLOOR, jnp.float32))
        top = jnp.max(top, axis=0, keepdims=True)

        def total(j, acc):
            def live(acc):
                tile = logits[pl.ds(pl.multiple_of(j * BLOCK, BLOCK), BLOCK), lanes]
                part = jnp.exp((tile - top) * scale)
                return acc + jnp.sum(part.reshape(BLOCK // 8, 8, BLOCK), axis=0)

            return lax.cond(used[step * count + b, j] > 0, live, lambda t: t, acc)

        acc = lax.fori_loop(0, tiles, total, jnp.zeros((8, BLOCK), jnp.float32))
        acc = jnp.sum(acc, axis=0, keepdims=True)
        some = acc > 0.0
        lse = jnp.where(some, top * scale + jnp.log(jnp.where(some, acc, 1.0)), FLOOR)
        out[b, 0:1, :] = lse
        out[b, 1:2, :] = found


def local(queries, passages, head, positives, negative_ids, negative_count):
    queries, passages = queries[0], passages[0]
    width = queries.shape[1]
    scale = width ** (-0.5)
    deep, wide = lax.axis_size("z"), lax.axis_size(ROW)
    high = lax.axis_size("xh")
    cores, steps = lax.axis_size("core"), lax.axis_size("y")
    z = lax.axis_index("z")
    rows = passages.shape[0]

    gathered = lax.all_gather(queries, "z", axis=0, tiled=True)

    head = lax.all_to_all(jnp.broadcast_to(head, (steps,) + head.shape), "y", 0, 0)
    met = lax.all_to_all(jnp.broadcast_to(passages, (wide,) + passages.shape), ROW, 0, 0)
    head = lax.all_to_all(jnp.broadcast_to(head, (cores,) + head.shape), "core", 0, 0)

    slots = negative_ids.shape[2]
    live = lax.broadcasted_iota(jnp.int32, (1, slots), 1) < negative_count
    listed = jnp.where(live, negative_ids[0], -1)
    packed = jnp.concatenate(
        [positives, jnp.pad(listed, ((0, 0), (0, BLOCK - slots)), constant_values=-1)], axis=0
    )
    met_lists = lax.all_gather(packed, "z")
    wanted, lists = met_lists[:, 0, :], met_lists[:, 1, :slots]

    run = rows * (wide // high)
    span = run * deep
    upper = wanted // span
    inside = wanted - upper * span - z * run
    target = jnp.where((inside >= 0) & (inside < run), upper * run + inside, -1)
    tiles = rows * wide // BLOCK
    tile = lax.iota(jnp.int32, tiles)
    per_run = run // BLOCK
    tile_id = (tile // per_run) * (span // BLOCK) + z * per_run + tile % per_run
    used = jnp.any(lists[:, :, None] == tile_id[None, None, :], axis=1).astype(jnp.int32)

    vmem = pl.BlockSpec(memory_space=pltpu.VMEM)
    proj, full = pl.pallas_call(
        passage_kernel,
        out_shape=(
            jax.ShapeDtypeStruct((rows * wide, width), jnp.bfloat16),
            jax.ShapeDtypeStruct((width, width), jnp.bfloat16),
        ),
        in_specs=[vmem, vmem],
        out_specs=(vmem, vmem),
        compiler_params=pltpu.CompilerParams(vmem_limit_bytes=VMEM_BYTES),
    )(met, head)

    chunks = 3
    per = deep // chunks
    stats = pl.pallas_call(
        functools.partial(query_kernel, scale),
        out_shape=jax.ShapeDtypeStruct((deep, 2, BLOCK), jnp.float32),
        grid_spec=pltpu.PrefetchScalarGridSpec(
            num_scalar_prefetch=1,
            grid=(chunks,),
            in_specs=[
                pl.BlockSpec((per * BLOCK, width), lambda i, u: (i, 0)),
                vmem,
                vmem,
                pl.BlockSpec((per, 1, BLOCK), lambda i, u: (i, 0, 0)),
            ],
            out_specs=pl.BlockSpec((per, 2, BLOCK), lambda i, u: (i, 0, 0)),
            scratch_shapes=[pltpu.VMEM((rows * wide, per * BLOCK), jnp.float32)],
        ),
        compiler_params=pltpu.CompilerParams(vmem_limit_bytes=VMEM_BYTES),
    )(used, gathered, full, proj, target[:, None, :])

    home = lax.all_to_all(stats, "z", 0, 0)
    logit = jnp.sum(home[:, 1, :], axis=0)
    also_listed = jnp.any(listed[0][:, None] == positives // BLOCK, axis=0)
    extra = jnp.where(also_listed, FLOOR, logit)
    top = jnp.maximum(jnp.max(home[:, 0, :], axis=0), extra)
    total = jnp.sum(jnp.exp(home[:, 0, :] - top), axis=0) + jnp.exp(extra - top)
    return (top + jnp.log(total) - logit)[None, :]


def solution(mesh):
    grid = Mesh(mesh.devices.reshape(2, 12, 8, 2, 2), ("xh", "z", "y", "core", "xl"))
    shard, part = ("y", "core"), ("xh", "z", "xl")
    in_specs = (
        P(shard, part, None),
        P(shard, part, None),
        P(shard, None),
        P(shard, part),
        P(shard, part, None),
        P(shard, part),
    )
    return jax.shard_map(
        local, mesh=grid, in_specs=in_specs, out_specs=P(shard, part), check_vma=False
    )
```

time: 443 us -> 137 us (0.31)
  blocking collectives: 281 us -> 67.7 us
  waiting for transfers between devices: 109 us -> 10.9 us
  Pallas kernels: 0 us -> 19.2 us
  starting transfers between devices: 0.08 us -> 16.3 us
  local copies, waits for them, and re-layouts: 18.6 us -> 5.68 us
  matrix products: 9.51 us -> 0 us
  other arithmetic: 9.42 us -> 1.15 us
    all_gather x5 -> x1, blocking collectives: 281 us -> 32.3 us  [local(): met_lists = lax.all_gather(packed, 'z')]
    all_gather x3 -> x1, waiting for transfers between devices: 108 us -> 0.01 us  [local(): gathered = lax.all_gather(queries, 'z', axis=0, tiled=True)]
    all_to_all x0 -> x2, blocking collectives: none -> 35.4 us  [the longest x1 29.1 us: local(): lax.all_to_all(jnp.broadcast_to(passages, (wide,) + passages.shape), ROW,...]
    pallas_call x0 -> x2, Pallas kernels: none -> 19.2 us  [the longest x1 14.7 us: local(): pl.pallas_call(functools.partial(query_kernel, scale), out_shape=jax.Shap...]
    gather x1 -> x0, local copies, waits for them, and re-layouts: 17.3 us -> none  [local(): jnp.take(paired, jnp.clip(local_target, 0, pair_count - 1), axis=0)]
    all_to_all x0 -> x2, starting transfers between devices: none -> 16.3 us  [the longest x1 9.17 us: local(): home = lax.all_to_all(stats, 'z', 0, 0)]
    all_to_all x0 -> x2, waiting for transfers between devices: none -> 10.1 us  [the longest x1 10.1 us: local(): home = lax.all_to_all(stats, 'z', 0, 0)]
    dot_general x3 -> x0, matrix products: 9.51 us -> none  [the longest x1 3.55 us: local(): jnp.einsum('qe,pe->qp', query_piece, paired, preferred_element_type=jnp.f...]
  transfers between devices with their start and end apart: 3 -> 3, of which waited for: 2 -> 1; matrix products, arithmetic and copies ran while one was open for 5% -> 2% of each run, Pallas kernels for 0% -> 3%
where the time goes in v1:
time: 137 us; the launch traced here: 135 us
  blocking collectives  67.7 us (49%)
  Pallas kernels  19.2 us (14%)
  starting transfers between devices  16.3 us (12%)
  between operations  14.2 us (10%)
  waiting for transfers between devices  10.9 us (8%)
  local copies, waits for them, and re-layouts  5.68 us (4%)
    all_gather x1, blocking collectives, local(): met_lists = lax.all_gather(packed, 'z')  32.3 us
    all_to_all x1, blocking collectives, local(): lax.all_to_all(jnp.broadcast_to(passages, (wide,) + passages.shape), ROW,...  29.1 us
    pallas_call x1, Pallas kernels, local(): pl.pallas_call(functools.partial(query_kernel, scale), out_shape=jax.Shap...  14.7 us
    all_to_all x1, waiting for transfers between devices, local(): home = lax.all_to_all(stats, 'z', 0, 0)  10.1 us
    all_to_all x1, starting transfers between devices, local(): home = lax.all_to_all(stats, 'z', 0, 0)  9.17 us
    all_to_all x1, starting transfers between devices, local(): lax.all_to_all(jnp.broadcast_to(head, (steps,) + head.shape), 'y', 0, 0)  7.1 us
    all_to_all x1, blocking collectives, local(): lax.all_to_all(jnp.broadcast_to(head, (cores,) + head.shape), 'core', 0, 0)  6.34 us
    pallas_call x1, Pallas kernels, local(): pl.pallas_call(passage_kernel, out_shape=(jax.ShapeDtypeStruct((rows * wi...  4.57 us
  transfers between devices with their start and end apart: 3, of which 1 were waited for; matrix products, arithmetic and copies ran while one was open for 2% of the time, Pallas kernels for 3%

profile of v1, /device:TPU:6, one launch (start us, length us, event | category | flops | bytes accessed | tf_op | source)
XLA Modules:
  0.0 135.1 jit_solution(10456217845978804332)
XLA Ops:
  6.5 0.0 all-gather.5.cloned.1.call-start
  6.5 0.7 all-gather.5.cloned.1.call-update
  7.3 1.3 broadcast_in_dim.28
  8.6 0.0 copy-start.2
  8.6 29.1 %all_to_all.20.passages = bf16[4,256,1024]{2,1,0:T(8,128)(2,1)} all-to-all(bf16[4,256,1024]{2,1,0:T(8,128)(2,1)S(1)} %broadcast_in_dim.28), channel_id=1, replica_groups=mesh['xh'=2,'z'=12,'y'=8,'core'=2,'xl'=2] {'xh','xl'}, dimensions={0} | all-to-all | bytes 4194304 | tf_op jit(solution)/shard_map/all_to_all | solution.py:88
  37.6 0.0 copy-done.2
  37.7 1.1 broadcast_in_dim.29
  38.8 7.1 %all-to-all-start.1 = ((bf16[8,64,1024]{2,1,0:T(8,128)(2,1)}), bf16[8,64,1024]{2,1,0:T(8,128)(2,1)S(1)}, u32[]{:S(2)}, u32[]{:S(2)}) async-start(bf16[8,64,1024]{2,1,0:T(8,128)(2,1)} %broadcast_in_dim.29), calls=%async_computation.1 | async-start | bytes 2097152 | tf_op jit(solution)/shard_map/all_to_all | solution.py:87
  46.6 0.0 copy-done.3
  46.6 32.3 %all-gather.2 = s32[12,2,128]{2,1,0:T(2,128)S(1)} all-gather(s32[1,2,128]{2,1,0:T(2,128)S(1)} %fusion.3), channel_id=2, replica_groups=mesh['xh'=2,'z'=12,'y'=8,'core'=2,'xl'=2] {'z'}, dimensions={0}, use_global_device_ids=true | all-gather | bytes 13312 | tf_op jit(solution)/shard_map/all_gather | solution.py:97
  79.0 0.4 compare_reduce_fusion
  79.3 0.1 and_select_fusion.target
  79.4 0.0 all-to-all-done.1
  79.4 0.3 broadcast_in_dim.30
  79.7 6.3 %all_to_all.21.head = bf16[2,8,64,1024]{3,2,1,0:T(8,128)(2,1)} all-to-all(bf16[2,8,64,1024]{3,2,1,0:T(8,128)(2,1)S(1)} %broadcast_in_dim.30), channel_id=1, replica_groups=mesh['xh'=2,'z'=12,'y'=8,'core'=2,'xl'=2] {'core'}, dimensions={0} | all-to-all | bytes 4194304 | tf_op jit(solution)/shard_map/all_to_all | solution.py:89
  86.0 4.6 %shard_map.64 = (bf16[1024,1024]{1,0:T(8,128)(2,1)S(1)}, bf16[1024,1024]{1,0:T(8,128)(2,1)S(1)}) custom-call(bf16[4,256,1024]{2,1,0:T(8,128)(2,1)} %all_to_all.20.passages, bf16[2,8,64,1024]{3,2,1,0:T(8,128)(2,1)} %all_to_all.21.head), custom_call_target="tpu_custom_call" | custom-call | tf_op jit(solution)/shard_map/pallas_call | solution.py:112
  90.6 0.0 copy-start
  90.6 1.4 %copy-done = bf16[1024,1024]{1,0:T(8,128)(2,1)} copy-done((bf16[1024,1024]{1,0:T(8,128)(2,1)}, bf16[1024,1024]{1,0:T(8,128)(2,1)S(1)}, u32[]{:S(2)}) %copy-start) | copy-done | bytes 2097176
  92.0 1.6 %copy-done.1 = bf16[1024,1024]{1,0:T(8,128)(2,1)S(1)} copy-done((bf16[1024,1024]{1,0:T(8,128)(2,1)S(1)}, bf16[1024,1024]{1,0:T(8,128)(2,1)}, u32[]{:S(2)}) %copy-start.1) | copy-done | bytes 2097176
  93.6 14.7 %shard_map.65 = f32[12,2,128]{2,1,0:T(2,128)} custom-call(s32[12,8]{1,0:T(8,128)S(1)} %convert_element_type.3.used, bf16[1536,1024]{1,0:T(8,128)(2,1)} %bitcast.43, bf16[1024,1024]{1,0:T(8,128)(2,1)S(1)} %copy-done.1, bf16[1024,1024]{1,0:T(8,128)(2,1)S(1)} %get-tuple-element.8.proj, s32[12,1,128]{2,1,0:T(1,128)S(1)} %and_select_fusion.target), custom_call_target="tpu_custom_call" | custom-call | tf_op jit(solution)/shard_map/pallas_call | solution.py:125
  108.2 9.2 %all-to-all-start.3 = ((f32[12,2,128]{2,1,0:T(2,128)}), f32[12,2,128]{2,1,0:T(2,128)S(1)}, u32[]{:S(2)}, u32[]{:S(2)}) async-start(f32[12,2,128]{2,1,0:T(2,128)} %shard_map.65), calls=%async_computation.3 | async-start | bytes 24576 | tf_op jit(solution)/shard_map/all_to_all | solution.py:143
  117.4 0.1 compare_reduce_fusion.1
  117.5 10.1 %all-to-all-done.3 = f32[12,2,128]{2,1,0:T(2,128)S(1)} async-done(((f32[12,2,128]{2,1,0:T(2,128)}), f32[12,2,128]{2,1,0:T(2,128)S(1)}, u32[]{:S(2)}, u32[]{:S(2)}) %all-to-all-start.3) | async-done | bytes 12320 | tf_op jit(solution)/shard_map/all_to_all | solution.py:143
  127.7 0.5 fusion.9
  (16 shorter events, 0.1 us)
Async XLA Ops:
  6.5 85.4 %all-gather.5.cloned.1.call-start = ((), (), s32[]{:S(2)}) async-start(), calls=%async_computation.4 | async-start | bytes 3407872 | tf_op jit(solution)/shard_map/all_gather | solution.py:85
  8.6 29.1 %copy-start.2 = (bf16[64,1024]{1,0:T(8,128)(2,1)S(1)}, bf16[64,1024]{1,0:T(8,128)(2,1)}, u32[]{:S(2)}) copy-start(bf16[64,1024]{1,0:T(8,128)(2,1)} %param.8) | copy-start | bytes 393220
  37.6 8.9 %copy-start.4 = (s32[1,1,12]{2,1,0:T(1,128)S(1)}, s32[1,1,12]{2,1,0:T(1,128)}, u32[]{:S(2)}) copy-start(s32[1,1,12]{2,1,0:T(1,128)} %param.10) | copy-start | bytes 148
  37.7 8.9 %copy-start.3 = (s32[1,128]{1,0:T(1,128)S(1)}, s32[1,128]{1,0:T(1,128)}, u32[]{:S(2)}) copy-start(s32[1,128]{1,0:T(1,128)} %param.9) | copy-start | bytes 1540
  38.8 40.6 %all-to-all-start.1 = ((bf16[8,64,1024]{2,1,0:T(8,128)(2,1)}), bf16[8,64,1024]{2,1,0:T(8,128)(2,1)S(1)}, u32[]{:S(2)}, u32[]{:S(2)}) async-start(bf16[8,64,1024]{2,1,0:T(8,128)(2,1)} %broadcast_in_dim.29), calls=%async_computation.1 | async-start | bytes 2097152 | tf_op jit(solution)/shard_map/all_to_all | solution.py:87
  90.6 1.4 %copy-start = (bf16[1024,1024]{1,0:T(8,128)(2,1)}, bf16[1024,1024]{1,0:T(8,128)(2,1)S(1)}, u32[]{:S(2)}) copy-start(bf16[1024,1024]{1,0:T(8,128)(2,1)S(1)} %get-tuple-element.7.full) | copy-start | bytes 6291460
  92.0 1.6 %copy-start.1 = (bf16[1024,1024]{1,0:T(8,128)(2,1)S(1)}, bf16[1024,1024]{1,0:T(8,128)(2,1)}, u32[]{:S(2)}) copy-start(bf16[1024,1024]{1,0:T(8,128)(2,1)} %copy-done) | copy-start | bytes 6291460
  108.2 19.4 %all-to-all-start.3 = ((f32[12,2,128]{2,1,0:T(2,128)}), f32[12,2,128]{2,1,0:T(2,128)S(1)}, u32[]{:S(2)}, u32[]{:S(2)}) async-start(f32[12,2,128]{2,1,0:T(2,128)} %shard_map.65), calls=%async_computation.3 | async-start | bytes 24576 | tf_op jit(solution)/shard_map/all_to_all | solution.py:143
Sparse Core Ops, SparseCore 0:
  9.7 71.2 all-gather.4

commit v2 on v1

v2 whole, which is shorter than its diff:
```python
import functools

import jax
import jax.numpy as jnp
from jax import lax
from jax.experimental import pallas as pl
from jax.experimental.pallas import tpu as pltpu
from jax.sharding import Mesh
from jax.sharding import PartitionSpec as P

BLOCK = 128
FLOOR = -1e30
NT = (((1,), (1,)), ((), ()))
VMEM_BYTES = 24 * 1024 * 1024
PARTS = (512, 1024)


def passage_kernel(core, mine, other, *refs):
    *pieces, full, proj = refs
    steps, depth, _ = mine.shape
    here = core[0]
    for y in range(steps):
        first = pl.multiple_of((2 * y + here) * depth, depth)
        second = pl.multiple_of((2 * y + 1 - here) * depth, depth)
        full[pl.ds(first, depth), :] = mine[y]
        full[pl.ds(second, depth), :] = other[y]
    rows = pieces[0].shape[0]
    for s, piece in enumerate(pieces):
        proj[pl.ds(s * rows, rows), :] = jnp.dot(
            piece[...], full[...], preferred_element_type=jnp.float32
        ).astype(proj.dtype)


def query_kernel(scale, used, queries, full, proj, target, out, query_buf, full_buf, logits, sems):
    rows = [pl.ds(sum(PARTS[:i]), part) for i, part in enumerate(PARTS)]
    fetch = [
        pltpu.make_async_copy(queries.at[r], query_buf.at[r], sems.at[i])
        for i, r in enumerate(rows)
    ]
    load = pltpu.make_async_copy(full, full_buf, sems.at[len(PARTS)])
    load.start()
    fetch[0].start()
    load.wait()
    for i, r in enumerate(rows):
        fetch[i].wait()
        if i == 0:
            for copy in fetch[1:]:
                copy.start()
        query_proj = jnp.dot(
            query_buf[r, :], full_buf[...], preferred_element_type=jnp.float32
        ).astype(jnp.bfloat16)
        logits[:, r] = lax.dot_general(
            proj[...], query_proj, NT, preferred_element_type=jnp.float32
        )
        reduce_logits(scale, used, target, out, logits, r)


def reduce_logits(scale, used, target, out, logits, rows):
    tiles = logits.shape[0] // BLOCK
    sub = lax.broadcasted_iota(jnp.int32, (BLOCK, BLOCK), 0)
    for b in range(rows.start // BLOCK, (rows.start + rows.size) // BLOCK):
        lanes = pl.ds(b * BLOCK, BLOCK)
        live = [used[b, j] > 0 for j in range(tiles)]
        wanted = jnp.broadcast_to(target[b], (BLOCK, BLOCK)) - sub
        found = jnp.zeros((BLOCK, BLOCK), jnp.float32)
        top = jnp.full((8, BLOCK), FLOOR, jnp.float32)
        for j in range(tiles):
            tile = logits[pl.ds(j * BLOCK, BLOCK), lanes]
            found = found + jnp.where(wanted == j * BLOCK, tile, 0.0)
            peak = jnp.max(tile.reshape(BLOCK // 8, 8, BLOCK), axis=0)
            top = jnp.maximum(top, jnp.where(live[j], peak, FLOOR))
        found = jnp.sum(found, axis=0, keepdims=True) * scale
        top = jnp.max(top, axis=0, keepdims=True)
        acc = jnp.zeros((8, BLOCK), jnp.float32)
        for j in range(tiles):
            tile = logits[pl.ds(j * BLOCK, BLOCK), lanes]
            term = jnp.exp(jnp.where(live[j], tile - top, FLOOR) * scale)
            acc = acc + jnp.sum(term.reshape(BLOCK // 8, 8, BLOCK), axis=0)
        acc = jnp.sum(acc, axis=0, keepdims=True)
        some = acc > 0.0
        out[b, 0:1, :] = jnp.where(some, top * scale + jnp.log(jnp.where(some, acc, 1.0)), FLOOR)
        out[b, 1:2, :] = found


def local(queries, passages, head, positives, negative_ids, negative_count):
    queries, passages = queries[0], passages[0]
    width = queries.shape[1]
    scale = width ** (-0.5)
    deep = lax.axis_size("z")
    steps = lax.axis_size("y")
    z, high, low = lax.axis_index("z"), lax.axis_index("xh"), lax.axis_index("xl")
    core = lax.axis_index("core")
    rows = passages.shape[0]
    assert 4 * rows == width
    flip = [(0, 1), (1, 0)]
    both = [(0, 3), (1, 2), (2, 1), (3, 0)]

    gathered = lax.all_gather(queries, "z", axis=0, tiled=True)

    pieces = [
        passages,
        lax.ppermute(passages, "xl", flip),
        lax.ppermute(passages, "xh", flip),
        lax.ppermute(passages, ("xh", "xl"), both),
    ]
    mine = lax.all_to_all(jnp.broadcast_to(head, (steps,) + head.shape), "y", 0, 0)
    other = lax.ppermute(mine, "core", flip)

    slots = negative_ids.shape[2]
    alive = lax.broadcasted_iota(jnp.int32, (1, slots), 1) < negative_count
    listed = jnp.where(alive, negative_ids[0], -1)
    packed = jnp.concatenate(
        [positives, jnp.pad(listed, ((0, 0), (0, BLOCK - slots)), constant_values=-1)], axis=0
    )
    met_lists = lax.all_gather(packed, "z")
    wanted, lists = met_lists[:, 0, :], met_lists[:, 1, :slots]

    run = 2 * rows
    span = run * deep
    inside = wanted % span - z * run
    piece = 2 * ((wanted // span) ^ high) + ((inside // rows) ^ low)
    target = jnp.where((inside >= 0) & (inside < run), piece * rows + inside % rows, -1)
    tiles = rows // BLOCK
    tile = lax.iota(jnp.int32, 4 * tiles)
    piece = tile // tiles
    tile_id = ((((piece // 2) ^ high) * deep + z) * 2 + ((piece % 2) ^ low)) * tiles + tile % tiles
    used = jnp.any(lists[:, :, None] == tile_id[None, None, :], axis=1).astype(jnp.int32)

    vmem = pl.BlockSpec(memory_space=pltpu.VMEM)
    full, proj = pl.pallas_call(
        passage_kernel,
        out_shape=(jax.ShapeDtypeStruct((width, width), jnp.bfloat16),) * 2,
        in_specs=[pl.BlockSpec(memory_space=pltpu.SMEM)] + [vmem] * 6,
        out_specs=(vmem, vmem),
        compiler_params=pltpu.CompilerParams(vmem_limit_bytes=VMEM_BYTES),
    )(core[None], mine, other, *pieces)

    count = deep * queries.shape[0]
    hbm = pl.BlockSpec(memory_space=pltpu.HBM)
    in_hbm = functools.partial(pltpu.with_memory_space_constraint, memory_space=pltpu.HBM)
    stats = pl.pallas_call(
        functools.partial(query_kernel, scale),
        out_shape=jax.ShapeDtypeStruct((deep, 2, BLOCK), jnp.float32),
        in_specs=[pl.BlockSpec(memory_space=pltpu.SMEM), hbm, hbm, vmem, vmem],
        out_specs=vmem,
        scratch_shapes=[
            pltpu.VMEM((count, width), jnp.bfloat16),
            pltpu.VMEM((width, width), jnp.bfloat16),
            pltpu.VMEM((width, count), jnp.float32),
            pltpu.SemaphoreType.DMA((len(PARTS) + 1,)),
        ],
        compiler_params=pltpu.CompilerParams(vmem_limit_bytes=VMEM_BYTES),
    )(used, in_hbm(gathered), in_hbm(full), proj, target[:, None, :])

    home = lax.all_to_all(stats, "z", 0, 0)
    logit = jnp.sum(home[:, 1, :], axis=0)
    also_listed = jnp.any(listed[0][:, None] == positives // BLOCK, axis=0)
    extra = jnp.where(also_listed, FLOOR, logit)
    top = jnp.maximum(jnp.max(home[:, 0, :], axis=0), extra)
    total = jnp.sum(jnp.exp(home[:, 0, :] - top), axis=0) + jnp.exp(extra - top)
    return (top + jnp.log(total) - logit)[None, :]


def solution(mesh):
    grid = Mesh(mesh.devices.reshape(2, 12, 8, 2, 2), ("xh", "z", "y", "core", "xl"))
    shard, part = ("y", "core"), ("xh", "z", "xl")
    in_specs = (
        P(shard, part, None),
        P(shard, part, None),
        P(shard, None),
        P(shard, part),
        P(shard, part, None),
        P(shard, part),
    )
    return jax.shard_map(
        local, mesh=grid, in_specs=in_specs, out_specs=P(shard, part), check_vma=False
    )
```

time: 137 us -> 123 us (0.90)
  blocking collectives: 67.7 us -> 32.3 us
  waiting for transfers between devices: 10.9 us -> 25.6 us
  starting transfers between devices: 16.3 us -> 25.7 us
  Pallas kernels: 19.2 us -> 14.9 us
  local copies, waits for them, and re-layouts: 5.68 us -> 8.47 us
    all_to_all x2 -> x0, blocking collectives: 35.4 us -> none  [the longest x1 29.1 us: local(): lax.all_to_all(jnp.broadcast_to(passages, (wide,) + passages.shape), ROW,...]
    ppermute x0 -> x4, starting transfers between devices: none -> 15.1 us  [the longest x1 8.5 us: local(): lax.ppermute(passages, 'xh', flip)]
    all_to_all x1, waiting for transfers between devices: 0.01 us -> 14.9 us  [local(): lax.all_to_all(jnp.broadcast_to(head, (steps,) + head.shape), 'y', 0, 0)]
    all_to_all x1, starting transfers between devices: 9.17 us -> 3.49 us  [local(): home = lax.all_to_all(stats, 'z', 0, 0)]
    unnamed x11 -> x19, local copies, waits for them, and re-layouts: 2.97 us -> 6.45 us
    pallas_call x1, Pallas kernels: 14.7 us -> 11.2 us  [local(): pl.pallas_call(functools.partial(query_kernel, scale), out_shape=jax.Shap...]
    broadcast_in_dim x2 -> x0, local copies, waits for them, and re-layouts: 1.55 us -> none  [the longest x1 1.3 us: local(): jnp.broadcast_to(passages, (wide,) + passages.shape)]
  transfers between devices with their start and end apart: 3 -> 7, of which waited for: 1 -> 2; matrix products, arithmetic and copies ran while one was open for 2% -> 2% of each run, Pallas kernels for 3% -> 3%
where the time goes in v2:
time: 123 us; the launch traced here: 122 us
  blocking collectives  32.3 us (26%)
  starting transfers between devices  25.7 us (21%)
  waiting for transfers between devices  25.6 us (21%)
  Pallas kernels  14.9 us (12%)
  between operations  14.2 us (12%)
  local copies, waits for them, and re-layouts  8.47 us (7%)
    all_gather x1, blocking collectives, local(): met_lists = lax.all_gather(packed, 'z')  32.3 us
    all_to_all x1, waiting for transfers between devices, local(): lax.all_to_all(jnp.broadcast_to(head, (steps,) + head.shape), 'y', 0, 0)  14.9 us
    pallas_call x1, Pallas kernels, local(): pl.pallas_call(functools.partial(query_kernel, scale), out_shape=jax.Shap...  11.2 us
    all_to_all x1, waiting for transfers between devices, local(): home = lax.all_to_all(stats, 'z', 0, 0)  9.94 us
    ppermute x1, starting transfers between devices, local(): lax.ppermute(passages, 'xh', flip)  8.5 us
    all_to_all x1, starting transfers between devices, local(): lax.all_to_all(jnp.broadcast_to(head, (steps,) + head.shape), 'y', 0, 0)  7.1 us
    unnamed x19, local copies, waits for them, and re-layouts  6.45 us
    pallas_call x1, Pallas kernels, local(): pl.pallas_call(passage_kernel, out_shape=(jax.ShapeDtypeStruct((width, wi...  3.71 us
  transfers between devices with their start and end apart: 7, of which 2 were waited for; matrix products, arithmetic and copies ran while one was open for 2% of the time, Pallas kernels for 3%

profile of v2, /device:TPU:6, one launch (start us, length us, event | category | flops | bytes accessed | tf_op | source)
XLA Modules:
  0.0 122.3 jit_solution(2585189228087300484)
XLA Ops:
  6.5 0.7 all-gather.5.cloned.1.call-update
  7.3 2.0 %broadcast_in_dim.26 = bf16[8,64,1024]{2,1,0:T(8,128)(2,1)} broadcast(bf16[64,1024]{1,0:T(8,128)(2,1)} %param.8), dimensions={1,2} | broadcast | bytes 1179648 | tf_op jit(solution)/shard_map/broadcast_in_dim | solution.py:106
  9.3 7.1 %all-to-all-start = ((bf16[8,64,1024]{2,1,0:T(8,128)(2,1)}), bf16[8,64,1024]{2,1,0:T(8,128)(2,1)S(1)}, u32[]{:S(2)}, u32[]{:S(2)}) async-start(bf16[8,64,1024]{2,1,0:T(8,128)(2,1)} %broadcast_in_dim.26), calls=%async_computation | async-start | bytes 2097152 | tf_op jit(solution)/shard_map/all_to_all | solution.py:106
  16.4 2.7 %collective-permute-start.1 = (bf16[256,1024]{1,0:T(8,128)(2,1)S(1)}, bf16[256,1024]{1,0:T(8,128)(2,1)S(1)}, u32[]{:S(2)}, u32[]{:S(2)}) collective-permute-start(bf16[256,1024]{1,0:T(8,128)(2,1)S(1)} %bitcast.44), channel_id=1, source_target_pairs={{0,1},{1,0},{2,3},{3,2},{4,5},{5,4},{6,7},{7,6},{8,9},{9,8},{10,11... | collective-permute-start | bytes 1572872 | tf_op jit(solution)/shard_map/ppermute | solution.py:102
  19.1 8.5 %collective-permute-start.2 = (bf16[256,1024]{1,0:T(8,128)(2,1)S(1)}, bf16[256,1024]{1,0:T(8,128)(2,1)}, u32[]{:S(2)}, u32[]{:S(2)}) collective-permute-start(bf16[256,1024]{1,0:T(8,128)(2,1)S(1)} %bitcast.45), channel_id=1, source_target_pairs={{0,384},{384,0},{1,385},{385,1},{2,386},{386,2},{3,387},{387,3},{4... | collective-permute-start | bytes 1572872 | tf_op jit(solution)/shard_map/ppermute | solution.py:103
  27.6 1.9 %collective-permute-start.3 = (bf16[256,1024]{1,0:T(8,128)(2,1)S(1)}, bf16[256,1024]{1,0:T(8,128)(2,1)}, u32[]{:S(2)}, u32[]{:S(2)}) collective-permute-start(bf16[256,1024]{1,0:T(8,128)(2,1)S(1)} %bitcast.46), channel_id=1, source_target_pairs={{0,385},{1,384},{384,1},{385,0},{2,387},{3,386},{386,3},{387,2},{4... | collective-permute-start | bytes 1572872 | tf_op jit(solution)/shard_map/ppermute | solution.py:104
  30.2 14.9 %all-to-all-done.mine = bf16[8,64,1024]{2,1,0:T(8,128)(2,1)S(1)} async-done(((bf16[8,64,1024]{2,1,0:T(8,128)(2,1)}), bf16[8,64,1024]{2,1,0:T(8,128)(2,1)S(1)}, u32[]{:S(2)}, u32[]{:S(2)}) %all-to-all-start) | async-done | bytes 1048608 | tf_op jit(solution)/shard_map/all_to_all | solution.py:106
  45.1 1.9 %collective-permute-start = (bf16[8,64,1024]{2,1,0:T(8,128)(2,1)S(1)}, bf16[8,64,1024]{2,1,0:T(8,128)(2,1)S(1)}, u32[]{:S(2)}, u32[]{:S(2)}) collective-permute-start(bf16[8,64,1024]{2,1,0:T(8,128)(2,1)S(1)} %all-to-all-done.mine), channel_id=1, source_target_pairs={{0,2},{2,0},{1,3},{3,1},{4,6},{6,4},{5,7},{7,5},{8,10},{10,8},{9,1... | collective-permute-start | bytes 3145736 | tf_op jit(solution)/shard_map/ppermute | solution.py:107
  47.1 32.3 %all-gather.2 = s32[12,2,128]{2,1,0:T(2,128)S(1)} all-gather(s32[1,2,128]{2,1,0:T(2,128)S(1)} %fusion.5), channel_id=2, replica_groups=mesh['xh'=2,'z'=12,'y'=8,'core'=2,'xl'=2] {'z'}, dimensions={0}, use_global_device_ids=true | all-gather | bytes 13312 | tf_op jit(solution)/shard_map/all_gather | solution.py:115
  79.5 0.4 compare_reduce_fusion
  79.8 0.1 and_select_fusion.3.target
  80.0 0.0 collective-permute-done.1.refs_1_
  80.0 0.8 copy-done.5
  80.8 1.0 copy-done.1
  81.8 1.2 copy-done.2
  83.0 1.0 copy-done.4
  84.1 1.0 copy-done.6
  85.1 3.7 %shard_map.64 = (bf16[1024,1024]{1,0:T(8,128)(2,1)S(1)}, bf16[1024,1024]{1,0:T(8,128)(2,1)S(1)}) custom-call(s32[1]{0:T(128)} %bitcast.4.core, bf16[8,64,1024]{2,1,0:T(8,128)(2,1)S(1)} %all-to-all-done.mine, bf16[8,64,1024]{2,1,0:T(8,128)(2,1)S(1)} %copy-done.2, bf16[256,1024]{1,0:T(8,128)(2,1)S(1)} %bitcast.47, bf16[256,1024]{1,0:T(8,128)(2,1)S(1)} %copy-done.6, ...), custom_call_target="tpu_custom_call" | custom-call | tf_op jit(solution)/shard_map/pallas_call | solution.py:130
  88.8 1.3 %copy-done = bf16[1024,1024]{1,0:T(8,128)(2,1)} copy-done((bf16[1024,1024]{1,0:T(8,128)(2,1)}, bf16[1024,1024]{1,0:T(8,128)(2,1)S(1)}, u32[]{:S(2)}) %copy-start) | copy-done | bytes 2097176
  90.2 11.2 %shard_map.65 = f32[12,2,128]{2,1,0:T(2,128)} custom-call(s32[12,8]{1,0:T(8,128)S(1)} %convert_element_type.3.used, bf16[1536,1024]{1,0:T(8,128)(2,1)} %bitcast.48, bf16[1024,1024]{1,0:T(8,128)(2,1)} %copy-done, bf16[1024,1024]{1,0:T(8,128)(2,1)S(1)} %get-tuple-element.8.proj, s32[12,1,128]{2,1,0:T(1,128)S(1)} %and_select_fusion.3.target), custom_call_target="tpu_custom_call" | custom-call | tf_op jit(solution)/shard_map/pallas_call | solution.py:141
  101.4 3.5 %all-to-all-start.1 = ((f32[12,2,128]{2,1,0:T(2,128)}), f32[12,2,128]{2,1,0:T(2,128)S(1)}, u32[]{:S(2)}, u32[]{:S(2)}) async-start(f32[12,2,128]{2,1,0:T(2,128)} %shard_map.65), calls=%async_computation.1 | async-start | bytes 24576 | tf_op jit(solution)/shard_map/all_to_all | solution.py:155
  104.9 0.1 compare_reduce_fusion.1
  105.0 9.9 %all-to-all-done.1 = f32[12,2,128]{2,1,0:T(2,128)S(1)} async-done(((f32[12,2,128]{2,1,0:T(2,128)}), f32[12,2,128]{2,1,0:T(2,128)S(1)}, u32[]{:S(2)}, u32[]{:S(2)}) %all-to-all-start.1) | async-done | bytes 12320 | tf_op jit(solution)/shard_map/all_to_all | solution.py:155
  115.0 0.5 fusion.11
  (28 shorter events, 0.2 us)
Async XLA Ops:
  6.5 9.8 %copy-start.3 = (bf16[1,256,1024]{2,1,0:T(8,128)(2,1)S(1)}, bf16[1,256,1024]{2,1,0:T(8,128)(2,1)}, u32[]{:S(2)}) copy-start(bf16[1,256,1024]{2,1,0:T(8,128)(2,1)} %param.7) | copy-start | bytes 1572868
  6.5 40.5 %copy-start.8 = (s32[1,1,12]{2,1,0:T(1,128)S(1)}, s32[1,1,12]{2,1,0:T(1,128)}, u32[]{:S(2)}) copy-start(s32[1,1,12]{2,1,0:T(1,128)} %param.10) | copy-start | bytes 148
  6.5 40.5 %copy-start.7 = (s32[1,128]{1,0:T(1,128)S(1)}, s32[1,128]{1,0:T(1,128)}, u32[]{:S(2)}) copy-start(s32[1,128]{1,0:T(1,128)} %param.9) | copy-start | bytes 1540
  6.5 83.6 %all-gather.5.cloned.1.call-start = ((), (), s32[]{:S(2)}) async-start(), calls=%async_computation.2 | async-start | bytes 3407872 | tf_op jit(solution)/shard_map/all_gather | solution.py:98
  9.3 35.8 %all-to-all-start = ((bf16[8,64,1024]{2,1,0:T(8,128)(2,1)}), bf16[8,64,1024]{2,1,0:T(8,128)(2,1)S(1)}, u32[]{:S(2)}, u32[]{:S(2)}) async-start(bf16[8,64,1024]{2,1,0:T(8,128)(2,1)} %broadcast_in_dim.26), calls=%async_computation | async-start | bytes 2097152 | tf_op jit(solution)/shard_map/all_to_all | solution.py:106
  16.4 63.6 %collective-permute-start.1 = (bf16[256,1024]{1,0:T(8,128)(2,1)S(1)}, bf16[256,1024]{1,0:T(8,128)(2,1)S(1)}, u32[]{:S(2)}, u32[]{:S(2)}) collective-permute-start(bf16[256,1024]{1,0:T(8,128)(2,1)S(1)} %bitcast.44), channel_id=1, source_target_pairs={{0,1},{1,0},{2,3},{3,2},{4,5},{5,4},{6,7},{7,6},{8,9},{9,8},{10,11... | collective-permute-start | bytes 1572872 | tf_op jit(solution)/shard_map/ppermute | solution.py:102
  19.1 61.7 %collective-permute-start.2 = (bf16[256,1024]{1,0:T(8,128)(2,1)S(1)}, bf16[256,1024]{1,0:T(8,128)(2,1)}, u32[]{:S(2)}, u32[]{:S(2)}) collective-permute-start(bf16[256,1024]{1,0:T(8,128)(2,1)S(1)} %bitcast.45), channel_id=1, source_target_pairs={{0,384},{384,0},{1,385},{385,1},{2,386},{386,2},{3,387},{387,3},{4... | collective-permute-start | bytes 1572872 | tf_op jit(solution)/shard_map/ppermute | solution.py:103
  27.6 53.2 %collective-permute-start.3 = (bf16[256,1024]{1,0:T(8,128)(2,1)S(1)}, bf16[256,1024]{1,0:T(8,128)(2,1)}, u32[]{:S(2)}, u32[]{:S(2)}) collective-permute-start(bf16[256,1024]{1,0:T(8,128)(2,1)S(1)} %bitcast.46), channel_id=1, source_target_pairs={{0,385},{1,384},{384,1},{385,0},{2,387},{3,386},{386,3},{387,2},{4... | collective-permute-start | bytes 1572872 | tf_op jit(solution)/shard_map/ppermute | solution.py:104
  45.1 35.7 %collective-permute-start = (bf16[8,64,1024]{2,1,0:T(8,128)(2,1)S(1)}, bf16[8,64,1024]{2,1,0:T(8,128)(2,1)S(1)}, u32[]{:S(2)}, u32[]{:S(2)}) collective-permute-start(bf16[8,64,1024]{2,1,0:T(8,128)(2,1)S(1)} %all-to-all-done.mine), channel_id=1, source_target_pairs={{0,2},{2,0},{1,3},{3,1},{4,6},{6,4},{5,7},{7,5},{8,10},{10,8},{9,1... | collective-permute-start | bytes 3145736 | tf_op jit(solution)/shard_map/ppermute | solution.py:107
  80.0 0.8 copy-start.5
  80.8 1.0 copy-start.1
  81.8 1.2 %copy-start.2 = (bf16[8,64,1024]{2,1,0:T(8,128)(2,1)S(1)}, bf16[8,64,1024]{2,1,0:T(8,128)(2,1)}, u32[]{:S(2)}) copy-start(bf16[8,64,1024]{2,1,0:T(8,128)(2,1)} %copy-done.1) | copy-start | bytes 3145732
  83.0 1.0 copy-start.4
  84.1 1.0 copy-start.6
  88.8 1.4 %copy-start = (bf16[1024,1024]{1,0:T(8,128)(2,1)}, bf16[1024,1024]{1,0:T(8,128)(2,1)S(1)}, u32[]{:S(2)}) copy-start(bf16[1024,1024]{1,0:T(8,128)(2,1)S(1)} %get-tuple-element.7.full) | copy-start | bytes 6291460
  101.4 13.5 %all-to-all-start.1 = ((f32[12,2,128]{2,1,0:T(2,128)}), f32[12,2,128]{2,1,0:T(2,128)S(1)}, u32[]{:S(2)}, u32[]{:S(2)}) async-start(f32[12,2,128]{2,1,0:T(2,128)} %shard_map.65), calls=%async_computation.1 | async-start | bytes 24576 | tf_op jit(solution)/shard_map/all_to_all | solution.py:155
Sparse Core Ops, SparseCore 0:
  9.8 71.4 all-gather.4

commit v3 on v2

--- a/solution.py
+++ b/solution.py
@@ -31,26 +31,26 @@
         ).astype(proj.dtype)
 
 
-def query_kernel(scale, used, queries, full, proj, target, out, query_buf, full_buf, logits, sems):
+def query_kernel(scale, used, queries, full, proj, target, out, query_buf, proj_buf, logits, sems):
     rows = [pl.ds(sum(PARTS[:i]), part) for i, part in enumerate(PARTS)]
     fetch = [
         pltpu.make_async_copy(queries.at[r], query_buf.at[r], sems.at[i])
         for i, r in enumerate(rows)
     ]
-    load = pltpu.make_async_copy(full, full_buf, sems.at[len(PARTS)])
+    load = pltpu.make_async_copy(proj, proj_buf, sems.at[len(PARTS)])
+    fetch[0].start()
     load.start()
-    fetch[0].start()
-    load.wait()
+    for copy in fetch[1:]:
+        copy.start()
     for i, r in enumerate(rows):
         fetch[i].wait()
+        query_proj = jnp.dot(
+            query_buf[r, :], full[...], preferred_element_type=jnp.float32
+        ).astype(jnp.bfloat16)
         if i == 0:
-            for copy in fetch[1:]:
-                copy.start()
-        query_proj = jnp.dot(
-            query_buf[r, :], full_buf[...], preferred_element_type=jnp.float32
-        ).astype(jnp.bfloat16)
+            load.wait()
         logits[:, r] = lax.dot_general(
-            proj[...], query_proj, NT, preferred_element_type=jnp.float32
+            proj_buf[...], query_proj, NT, preferred_element_type=jnp.float32
         )
         reduce_logits(scale, used, target, out, logits, r)
 
@@ -112,7 +112,7 @@
     packed = jnp.concatenate(
         [positives, jnp.pad(listed, ((0, 0), (0, BLOCK - slots)), constant_values=-1)], axis=0
     )
-    met_lists = lax.all_gather(packed, "z")
+    met_lists = lax.all_to_all(jnp.broadcast_to(packed, (deep,) + packed.shape), "z", 0, 0)
     wanted, lists = met_lists[:, 0, :], met_lists[:, 1, :slots]
 
     run = 2 * rows
@@ -141,7 +141,7 @@
     stats = pl.pallas_call(
         functools.partial(query_kernel, scale),
         out_shape=jax.ShapeDtypeStruct((deep, 2, BLOCK), jnp.float32),
-        in_specs=[pl.BlockSpec(memory_space=pltpu.SMEM), hbm, hbm, vmem, vmem],
+        in_specs=[pl.BlockSpec(memory_space=pltpu.SMEM), hbm, vmem, hbm, vmem],
         out_specs=vmem,
         scratch_shapes=[
             pltpu.VMEM((count, width), jnp.bfloat16),
@@ -150,7 +150,7 @@
             pltpu.SemaphoreType.DMA((len(PARTS) + 1,)),
         ],
         compiler_params=pltpu.CompilerParams(vmem_limit_bytes=VMEM_BYTES),
-    )(used, in_hbm(gathered), in_hbm(full), proj, target[:, None, :])
+    )(used, in_hbm(gathered), full, in_hbm(proj), target[:, None, :])
 
     home = lax.all_to_all(stats, "z", 0, 0)
     logit = jnp.sum(home[:, 1, :], axis=0)

time: 123 us -> 116 us (0.943)
  blocking collectives: 32.3 us -> 0 us
  starting transfers between devices: 25.7 us -> 40.8 us
  waiting for transfers between devices: 25.6 us -> 35.7 us
    all_gather x1 -> x0, blocking collectives: 32.3 us -> none  [local(): met_lists = lax.all_gather(packed, 'z')]
    all_to_all x0 -> x1, starting transfers between devices: none -> 15.2 us  [local(): lax.all_to_all(jnp.broadcast_to(packed, (deep,) + packed.shape), 'z', 0, 0)]
    all_to_all x0 -> x1, waiting for transfers between devices: none -> 10.1 us  [local(): lax.all_to_all(jnp.broadcast_to(packed, (deep,) + packed.shape), 'z', 0, 0)]
  transfers between devices with their start and end apart: 7 -> 8, of which waited for: 2 -> 3; matrix products, arithmetic and copies ran while one was open for 2% -> 3% of each run, Pallas kernels for 3% -> 3%
where the time goes in v3:
time: 116 us; the launch traced here: 115 us
  starting transfers between devices  40.8 us (35%)
  waiting for transfers between devices  35.7 us (31%)
  Pallas kernels  14.4 us (12%)
  between operations  14.2 us (12%)
  local copies, waits for them, and re-layouts  9.11 us (8%)
  other arithmetic  1.21 us (1%)
    all_to_all x1, starting transfers between devices, local(): lax.all_to_all(jnp.broadcast_to(packed, (deep,) + packed.shape), 'z', 0, 0)  15.2 us
    all_to_all x1, waiting for transfers between devices, local(): lax.all_to_all(jnp.broadcast_to(head, (steps,) + head.shape), 'y', 0, 0)  14.9 us
    pallas_call x1, Pallas kernels, local(): pl.pallas_call(functools.partial(query_kernel, scale), out_shape=jax.Shap...  10.8 us
    all_to_all x1, waiting for transfers between devices, local(): lax.all_to_all(jnp.broadcast_to(packed, (deep,) + packed.shape), 'z', 0, 0)  10.1 us
    all_to_all x1, waiting for transfers between devices, local(): home = lax.all_to_all(stats, 'z', 0, 0)  10 us
    ppermute x1, starting transfers between devices, local(): lax.ppermute(passages, 'xh', flip)  8.5 us
    all_to_all x1, starting transfers between devices, local(): lax.all_to_all(jnp.broadcast_to(head, (steps,) + head.shape), 'y', 0, 0)  7.1 us
    unnamed x19, local copies, waits for them, and re-layouts  6.47 us
  transfers between devices with their start and end apart: 8, of which 3 were waited for; matrix products, arithmetic and copies ran while one was open for 3% of the time, Pallas kernels for 3%

profile of v3, /device:TPU:6, one launch (start us, length us, event | category | flops | bytes accessed | tf_op | source)
XLA Modules:
  0.0 115.5 jit_solution(12939455518748492687)
XLA Ops:
  6.5 0.7 all-gather.3.cloned.1.call-update
  7.3 2.0 %broadcast_in_dim.30 = bf16[8,64,1024]{2,1,0:T(8,128)(2,1)} broadcast(bf16[64,1024]{1,0:T(8,128)(2,1)} %param.8), dimensions={1,2} | broadcast | bytes 1179648 | tf_op jit(solution)/shard_map/broadcast_in_dim | solution.py:106
  9.3 7.1 %all-to-all-start.1 = ((bf16[8,64,1024]{2,1,0:T(8,128)(2,1)}), bf16[8,64,1024]{2,1,0:T(8,128)(2,1)S(1)}, u32[]{:S(2)}, u32[]{:S(2)}) async-start(bf16[8,64,1024]{2,1,0:T(8,128)(2,1)} %broadcast_in_dim.30), calls=%async_computation.1 | async-start | bytes 2097152 | tf_op jit(solution)/shard_map/all_to_all | solution.py:106
  16.4 2.7 %collective-permute-start.1 = (bf16[256,1024]{1,0:T(8,128)(2,1)S(1)}, bf16[256,1024]{1,0:T(8,128)(2,1)S(1)}, u32[]{:S(2)}, u32[]{:S(2)}) collective-permute-start(bf16[256,1024]{1,0:T(8,128)(2,1)S(1)} %bitcast.42), channel_id=1, source_target_pairs={{0,1},{1,0},{2,3},{3,2},{4,5},{5,4},{6,7},{7,6},{8,9},{9,8},{10,11... | collective-permute-start | bytes 1572872 | tf_op jit(solution)/shard_map/ppermute | solution.py:102
  19.1 8.5 %collective-permute-start.2 = (bf16[256,1024]{1,0:T(8,128)(2,1)S(1)}, bf16[256,1024]{1,0:T(8,128)(2,1)}, u32[]{:S(2)}, u32[]{:S(2)}) collective-permute-start(bf16[256,1024]{1,0:T(8,128)(2,1)S(1)} %bitcast.43), channel_id=1, source_target_pairs={{0,384},{384,0},{1,385},{385,1},{2,386},{386,2},{3,387},{387,3},{4... | collective-permute-start | bytes 1572872 | tf_op jit(solution)/shard_map/ppermute | solution.py:103
  27.6 1.9 %collective-permute-start.3 = (bf16[256,1024]{1,0:T(8,128)(2,1)S(1)}, bf16[256,1024]{1,0:T(8,128)(2,1)}, u32[]{:S(2)}, u32[]{:S(2)}) collective-permute-start(bf16[256,1024]{1,0:T(8,128)(2,1)S(1)} %bitcast.44), channel_id=1, source_target_pairs={{0,385},{1,384},{384,1},{385,0},{2,387},{3,386},{386,3},{387,2},{4... | collective-permute-start | bytes 1572872 | tf_op jit(solution)/shard_map/ppermute | solution.py:104
  30.2 14.9 %all-to-all-done.1.mine = bf16[8,64,1024]{2,1,0:T(8,128)(2,1)S(1)} async-done(((bf16[8,64,1024]{2,1,0:T(8,128)(2,1)}), bf16[8,64,1024]{2,1,0:T(8,128)(2,1)S(1)}, u32[]{:S(2)}, u32[]{:S(2)}) %all-to-all-start.1) | async-done | bytes 1048608 | tf_op jit(solution)/shard_map/all_to_all | solution.py:106
  45.1 1.9 %collective-permute-start = (bf16[8,64,1024]{2,1,0:T(8,128)(2,1)S(1)}, bf16[8,64,1024]{2,1,0:T(8,128)(2,1)S(1)}, u32[]{:S(2)}, u32[]{:S(2)}) collective-permute-start(bf16[8,64,1024]{2,1,0:T(8,128)(2,1)S(1)} %all-to-all-done.1.mine), channel_id=1, source_target_pairs={{0,2},{2,0},{1,3},{3,1},{4,6},{6,4},{5,7},{7,5},{8,10},{10,8},{9,1... | collective-permute-start | bytes 3145736 | tf_op jit(solution)/shard_map/ppermute | solution.py:107
  47.1 0.6 broadcast_in_dim.28
  47.7 15.2 %all-to-all-start = ((s32[12,2,128]{2,1,0:T(2,128)}), s32[12,2,128]{2,1,0:T(2,128)S(1)}, u32[]{:S(2)}, u32[]{:S(2)}) async-start(s32[12,2,128]{2,1,0:T(2,128)} %broadcast_in_dim.28), calls=%async_computation | async-start | bytes 24576 | tf_op jit(solution)/shard_map/all_to_all | solution.py:115
  62.9 10.1 %all-to-all-done = s32[12,2,128]{2,1,0:T(2,128)S(1)} async-done(((s32[12,2,128]{2,1,0:T(2,128)}), s32[12,2,128]{2,1,0:T(2,128)S(1)}, u32[]{:S(2)}, u32[]{:S(2)}) %all-to-all-start) | async-done | bytes 12320 | tf_op jit(solution)/shard_map/all_to_all | solution.py:115
  73.0 0.4 compare_reduce_fusion
  73.4 0.1 and_select_fusion.3.target
  73.5 0.8 copy-done.5
  74.4 1.0 copy-done.1
  75.3 1.2 %copy-done.2 = bf16[8,64,1024]{2,1,0:T(8,128)(2,1)S(1)} copy-done((bf16[8,64,1024]{2,1,0:T(8,128)(2,1)S(1)}, bf16[8,64,1024]{2,1,0:T(8,128)(2,1)}, u32[]{:S(2)}) %copy-start.2) | copy-done | bytes 1048600
  76.6 1.0 copy-done.4
  77.6 1.0 copy-done.6
  78.7 3.7 %shard_map.64 = (bf16[1024,1024]{1,0:T(8,128)(2,1)S(1)}, bf16[1024,1024]{1,0:T(8,128)(2,1)S(1)}) custom-call(s32[1]{0:T(128)} %bitcast.3.core, bf16[8,64,1024]{2,1,0:T(8,128)(2,1)S(1)} %all-to-all-done.1.mine, bf16[8,64,1024]{2,1,0:T(8,128)(2,1)S(1)} %copy-done.2, bf16[256,1024]{1,0:T(8,128)(2,1)S(1)} %bitcast.45, bf16[256,1024]{1,0:T(8,128)(2,1)S(1)} %copy-done.6, ...), custom_call_target="tpu_custom_call" | custom-call | tf_op jit(solution)/shard_map/pallas_call | solution.py:130
  82.4 1.3 %copy-done = bf16[1024,1024]{1,0:T(8,128)(2,1)} copy-done((bf16[1024,1024]{1,0:T(8,128)(2,1)}, bf16[1024,1024]{1,0:T(8,128)(2,1)S(1)}, u32[]{:S(2)}) %copy-start) | copy-done | bytes 2097176
  83.7 10.8 %shard_map.65 = f32[12,2,128]{2,1,0:T(2,128)} custom-call(s32[12,8]{1,0:T(8,128)S(1)} %convert_element_type.3.used, bf16[1536,1024]{1,0:T(8,128)(2,1)} %bitcast.46, bf16[1024,1024]{1,0:T(8,128)(2,1)S(1)} %get-tuple-element.7.full, bf16[1024,1024]{1,0:T(8,128)(2,1)} %copy-done, s32[12,1,128]{2,1,0:T(1,128)S(1)} %and_select_fusion.3.target), custom_call_target="tpu_custom_call" | custom-call | tf_op jit(solution)/shard_map/pallas_call | solution.py:141
  94.4 3.5 %all-to-all-start.2 = ((f32[12,2,128]{2,1,0:T(2,128)}), f32[12,2,128]{2,1,0:T(2,128)S(1)}, u32[]{:S(2)}, u32[]{:S(2)}) async-start(f32[12,2,128]{2,1,0:T(2,128)} %shard_map.65), calls=%async_computation.2 | async-start | bytes 24576 | tf_op jit(solution)/shard_map/all_to_all | solution.py:155
  98.0 10.0 %all-to-all-done.2 = f32[12,2,128]{2,1,0:T(2,128)S(1)} async-done(((f32[12,2,128]{2,1,0:T(2,128)}), f32[12,2,128]{2,1,0:T(2,128)S(1)}, u32[]{:S(2)}, u32[]{:S(2)}) %all-to-all-start.2) | async-done | bytes 12320 | tf_op jit(solution)/shard_map/all_to_all | solution.py:155
  108.1 0.5 fusion.10
  (30 shorter events, 0.3 us)
Async XLA Ops:
  6.5 9.9 %copy-start.3 = (bf16[1,256,1024]{2,1,0:T(8,128)(2,1)S(1)}, bf16[1,256,1024]{2,1,0:T(8,128)(2,1)}, u32[]{:S(2)}) copy-start(bf16[1,256,1024]{2,1,0:T(8,128)(2,1)} %param.7) | copy-start | bytes 1572868
  6.5 40.5 %copy-start.8 = (s32[1,1,12]{2,1,0:T(1,128)S(1)}, s32[1,1,12]{2,1,0:T(1,128)}, u32[]{:S(2)}) copy-start(s32[1,1,12]{2,1,0:T(1,128)} %param.10) | copy-start | bytes 148
  6.5 40.5 %copy-start.7 = (s32[1,128]{1,0:T(1,128)S(1)}, s32[1,128]{1,0:T(1,128)}, u32[]{:S(2)}) copy-start(s32[1,128]{1,0:T(1,128)} %param.9) | copy-start | bytes 1540
  6.5 77.1 %all-gather.3.cloned.1.call-start = ((), (), s32[]{:S(2)}) async-start(), calls=%async_computation.3 | async-start | bytes 3407872 | tf_op jit(solution)/shard_map/all_gather | solution.py:98
  9.3 35.8 %all-to-all-start.1 = ((bf16[8,64,1024]{2,1,0:T(8,128)(2,1)}), bf16[8,64,1024]{2,1,0:T(8,128)(2,1)S(1)}, u32[]{:S(2)}, u32[]{:S(2)}) async-start(bf16[8,64,1024]{2,1,0:T(8,128)(2,1)} %broadcast_in_dim.30), calls=%async_computation.1 | async-start | bytes 2097152 | tf_op jit(solution)/shard_map/all_to_all | solution.py:106
  16.4 57.1 %collective-permute-start.1 = (bf16[256,1024]{1,0:T(8,128)(2,1)S(1)}, bf16[256,1024]{1,0:T(8,128)(2,1)S(1)}, u32[]{:S(2)}, u32[]{:S(2)}) collective-permute-start(bf16[256,1024]{1,0:T(8,128)(2,1)S(1)} %bitcast.42), channel_id=1, source_target_pairs={{0,1},{1,0},{2,3},{3,2},{4,5},{5,4},{6,7},{7,6},{8,9},{9,8},{10,11... | collective-permute-start | bytes 1572872 | tf_op jit(solution)/shard_map/ppermute | solution.py:102
  19.1 55.2 %collective-permute-start.2 = (bf16[256,1024]{1,0:T(8,128)(2,1)S(1)}, bf16[256,1024]{1,0:T(8,128)(2,1)}, u32[]{:S(2)}, u32[]{:S(2)}) collective-permute-start(bf16[256,1024]{1,0:T(8,128)(2,1)S(1)} %bitcast.43), channel_id=1, source_target_pairs={{0,384},{384,0},{1,385},{385,1},{2,386},{386,2},{3,387},{387,3},{4... | collective-permute-start | bytes 1572872 | tf_op jit(solution)/shard_map/ppermute | solution.py:103
  27.6 46.7 %collective-permute-start.3 = (bf16[256,1024]{1,0:T(8,128)(2,1)S(1)}, bf16[256,1024]{1,0:T(8,128)(2,1)}, u32[]{:S(2)}, u32[]{:S(2)}) collective-permute-start(bf16[256,1024]{1,0:T(8,128)(2,1)S(1)} %bitcast.44), channel_id=1, source_target_pairs={{0,385},{1,384},{384,1},{385,0},{2,387},{3,386},{386,3},{387,2},{4... | collective-permute-start | bytes 1572872 | tf_op jit(solution)/shard_map/ppermute | solution.py:104
  45.1 29.2 %collective-permute-start = (bf16[8,64,1024]{2,1,0:T(8,128)(2,1)S(1)}, bf16[8,64,1024]{2,1,0:T(8,128)(2,1)S(1)}, u32[]{:S(2)}, u32[]{:S(2)}) collective-permute-start(bf16[8,64,1024]{2,1,0:T(8,128)(2,1)S(1)} %all-to-all-done.1.mine), channel_id=1, source_target_pairs={{0,2},{2,0},{1,3},{3,1},{4,6},{6,4},{5,7},{7,5},{8,10},{10,8},{9,1... | collective-permute-start | bytes 3145736 | tf_op jit(solution)/shard_map/ppermute | solution.py:107
  47.7 25.3 %all-to-all-start = ((s32[12,2,128]{2,1,0:T(2,128)}), s32[12,2,128]{2,1,0:T(2,128)S(1)}, u32[]{:S(2)}, u32[]{:S(2)}) async-start(s32[12,2,128]{2,1,0:T(2,128)} %broadcast_in_dim.28), calls=%async_computation | async-start | bytes 24576 | tf_op jit(solution)/shard_map/all_to_all | solution.py:115
  73.5 0.8 copy-start.5
  74.3 1.0 copy-start.1
  75.3 1.2 %copy-start.2 = (bf16[8,64,1024]{2,1,0:T(8,128)(2,1)S(1)}, bf16[8,64,1024]{2,1,0:T(8,128)(2,1)}, u32[]{:S(2)}) copy-start(bf16[8,64,1024]{2,1,0:T(8,128)(2,1)} %copy-done.1) | copy-start | bytes 3145732
  76.6 1.0 copy-start.4
  77.6 1.0 copy-start.6
  82.3 1.3 %copy-start = (bf16[1024,1024]{1,0:T(8,128)(2,1)}, bf16[1024,1024]{1,0:T(8,128)(2,1)S(1)}, u32[]{:S(2)}) copy-start(bf16[1024,1024]{1,0:T(8,128)(2,1)S(1)} %get-tuple-element.8.proj) | copy-start | bytes 6291460
  94.4 13.6 %all-to-all-start.2 = ((f32[12,2,128]{2,1,0:T(2,128)}), f32[12,2,128]{2,1,0:T(2,128)S(1)}, u32[]{:S(2)}, u32[]{:S(2)}) async-start(f32[12,2,128]{2,1,0:T(2,128)} %shard_map.65), calls=%async_computation.2 | async-start | bytes 24576 | tf_op jit(solution)/shard_map/all_to_all | solution.py:155
Sparse Core Ops, SparseCore 0:
  9.8 71.5 all-gather.2

commit v4 on v3

--- a/solution.py
+++ b/solution.py
@@ -12,54 +12,54 @@
 FLOOR = -1e30
 NT = (((1,), (1,)), ((), ()))
 VMEM_BYTES = 24 * 1024 * 1024
-PARTS = (512, 1024)
-
-
-def passage_kernel(core, mine, other, *refs):
-    *pieces, full, proj = refs
+
+
+def passage_kernel(core, mine, other, p0, p1, p2, p3, proj, full, head_buf, piece_buf, sems):
+    pieces = (p0, p1, p2, p3)
+    heads = [
+        pltpu.make_async_copy(half, head_buf.at[i], sems.at[i]) for i, half in enumerate((mine, other))
+    ]
+    loads = [
+        pltpu.make_async_copy(piece, piece_buf.at[i], sems.at[2 + i])
+        for i, piece in enumerate(pieces)
+    ]
+    for copy in heads + loads:
+        copy.start()
+    for copy in heads:
+        copy.wait()
     steps, depth, _ = mine.shape
     here = core[0]
     for y in range(steps):
         first = pl.multiple_of((2 * y + here) * depth, depth)
         second = pl.multiple_of((2 * y + 1 - here) * depth, depth)
-        full[pl.ds(first, depth), :] = mine[y]
-        full[pl.ds(second, depth), :] = other[y]
-    rows = pieces[0].shape[0]
-    for s, piece in enumerate(pieces):
-        proj[pl.ds(s * rows, rows), :] = jnp.dot(
-            piece[...], full[...], preferred_element_type=jnp.float32
+        full[pl.ds(first, depth), :] = head_buf[0, y]
+        full[pl.ds(second, depth), :] = head_buf[1, y]
+    for copy in loads:
+        copy.wait()
+    rows = p0.shape[0]
+    for i in range(len(pieces)):
+        proj[pl.ds(i * rows, rows), :] = jnp.dot(
+            piece_buf[i], full[...], preferred_element_type=jnp.float32
         ).astype(proj.dtype)
 
 
-def query_kernel(scale, used, queries, full, proj, target, out, query_buf, proj_buf, logits, sems):
-    rows = [pl.ds(sum(PARTS[:i]), part) for i, part in enumerate(PARTS)]
-    fetch = [
-        pltpu.make_async_copy(queries.at[r], query_buf.at[r], sems.at[i])
-        for i, r in enumerate(rows)
-    ]
-    load = pltpu.make_async_copy(proj, proj_buf, sems.at[len(PARTS)])
-    fetch[0].start()
-    load.start()
-    for copy in fetch[1:]:
-        copy.start()
-    for i, r in enumerate(rows):
-        fetch[i].wait()
-        query_proj = jnp.dot(
-            query_buf[r, :], full[...], preferred_element_type=jnp.float32
-        ).astype(jnp.bfloat16)
-        if i == 0:
-            load.wait()
-        logits[:, r] = lax.dot_general(
-            proj_buf[...], query_proj, NT, preferred_element_type=jnp.float32
-        )
-        reduce_logits(scale, used, target, out, logits, r)
-
-
-def reduce_logits(scale, used, target, out, logits, rows):
+def query_kernel(scale, turns, earlier, place, used, *refs):
+    count = len(turns)
+    blocks, (full, proj, target) = refs[:count], refs[count : count + 3]
+    before, (out, query_buf, logits) = refs[count + 3 : -3], refs[-3:]
+    for n, block in enumerate(blocks):
+        query_buf[pl.ds(n * BLOCK, BLOCK), :] = block[...]
+    query_proj = jnp.dot(
+        query_buf[...], full[...], preferred_element_type=jnp.float32
+    ).astype(jnp.bfloat16)
+    logits[...] = lax.dot_general(proj[...], query_proj, NT, preferred_element_type=jnp.float32)
+    for group, stats in zip(earlier, before):
+        for n, turn in enumerate(group):
+            out[place[turn]] = stats[n]
     tiles = logits.shape[0] // BLOCK
     sub = lax.broadcasted_iota(jnp.int32, (BLOCK, BLOCK), 0)
-    for b in range(rows.start // BLOCK, (rows.start + rows.size) // BLOCK):
-        lanes = pl.ds(b * BLOCK, BLOCK)
+    for n, turn in enumerate(turns):
+        b, lanes = place[turn], pl.ds(n * BLOCK, BLOCK)
         live = [used[b, j] > 0 for j in range(tiles)]
         wanted = jnp.broadcast_to(target[b], (BLOCK, BLOCK)) - sub
         found = jnp.zeros((BLOCK, BLOCK), jnp.float32)
@@ -78,8 +78,9 @@
             acc = acc + jnp.sum(term.reshape(BLOCK // 8, 8, BLOCK), axis=0)
         acc = jnp.sum(acc, axis=0, keepdims=True)
         some = acc > 0.0
-        out[b, 0:1, :] = jnp.where(some, top * scale + jnp.log(jnp.where(some, acc, 1.0)), FLOOR)
-        out[b, 1:2, :] = found
+        lse = jnp.where(some, top * scale + jnp.log(jnp.where(some, acc, 1.0)), FLOOR)
+        row = b if earlier else n
+        out[row] = jnp.concatenate([lse, found], axis=0)
 
 
 def local(queries, passages, head, positives, negative_ids, negative_count):
@@ -91,11 +92,17 @@
     z, high, low = lax.axis_index("z"), lax.axis_index("xh"), lax.axis_index("xl")
     core = lax.axis_index("core")
     rows = passages.shape[0]
-    assert 4 * rows == width
+    assert 4 * rows == width and queries.shape[0] == BLOCK
     flip = [(0, 1), (1, 0)]
     both = [(0, 3), (1, 2), (2, 1), (3, 0)]
 
-    gathered = lax.all_gather(queries, "z", axis=0, tiled=True)
+    ahead = [(i, (i + 1) % deep) for i in range(deep)]
+    back = [(i, (i - 1) % deep) for i in range(deep)]
+    met = {0: queries}
+    for turn in range(1, deep // 2 + 1):
+        met[deep - turn] = lax.ppermute(met[(deep - turn + 1) % deep], "z", ahead)
+        if 2 * turn < deep:
+            met[turn] = lax.ppermute(met[turn - 1], "z", back)
 
     pieces = [
         passages,
@@ -127,30 +134,51 @@
     used = jnp.any(lists[:, :, None] == tile_id[None, None, :], axis=1).astype(jnp.int32)
 
     vmem = pl.BlockSpec(memory_space=pltpu.VMEM)
-    full, proj = pl.pallas_call(
-        passage_kernel,
-        out_shape=(jax.ShapeDtypeStruct((width, width), jnp.bfloat16),) * 2,
-        in_specs=[pl.BlockSpec(memory_space=pltpu.SMEM)] + [vmem] * 6,
-        out_specs=(vmem, vmem),
-        compiler_params=pltpu.CompilerParams(vmem_limit_bytes=VMEM_BYTES),
-    )(core[None], mine, other, *pieces)
-
-    count = deep * queries.shape[0]
+    smem = pl.BlockSpec(memory_space=pltpu.SMEM)
     hbm = pl.BlockSpec(memory_space=pltpu.HBM)
     in_hbm = functools.partial(pltpu.with_memory_space_constraint, memory_space=pltpu.HBM)
-    stats = pl.pallas_call(
-        functools.partial(query_kernel, scale),
-        out_shape=jax.ShapeDtypeStruct((deep, 2, BLOCK), jnp.float32),
-        in_specs=[pl.BlockSpec(memory_space=pltpu.SMEM), hbm, vmem, hbm, vmem],
-        out_specs=vmem,
+    params = pltpu.CompilerParams(vmem_limit_bytes=VMEM_BYTES)
+    square = jax.ShapeDtypeStruct((width, width), jnp.bfloat16)
+    proj, full = pl.pallas_call(
+        passage_kernel,
+        out_shape=(square, square),
+        in_specs=[smem] + [hbm] * 6,
+        out_specs=(vmem, vmem),
         scratch_shapes=[
-            pltpu.VMEM((count, width), jnp.bfloat16),
-            pltpu.VMEM((width, width), jnp.bfloat16),
-            pltpu.VMEM((width, count), jnp.float32),
-            pltpu.SemaphoreType.DMA((len(PARTS) + 1,)),
+            pltpu.VMEM((2,) + mine.shape, jnp.bfloat16),
+            pltpu.VMEM((4,) + passages.shape, jnp.bfloat16),
+            pltpu.SemaphoreType.DMA((6,)),
         ],
-        compiler_params=pltpu.CompilerParams(vmem_limit_bytes=VMEM_BYTES),
-    )(used, in_hbm(gathered), full, in_hbm(proj), target[:, None, :])
+        compiler_params=params,
+        cost_estimate=pl.CostEstimate(flops=2 * width**3, transcendentals=0, bytes_accessed=8 * width**2),
+    )(core[None], *map(in_hbm, (mine, other, *pieces)))
+
+    place = (z + lax.iota(jnp.int32, deep)) % deep
+    groups = [(0, deep - 1, 1)] + [(deep - t, t) for t in range(2, deep // 2)] + [(deep // 2,)]
+    stats = []
+    for group in groups:
+        last = group is groups[-1]
+        count = len(group)
+        out = jax.ShapeDtypeStruct((deep if last else count, 2, BLOCK), jnp.float32)
+        before = stats if last else []
+        result = pl.pallas_call(
+            functools.partial(query_kernel, scale, group, groups[:-1] if last else []),
+            out_shape=out,
+            in_specs=[smem, smem] + [vmem] * (count + 3 + len(before)),
+            out_specs=vmem,
+            scratch_shapes=[
+                pltpu.VMEM((count * BLOCK, width), jnp.bfloat16),
+                pltpu.VMEM((width, count * BLOCK), jnp.float32),
+            ],
+            compiler_params=params,
+            cost_estimate=pl.CostEstimate(
+                flops=4 * count * BLOCK * width**2,
+                transcendentals=count * BLOCK * width,
+                bytes_accessed=2 * count * BLOCK * width,
+            ),
+        )(place, used, *[met[t] for t in group], full, proj, target[:, None, :], *before)
+        stats.append(result)
+    stats = stats[-1]
 
     home = lax.all_to_all(stats, "z", 0, 0)
     logit = jnp.sum(home[:, 1, :], axis=0)

time: 116 us -> 126 us (1.086); the launches traced: 115 us -> 124 us
  starting transfers between devices: 40.8 us -> 83.2 us
  waiting for transfers between devices: 35.7 us -> 16.5 us
  between operations: 14.2 us -> 1.04 us
  local copies, waits for them, and re-layouts: 9.11 us -> 2.67 us
  Pallas kernels: 14.4 us -> 19.6 us
    ppermute x0 -> x11, starting transfers between devices: none -> 47.5 us  [the longest x5 33.5 us: local(): met[turn] = lax.ppermute(met[turn - 1], 'z', back)]
    all_to_all x1, waiting for transfers between devices: 14.9 us -> 0.01 us  [local(): lax.all_to_all(jnp.broadcast_to(head, (steps,) + head.shape), 'y', 0, 0)]
    all_to_all x1, waiting for transfers between devices: 10.1 us -> 0.01 us  [local(): lax.all_to_all(jnp.broadcast_to(packed, (deep,) + packed.shape), 'z', 0, 0)]
    all_to_all x1, starting transfers between devices: 15.2 us -> 7.8 us  [local(): lax.all_to_all(jnp.broadcast_to(packed, (deep,) + packed.shape), 'z', 0, 0)]
    ppermute x0 -> x11, waiting for transfers between devices: none -> 6.47 us  [the longest x6 4.09 us: local(): met[deep - turn] = lax.ppermute(met[(deep - turn + 1) % deep], 'z', ahead)]
    unnamed x19 -> x9, local copies, waits for them, and re-layouts: 6.47 us -> 0.02 us
    all_to_all x1, starting transfers between devices: 3.48 us -> 9.28 us  [local(): home = lax.all_to_all(stats, 'z', 0, 0)]
    ppermute x1, starting transfers between devices: 8.5 us -> 3.02 us  [local(): lax.ppermute(passages, 'xh', flip)]
  transfers between devices with their start and end apart: 8 -> 18, of which waited for: 3 -> 3; matrix products, arithmetic and copies ran while one was open for 3% -> 1% of each run, Pallas kernels for 3% -> 14%
where the time goes in v4:
time: 126 us; the launch traced here: 124 us
  starting transfers between devices  83.2 us (66%)
  Pallas kernels  19.6 us (16%)
  waiting for transfers between devices  16.5 us (13%)
  local copies, waits for them, and re-layouts  2.67 us (2%)
    ppermute x5, starting transfers between devices, local(): met[turn] = lax.ppermute(met[turn - 1], 'z', back)  33.5 us
    pallas_call x6, Pallas kernels, local(): pl.pallas_call(functools.partial(query_kernel, scale, group, groups[:-1]...  15 us
    ppermute x6, starting transfers between devices, local(): met[deep - turn] = lax.ppermute(met[(deep - turn + 1) % deep], 'z', ahead)  14.1 us
    all_to_all x1, waiting for transfers between devices, local(): home = lax.all_to_all(stats, 'z', 0, 0)  10 us
    all_to_all x1, starting transfers between devices, local(): home = lax.all_to_all(stats, 'z', 0, 0)  9.28 us
    all_to_all x1, starting transfers between devices, local(): lax.all_to_all(jnp.broadcast_to(packed, (deep,) + packed.shape), 'z', 0, 0)  7.8 us
    all_to_all x1, starting transfers between devices, local(): lax.all_to_all(jnp.broadcast_to(head, (steps,) + head.shape), 'y', 0, 0)  7.1 us
    pallas_call x1, Pallas kernels, local(): pl.pallas_call(passage_kernel, out_shape=(square, square), in_specs=[smem...  4.57 us
  transfers between devices with their start and end apart: 18, of which 3 were waited for; matrix products, arithmetic and copies ran while one was open for 1% of the time, Pallas kernels for 14%

profile of v4, /device:TPU:6, one launch (start us, length us, event | category | flops | bytes accessed | tf_op | source)
XLA Modules:
  0.0 124.2 jit_solution(10230892077864521171)
XLA Ops:
  0.0 2.0 %broadcast_in_dim.35 = bf16[8,64,1024]{2,1,0:T(8,128)(2,1)} broadcast(bf16[64,1024]{1,0:T(8,128)(2,1)} %param.8), dimensions={1,2} | broadcast | bytes 1179648 | tf_op jit(solution)/shard_map/broadcast_in_dim | solution.py:113
  2.1 7.1 %all-to-all-start.1 = ((bf16[8,64,1024]{2,1,0:T(8,128)(2,1)}), bf16[8,64,1024]{2,1,0:T(8,128)(2,1)S(1)}, u32[]{:S(2)}, u32[]{:S(2)}) async-start(bf16[8,64,1024]{2,1,0:T(8,128)(2,1)} %broadcast_in_dim.35), calls=%async_computation.1 | async-start | bytes 2097152 | tf_op jit(solution)/shard_map/all_to_all | solution.py:113
  9.2 4.3 %collective-permute-start = (bf16[128,1024]{1,0:T(8,128)(2,1)S(1)}, bf16[128,1024]{1,0:T(8,128)(2,1)S(1)}, u32[]{:S(2)}, u32[]{:S(2)}) collective-permute-start(bf16[128,1024]{1,0:T(8,128)(2,1)S(1)} %bitcast.42), channel_id=1, source_target_pairs={{0,32},{32,64},{64,96},{96,128},{128,160},{160,192},{192,224},{224... | collective-permute-start | bytes 786440 | tf_op jit(solution)/shard_map/ppermute | solution.py:103
  13.5 12.2 %collective-permute-start.10 = (bf16[128,1024]{1,0:T(8,128)(2,1)S(1)}, bf16[128,1024]{1,0:T(8,128)(2,1)S(1)}, u32[]{:S(2)}, u32[]{:S(2)}) collective-permute-start(bf16[128,1024]{1,0:T(8,128)(2,1)S(1)} %bitcast.43), channel_id=1, source_target_pairs={{0,352},{32,0},{64,32},{96,64},{128,96},{160,128},{192,160},{224,1... | collective-permute-start | bytes 786440 | tf_op jit(solution)/shard_map/ppermute | solution.py:105
  25.7 4.1 %collective-permute-done.refs_1_ = bf16[128,1024]{1,0:T(8,128)(2,1)S(1)} collective-permute-done((bf16[128,1024]{1,0:T(8,128)(2,1)S(1)}, bf16[128,1024]{1,0:T(8,128)(2,1)S(1)}, u32[]{:S(2)}, u32[]{:S(2)}) %collective-permute-start) | collective-permute-done | bytes 262176 | tf_op jit(solution)/shard_map/ppermute | solution.py:103
  31.7 2.7 %collective-permute-start.7 = (bf16[256,1024]{1,0:T(8,128)(2,1)}, bf16[256,1024]{1,0:T(8,128)(2,1)}, u32[]{:S(2)}, u32[]{:S(2)}) collective-permute-start(bf16[256,1024]{1,0:T(8,128)(2,1)} %bitcast.4.p0), channel_id=1, source_target_pairs={{0,1},{1,0},{2,3},{3,2},{4,5},{5,4},{6,7},{7,6},{8,9},{9,8},{10,11... | collective-permute-start | bytes 1572872 | tf_op jit(solution)/shard_map/ppermute | solution.py:109
  34.4 3.0 %collective-permute-start.8 = (bf16[256,1024]{1,0:T(8,128)(2,1)}, bf16[256,1024]{1,0:T(8,128)(2,1)}, u32[]{:S(2)}, u32[]{:S(2)}) collective-permute-start(bf16[256,1024]{1,0:T(8,128)(2,1)} %bitcast.4.p0), channel_id=1, source_target_pairs={{0,384},{384,0},{1,385},{385,1},{2,386},{386,2},{3,387},{387,3},{4... | collective-permute-start | bytes 1572872 | tf_op jit(solution)/shard_map/ppermute | solution.py:110
  38.1 5.1 %collective-permute-start.11 = (bf16[128,1024]{1,0:T(8,128)(2,1)S(1)}, bf16[128,1024]{1,0:T(8,128)(2,1)S(1)}, u32[]{:S(2)}, u32[]{:S(2)}) collective-permute-start(bf16[128,1024]{1,0:T(8,128)(2,1)S(1)} %collective-permute-done.10.refs_2_), channel_id=1, source_target_pairs={{0,352},{32,0},{64,32},{96,64},{128,96},{160,128},{192,160},{224,1... | collective-permute-start | bytes 786440 | tf_op jit(solution)/shard_map/ppermute | solution.py:105
  47.8 7.8 %all-to-all-start = ((s32[12,2,128]{2,1,0:T(2,128)}), s32[12,2,128]{2,1,0:T(2,128)S(1)}, u32[]{:S(2)}, u32[]{:S(2)}) async-start(s32[12,2,128]{2,1,0:T(2,128)} %broadcast_in_dim.33), calls=%async_computation | async-start | bytes 24576 | tf_op jit(solution)/shard_map/all_to_all | solution.py:122
  55.6 5.1 %collective-permute-start.12 = (bf16[128,1024]{1,0:T(8,128)(2,1)S(1)}, bf16[128,1024]{1,0:T(8,128)(2,1)S(1)}, u32[]{:S(2)}, u32[]{:S(2)}) collective-permute-start(bf16[128,1024]{1,0:T(8,128)(2,1)S(1)} %collective-permute-done.11.refs_1_), channel_id=1, source_target_pairs={{0,352},{32,0},{64,32},{96,64},{128,96},{160,128},{192,160},{224,1... | collective-permute-start | bytes 786440 | tf_op jit(solution)/shard_map/ppermute | solution.py:105
  62.7 3.8 %collective-permute-start.9 = (bf16[256,1024]{1,0:T(8,128)(2,1)}, bf16[256,1024]{1,0:T(8,128)(2,1)}, u32[]{:S(2)}, u32[]{:S(2)}) collective-permute-start(bf16[256,1024]{1,0:T(8,128)(2,1)} %bitcast.4.p0), channel_id=1, source_target_pairs={{0,385},{1,384},{384,1},{385,0},{2,387},{3,386},{386,3},{387,2},{4... | collective-permute-start | bytes 1572872 | tf_op jit(solution)/shard_map/ppermute | solution.py:111
  66.6 5.4 %collective-permute-start.13 = (bf16[128,1024]{1,0:T(8,128)(2,1)S(1)}, bf16[128,1024]{1,0:T(8,128)(2,1)S(1)}, u32[]{:S(2)}, u32[]{:S(2)}) collective-permute-start(bf16[128,1024]{1,0:T(8,128)(2,1)S(1)} %collective-permute-done.12.refs_1_), channel_id=1, source_target_pairs={{0,352},{32,0},{64,32},{96,64},{128,96},{160,128},{192,160},{224,1... | collective-permute-start | bytes 786440 | tf_op jit(solution)/shard_map/ppermute | solution.py:105
  74.5 2.4 %collective-permute-done.13.refs_1_ = bf16[128,1024]{1,0:T(8,128)(2,1)S(1)} collective-permute-done((bf16[128,1024]{1,0:T(8,128)(2,1)S(1)}, bf16[128,1024]{1,0:T(8,128)(2,1)S(1)}, u32[]{:S(2)}, u32[]{:S(2)}) %collective-permute-start.13) | collective-permute-done | bytes 262176 | tf_op jit(solution)/shard_map/ppermute | solution.py:105
  76.8 5.6 %collective-permute-start.14 = (bf16[128,1024]{1,0:T(8,128)(2,1)S(1)}, bf16[128,1024]{1,0:T(8,128)(2,1)S(1)}, u32[]{:S(2)}, u32[]{:S(2)}) collective-permute-start(bf16[128,1024]{1,0:T(8,128)(2,1)S(1)} %collective-permute-done.13.refs_1_), channel_id=1, source_target_pairs={{0,352},{32,0},{64,32},{96,64},{128,96},{160,128},{192,160},{224,1... | collective-permute-start | bytes 786440 | tf_op jit(solution)/shard_map/ppermute | solution.py:105
  82.4 2.1 %collective-permute-start.5 = (bf16[128,1024]{1,0:T(8,128)(2,1)S(1)}, bf16[128,1024]{1,0:T(8,128)(2,1)S(1)}, u32[]{:S(2)}, u32[]{:S(2)}) collective-permute-start(bf16[128,1024]{1,0:T(8,128)(2,1)S(1)} %collective-permute-done.4.refs_0_), channel_id=1, source_target_pairs={{0,32},{32,64},{64,96},{96,128},{128,160},{160,192},{192,224},{224... | collective-permute-start | bytes 786440 | tf_op jit(solution)/shard_map/ppermute | solution.py:103
  84.6 4.6 %shard_map.64 = (bf16[1024,1024]{1,0:T(8,128)(2,1)S(1)}, bf16[1024,1024]{1,0:T(8,128)(2,1)S(1)}) custom-call(s32[1]{0:T(128)} %bitcast.3.core, bf16[8,64,1024]{2,1,0:T(8,128)(2,1)} %copy-done.1, bf16[8,64,1024]{2,1,0:T(8,128)(2,1)} %collective-permute-done.6.other, bf16[256,1024]{1,0:T(8,128)(2,1)} %bitcast.4.p0, ...), custom_call_target="tpu_custom_call" | custom-call | flops 2147483648 | bytes 8388608 | tf_op jit(solution)/shard_map/pallas_call | solution.py:142
  89.2 2.3 %shard_map.68.refs_7_ = f32[2,2,128]{2,1,0:T(2,128)S(1)} custom-call(s32[12]{0:T(128)S(1)} %and_select_fusion.10.place, s32[12,8]{1,0:T(8,128)S(1)} %convert_element_type.3.used, bf16[128,1024]{1,0:T(8,128)(2,1)S(1)} %collective-permute-done.3.refs_0_, bf16[128,1024]{1,0:T(8,128)(2,1)S(1)} %collective-permute-done.13.refs_1_, ...), custom_call_target="tpu_custom_call" | custom-call | flops 1073741824 | bytes 524288 | tf_op jit(solution)/shard_map/pallas_call | solution.py:164
  91.5 2.3 %shard_map.67.refs_6_ = f32[2,2,128]{2,1,0:T(2,128)S(1)} custom-call(s32[12]{0:T(128)S(1)} %and_select_fusion.10.place, s32[12,8]{1,0:T(8,128)S(1)} %convert_element_type.3.used, bf16[128,1024]{1,0:T(8,128)(2,1)S(1)} %collective-permute-done.2.refs_0_, bf16[128,1024]{1,0:T(8,128)(2,1)S(1)} %collective-permute-done.12.refs_1_, ...), custom_call_target="tpu_custom_call" | custom-call | flops 1073741824 | bytes 524288 | tf_op jit(solution)/shard_map/pallas_call | solution.py:164
  93.8 2.3 %shard_map.66.refs_5_ = f32[2,2,128]{2,1,0:T(2,128)S(1)} custom-call(s32[12]{0:T(128)S(1)} %and_select_fusion.10.place, s32[12,8]{1,0:T(8,128)S(1)} %convert_element_type.3.used, bf16[128,1024]{1,0:T(8,128)(2,1)S(1)} %collective-permute-done.1.refs_0_, bf16[128,1024]{1,0:T(8,128)(2,1)S(1)} %collective-permute-done.11.refs_1_, ...), custom_call_target="tpu_custom_call" | custom-call | flops 1073741824 | bytes 524288 | tf_op jit(solution)/shard_map/pallas_call | solution.py:164
  96.2 2.3 %shard_map.69.refs_8_ = f32[2,2,128]{2,1,0:T(2,128)S(1)} custom-call(s32[12]{0:T(128)S(1)} %and_select_fusion.10.place, s32[12,8]{1,0:T(8,128)S(1)} %convert_element_type.3.used, bf16[128,1024]{1,0:T(8,128)(2,1)S(1)} %collective-permute-done.4.refs_0_, bf16[128,1024]{1,0:T(8,128)(2,1)S(1)} %collective-permute-done.14.refs_1_, ...), custom_call_target="tpu_custom_call" | custom-call | flops 1073741824 | bytes 524288 | tf_op jit(solution)/shard_map/pallas_call | solution.py:164
  98.5 3.1 %shard_map.65.refs_4_ = f32[3,2,128]{2,1,0:T(2,128)S(1)} custom-call(s32[12]{0:T(128)S(1)} %and_select_fusion.10.place, s32[12,8]{1,0:T(8,128)S(1)} %convert_element_type.3.used, bf16[128,1024]{1,0:T(8,128)(2,1)S(1)} %bitcast.44, bf16[128,1024]{1,0:T(8,128)(2,1)S(1)} %collective-permute-done.refs_1_, bf16[128,1024]{1,0:T(8,128)(2,1)S(1)} %collective-permute-done.10.refs_2_, ...), custom_call_target="tpu_custom_call" | custom-call | flops 1610612736 | bytes 786432 | tf_op jit(solution)/shard_map/pallas_call | solution.py:164
  101.6 2.5 %shard_map.70 = f32[12,2,128]{2,1,0:T(2,128)} custom-call(s32[12]{0:T(128)S(1)} %and_select_fusion.10.place, s32[12,8]{1,0:T(8,128)S(1)} %convert_element_type.3.used, bf16[128,1024]{1,0:T(8,128)(2,1)S(1)} %collective-permute-done.5.refs_0_, bf16[1024,1024]{1,0:T(8,128)(2,1)S(1)} %get-tuple-element.7.refs_3_.refs_2_.refs_1_, ...), custom_call_target="tpu_custom_call" | custom-call | flops 536870912 | bytes 262144 | tf_op jit(solution)/shard_map/pallas_call | solution.py:164
  104.2 9.3 %all-to-all-start.2 = ((f32[12,2,128]{2,1,0:T(2,128)}), f32[12,2,128]{2,1,0:T(2,128)S(1)}, u32[]{:S(2)}, u32[]{:S(2)}) async-start(f32[12,2,128]{2,1,0:T(2,128)} %shard_map.70), calls=%async_computation.2 | async-start | bytes 24576 | tf_op jit(solution)/shard_map/all_to_all | solution.py:183
  113.6 10.0 %all-to-all-done.2 = f32[12,2,128]{2,1,0:T(2,128)S(1)} async-done(((f32[12,2,128]{2,1,0:T(2,128)}), f32[12,2,128]{2,1,0:T(2,128)S(1)}, u32[]{:S(2)}, u32[]{:S(2)}) %all-to-all-start.2) | async-done | bytes 12320 | tf_op jit(solution)/shard_map/all_to_all | solution.py:183
  (45 shorter events, 11.5 us)
Async XLA Ops:
  0.0 9.2 %copy-start = (bf16[1,128,1024]{2,1,0:T(8,128)(2,1)S(1)}, bf16[1,128,1024]{2,1,0:T(8,128)(2,1)}, u32[]{:S(2)}) copy-start(bf16[1,128,1024]{2,1,0:T(8,128)(2,1)} %param.6) | copy-start | bytes 786436
  0.0 38.1 %copy-start.3 = (s32[1,1,12]{2,1,0:T(1,128)S(1)}, s32[1,1,12]{2,1,0:T(1,128)}, u32[]{:S(2)}) copy-start(s32[1,1,12]{2,1,0:T(1,128)} %param.10) | copy-start | bytes 148
  0.0 47.2 %copy-start.2 = (s32[1,128]{1,0:T(1,128)S(1)}, s32[1,128]{1,0:T(1,128)}, u32[]{:S(2)}) copy-start(s32[1,128]{1,0:T(1,128)} %param.9) | copy-start | bytes 1540
  2.1 43.2 %all-to-all-start.1 = ((bf16[8,64,1024]{2,1,0:T(8,128)(2,1)}), bf16[8,64,1024]{2,1,0:T(8,128)(2,1)S(1)}, u32[]{:S(2)}, u32[]{:S(2)}) async-start(bf16[8,64,1024]{2,1,0:T(8,128)(2,1)} %broadcast_in_dim.35), calls=%async_computation.1 | async-start | bytes 2097152 | tf_op jit(solution)/shard_map/all_to_all | solution.py:113
  9.2 20.6 %collective-permute-start = (bf16[128,1024]{1,0:T(8,128)(2,1)S(1)}, bf16[128,1024]{1,0:T(8,128)(2,1)S(1)}, u32[]{:S(2)}, u32[]{:S(2)}) collective-permute-start(bf16[128,1024]{1,0:T(8,128)(2,1)S(1)} %bitcast.42), channel_id=1, source_target_pairs={{0,32},{32,64},{64,96},{96,128},{128,160},{160,192},{192,224},{224... | collective-permute-start | bytes 786440 | tf_op jit(solution)/shard_map/ppermute | solution.py:103
  13.5 24.7 %collective-permute-start.10 = (bf16[128,1024]{1,0:T(8,128)(2,1)S(1)}, bf16[128,1024]{1,0:T(8,128)(2,1)S(1)}, u32[]{:S(2)}, u32[]{:S(2)}) collective-permute-start(bf16[128,1024]{1,0:T(8,128)(2,1)S(1)} %bitcast.43), channel_id=1, source_target_pairs={{0,352},{32,0},{64,32},{96,64},{128,96},{160,128},{192,160},{224,1... | collective-permute-start | bytes 786440 | tf_op jit(solution)/shard_map/ppermute | solution.py:105
  29.8 13.5 %collective-permute-start.1 = (bf16[128,1024]{1,0:T(8,128)(2,1)S(1)}, bf16[128,1024]{1,0:T(8,128)(2,1)S(1)}, u32[]{:S(2)}, u32[]{:S(2)}) collective-permute-start(bf16[128,1024]{1,0:T(8,128)(2,1)S(1)} %collective-permute-done.refs_1_), channel_id=1, source_target_pairs={{0,32},{32,64},{64,96},{96,128},{128,160},{160,192},{192,224},{224... | collective-permute-start | bytes 786440 | tf_op jit(solution)/shard_map/ppermute | solution.py:103
  31.7 31.0 %collective-permute-start.7 = (bf16[256,1024]{1,0:T(8,128)(2,1)}, bf16[256,1024]{1,0:T(8,128)(2,1)}, u32[]{:S(2)}, u32[]{:S(2)}) collective-permute-start(bf16[256,1024]{1,0:T(8,128)(2,1)} %bitcast.4.p0), channel_id=1, source_target_pairs={{0,1},{1,0},{2,3},{3,2},{4,5},{5,4},{6,7},{7,6},{8,9},{9,8},{10,11... | collective-permute-start | bytes 1572872 | tf_op jit(solution)/shard_map/ppermute | solution.py:109
  34.4 50.1 %collective-permute-start.8 = (bf16[256,1024]{1,0:T(8,128)(2,1)}, bf16[256,1024]{1,0:T(8,128)(2,1)}, u32[]{:S(2)}, u32[]{:S(2)}) collective-permute-start(bf16[256,1024]{1,0:T(8,128)(2,1)} %bitcast.4.p0), channel_id=1, source_target_pairs={{0,384},{384,0},{1,385},{385,1},{2,386},{386,2},{3,387},{387,3},{4... | collective-permute-start | bytes 1572872 | tf_op jit(solution)/shard_map/ppermute | solution.py:110
  38.1 17.5 %collective-permute-start.11 = (bf16[128,1024]{1,0:T(8,128)(2,1)S(1)}, bf16[128,1024]{1,0:T(8,128)(2,1)S(1)}, u32[]{:S(2)}, u32[]{:S(2)}) collective-permute-start(bf16[128,1024]{1,0:T(8,128)(2,1)S(1)} %collective-permute-done.10.refs_2_), channel_id=1, source_target_pairs={{0,352},{32,0},{64,32},{96,64},{128,96},{160,128},{192,160},{224,1... | collective-permute-start | bytes 786440 | tf_op jit(solution)/shard_map/ppermute | solution.py:105
  43.3 17.5 %collective-permute-start.2 = (bf16[128,1024]{1,0:T(8,128)(2,1)S(1)}, bf16[128,1024]{1,0:T(8,128)(2,1)S(1)}, u32[]{:S(2)}, u32[]{:S(2)}) collective-permute-start(bf16[128,1024]{1,0:T(8,128)(2,1)S(1)} %collective-permute-done.1.refs_0_), channel_id=1, source_target_pairs={{0,32},{32,64},{64,96},{96,128},{128,160},{160,192},{192,224},{224... | collective-permute-start | bytes 786440 | tf_op jit(solution)/shard_map/ppermute | solution.py:103
  45.2 39.3 %copy-start.1 = (bf16[8,64,1024]{2,1,0:T(8,128)(2,1)}, bf16[8,64,1024]{2,1,0:T(8,128)(2,1)S(1)}, u32[]{:S(2)}) copy-start(bf16[8,64,1024]{2,1,0:T(8,128)(2,1)S(1)} %all-to-all-done.1.mine) | copy-start | bytes 3145732
  45.2 39.3 %collective-permute-start.6 = (bf16[8,64,1024]{2,1,0:T(8,128)(2,1)S(1)}, bf16[8,64,1024]{2,1,0:T(8,128)(2,1)}, u32[]{:S(2)}, u32[]{:S(2)}) collective-permute-start(bf16[8,64,1024]{2,1,0:T(8,128)(2,1)S(1)} %all-to-all-done.1.mine), channel_id=1, source_target_pairs={{0,2},{2,0},{1,3},{3,1},{4,6},{6,4},{5,7},{7,5},{8,10},{10,8},{9,1... | collective-permute-start | bytes 3145736 | tf_op jit(solution)/shard_map/ppermute | solution.py:114
  47.8 18.7 %all-to-all-start = ((s32[12,2,128]{2,1,0:T(2,128)}), s32[12,2,128]{2,1,0:T(2,128)S(1)}, u32[]{:S(2)}, u32[]{:S(2)}) async-start(s32[12,2,128]{2,1,0:T(2,128)} %broadcast_in_dim.33), calls=%async_computation | async-start | bytes 24576 | tf_op jit(solution)/shard_map/all_to_all | solution.py:122
  55.6 10.9 %collective-permute-start.12 = (bf16[128,1024]{1,0:T(8,128)(2,1)S(1)}, bf16[128,1024]{1,0:T(8,128)(2,1)S(1)}, u32[]{:S(2)}, u32[]{:S(2)}) collective-permute-start(bf16[128,1024]{1,0:T(8,128)(2,1)S(1)} %collective-permute-done.11.refs_1_), channel_id=1, source_target_pairs={{0,352},{32,0},{64,32},{96,64},{128,96},{160,128},{192,160},{224,1... | collective-permute-start | bytes 786440 | tf_op jit(solution)/shard_map/ppermute | solution.py:105
  60.8 11.3 %collective-permute-start.3 = (bf16[128,1024]{1,0:T(8,128)(2,1)S(1)}, bf16[128,1024]{1,0:T(8,128)(2,1)S(1)}, u32[]{:S(2)}, u32[]{:S(2)}) collective-permute-start(bf16[128,1024]{1,0:T(8,128)(2,1)S(1)} %collective-permute-done.2.refs_0_), channel_id=1, source_target_pairs={{0,32},{32,64},{64,96},{96,128},{128,160},{160,192},{192,224},{224... | collective-permute-start | bytes 786440 | tf_op jit(solution)/shard_map/ppermute | solution.py:103
  62.7 21.8 %collective-permute-start.9 = (bf16[256,1024]{1,0:T(8,128)(2,1)}, bf16[256,1024]{1,0:T(8,128)(2,1)}, u32[]{:S(2)}, u32[]{:S(2)}) collective-permute-start(bf16[256,1024]{1,0:T(8,128)(2,1)} %bitcast.4.p0), channel_id=1, source_target_pairs={{0,385},{1,384},{384,1},{385,0},{2,387},{3,386},{386,3},{387,2},{4... | collective-permute-start | bytes 1572872 | tf_op jit(solution)/shard_map/ppermute | solution.py:111
  66.6 10.2 %collective-permute-start.13 = (bf16[128,1024]{1,0:T(8,128)(2,1)S(1)}, bf16[128,1024]{1,0:T(8,128)(2,1)S(1)}, u32[]{:S(2)}, u32[]{:S(2)}) collective-permute-start(bf16[128,1024]{1,0:T(8,128)(2,1)S(1)} %collective-permute-done.12.refs_1_), channel_id=1, source_target_pairs={{0,352},{32,0},{64,32},{96,64},{128,96},{160,128},{192,160},{224,1... | collective-permute-start | bytes 786440 | tf_op jit(solution)/shard_map/ppermute | solution.py:105
  72.0 10.4 %collective-permute-start.4 = (bf16[128,1024]{1,0:T(8,128)(2,1)S(1)}, bf16[128,1024]{1,0:T(8,128)(2,1)S(1)}, u32[]{:S(2)}, u32[]{:S(2)}) collective-permute-start(bf16[128,1024]{1,0:T(8,128)(2,1)S(1)} %collective-permute-done.3.refs_0_), channel_id=1, source_target_pairs={{0,32},{32,64},{64,96},{96,128},{128,160},{160,192},{192,224},{224... | collective-permute-start | bytes 786440 | tf_op jit(solution)/shard_map/ppermute | solution.py:103
  76.8 19.3 %collective-permute-start.14 = (bf16[128,1024]{1,0:T(8,128)(2,1)S(1)}, bf16[128,1024]{1,0:T(8,128)(2,1)S(1)}, u32[]{:S(2)}, u32[]{:S(2)}) collective-permute-start(bf16[128,1024]{1,0:T(8,128)(2,1)S(1)} %collective-permute-done.13.refs_1_), channel_id=1, source_target_pairs={{0,352},{32,0},{64,32},{96,64},{128,96},{160,128},{192,160},{224,1... | collective-permute-start | bytes 786440 | tf_op jit(solution)/shard_map/ppermute | solution.py:105
  82.4 19.2 %collective-permute-start.5 = (bf16[128,1024]{1,0:T(8,128)(2,1)S(1)}, bf16[128,1024]{1,0:T(8,128)(2,1)S(1)}, u32[]{:S(2)}, u32[]{:S(2)}) collective-permute-start(bf16[128,1024]{1,0:T(8,128)(2,1)S(1)} %collective-permute-done.4.refs_0_), channel_id=1, source_target_pairs={{0,32},{32,64},{64,96},{96,128},{128,160},{160,192},{192,224},{224... | collective-permute-start | bytes 786440 | tf_op jit(solution)/shard_map/ppermute | solution.py:103
  104.2 19.4 %all-to-all-start.2 = ((f32[12,2,128]{2,1,0:T(2,128)}), f32[12,2,128]{2,1,0:T(2,128)S(1)}, u32[]{:S(2)}, u32[]{:S(2)}) async-start(f32[12,2,128]{2,1,0:T(2,128)} %shard_map.70), calls=%async_computation.2 | async-start | bytes 24576 | tf_op jit(solution)/shard_map/all_to_all | solution.py:183

commit v5 on v3

--- a/solution.py
+++ b/solution.py
@@ -15,42 +15,50 @@
 PARTS = (512, 1024)
 
 
-def passage_kernel(core, mine, other, *refs):
-    *pieces, full, proj = refs
+def passage_kernel(core, mine, other, p0, p1, p2, p3, keys, full, proj, head_buf, piece_buf, sems):
+    pieces = (p0, p1, p2, p3)
+    heads = [
+        pltpu.make_async_copy(half, head_buf.at[i], sems.at[i]) for i, half in enumerate((mine, other))
+    ]
+    loads = [
+        pltpu.make_async_copy(piece, piece_buf.at[i], sems.at[2 + i])
+        for i, piece in enumerate(pieces)
+    ]
+    for copy in heads + loads:
+        copy.start()
+    for copy in heads:
+        copy.wait()
     steps, depth, _ = mine.shape
     here = core[0]
     for y in range(steps):
         first = pl.multiple_of((2 * y + here) * depth, depth)
         second = pl.multiple_of((2 * y + 1 - here) * depth, depth)
-        full[pl.ds(first, depth), :] = mine[y]
-        full[pl.ds(second, depth), :] = other[y]
-    rows = pieces[0].shape[0]
-    for s, piece in enumerate(pieces):
-        proj[pl.ds(s * rows, rows), :] = jnp.dot(
-            piece[...], full[...], preferred_element_type=jnp.float32
+        full[pl.ds(first, depth), :] = head_buf[0, y]
+        full[pl.ds(second, depth), :] = head_buf[1, y]
+    for copy in loads:
+        copy.wait()
+    rows = p0.shape[0]
+    for i in range(len(pieces)):
+        proj[pl.ds(i * rows, rows), :] = jnp.dot(
+            piece_buf[i], full[...], preferred_element_type=jnp.float32
         ).astype(proj.dtype)
+    keys[...] = lax.dot_general(
+        proj[...], full[...], NT, preferred_element_type=jnp.float32
+    ).astype(keys.dtype)
 
 
-def query_kernel(scale, used, queries, full, proj, target, out, query_buf, proj_buf, logits, sems):
+def query_kernel(scale, used, queries, keys, target, out, query_buf, logits, sems):
     rows = [pl.ds(sum(PARTS[:i]), part) for i, part in enumerate(PARTS)]
     fetch = [
         pltpu.make_async_copy(queries.at[r], query_buf.at[r], sems.at[i])
         for i, r in enumerate(rows)
     ]
-    load = pltpu.make_async_copy(proj, proj_buf, sems.at[len(PARTS)])
-    fetch[0].start()
-    load.start()
-    for copy in fetch[1:]:
+    for copy in fetch:
         copy.start()
-    for i, r in enumerate(rows):
-        fetch[i].wait()
-        query_proj = jnp.dot(
-            query_buf[r, :], full[...], preferred_element_type=jnp.float32
-        ).astype(jnp.bfloat16)
-        if i == 0:
-            load.wait()
+    for copy, r in zip(fetch, rows):
+        copy.wait()
         logits[:, r] = lax.dot_general(
-            proj_buf[...], query_proj, NT, preferred_element_type=jnp.float32
+            keys[...], query_buf[r, :], NT, preferred_element_type=jnp.float32
         )
         reduce_logits(scale, used, target, out, logits, r)
 
@@ -104,6 +112,7 @@
         lax.ppermute(passages, ("xh", "xl"), both),
     ]
     mine = lax.all_to_all(jnp.broadcast_to(head, (steps,) + head.shape), "y", 0, 0)
+    mine, *pieces = lax.optimization_barrier((mine, *pieces))
     other = lax.ppermute(mine, "core", flip)
 
     slots = negative_ids.shape[2]
@@ -112,7 +121,28 @@
     packed = jnp.concatenate(
         [positives, jnp.pad(listed, ((0, 0), (0, BLOCK - slots)), constant_values=-1)], axis=0
     )
+    vmem = pl.BlockSpec(memory_space=pltpu.VMEM)
+    smem = pl.BlockSpec(memory_space=pltpu.SMEM)
+    hbm = pl.BlockSpec(memory_space=pltpu.HBM)
+    in_hbm = functools.partial(pltpu.with_memory_space_constraint, memory_space=pltpu.HBM)
+    params = pltpu.CompilerParams(vmem_limit_bytes=VMEM_BYTES)
+    keys = pl.pallas_call(
+        passage_kernel,
+        out_shape=jax.ShapeDtypeStruct((width, width), jnp.bfloat16),
+        in_specs=[smem] + [hbm] * 6,
+        out_specs=vmem,
+        scratch_shapes=[
+            pltpu.VMEM((width, width), jnp.bfloat16),
+            pltpu.VMEM((width, width), jnp.bfloat16),
+            pltpu.VMEM((2,) + mine.shape, jnp.bfloat16),
+            pltpu.VMEM((4,) + passages.shape, jnp.bfloat16),
+            pltpu.SemaphoreType.DMA((6,)),
+        ],
+        compiler_params=params,
+    )(core[None], *map(in_hbm, (mine, other, *pieces)))
+
     met_lists = lax.all_to_all(jnp.broadcast_to(packed, (deep,) + packed.shape), "z", 0, 0)
+    met_lists, keys = lax.optimization_barrier((met_lists, keys))
     wanted, lists = met_lists[:, 0, :], met_lists[:, 1, :slots]
 
     run = 2 * rows
@@ -126,31 +156,19 @@
     tile_id = ((((piece // 2) ^ high) * deep + z) * 2 + ((piece % 2) ^ low)) * tiles + tile % tiles
     used = jnp.any(lists[:, :, None] == tile_id[None, None, :], axis=1).astype(jnp.int32)
 
-    vmem = pl.BlockSpec(memory_space=pltpu.VMEM)
-    full, proj = pl.pallas_call(
-        passage_kernel,
-        out_shape=(jax.ShapeDtypeStruct((width, width), jnp.bfloat16),) * 2,
-        in_specs=[pl.BlockSpec(memory_space=pltpu.SMEM)] + [vmem] * 6,
-        out_specs=(vmem, vmem),
-        compiler_params=pltpu.CompilerParams(vmem_limit_bytes=VMEM_BYTES),
-    )(core[None], mine, other, *pieces)
-
     count = deep * queries.shape[0]
-    hbm = pl.BlockSpec(memory_space=pltpu.HBM)
-    in_hbm = functools.partial(pltpu.with_memory_space_constraint, memory_space=pltpu.HBM)
     stats = pl.pallas_call(
         functools.partial(query_kernel, scale),
         out_shape=jax.ShapeDtypeStruct((deep, 2, BLOCK), jnp.float32),
-        in_specs=[pl.BlockSpec(memory_space=pltpu.SMEM), hbm, vmem, hbm, vmem],
+        in_specs=[smem, hbm, vmem, vmem],
         out_specs=vmem,
         scratch_shapes=[
             pltpu.VMEM((count, width), jnp.bfloat16),
-            pltpu.VMEM((width, width), jnp.bfloat16),
             pltpu.VMEM((width, count), jnp.float32),
-            pltpu.SemaphoreType.DMA((len(PARTS) + 1,)),
+            pltpu.SemaphoreType.DMA((len(PARTS),)),
         ],
-        compiler_params=pltpu.CompilerParams(vmem_limit_bytes=VMEM_BYTES),
-    )(used, in_hbm(gathered), full, in_hbm(proj), target[:, None, :])
+        compiler_params=params,
+    )(used, in_hbm(gathered), keys, target[:, None, :])
 
     home = lax.all_to_all(stats, "z", 0, 0)
     logit = jnp.sum(home[:, 1, :], axis=0)

time: 116 us -> 114 us (0.983)
  local copies, waits for them, and re-layouts: 9.11 us -> 3.61 us
  starting transfers between devices: 40.8 us -> 44.1 us
    all_to_all x1, waiting for transfers between devices: 14.9 us -> 0.01 us  [local(): lax.all_to_all(jnp.broadcast_to(head, (steps,) + head.shape), 'y', 0, 0)]
    ppermute x1, waiting for transfers between devices: 0.01 us -> 9.79 us  [local(): lax.ppermute(passages, 'xh', flip)]
    all_to_all x1, waiting for transfers between devices: 10.1 us -> 2.41 us  [local(): lax.all_to_all(jnp.broadcast_to(packed, (deep,) + packed.shape), 'z', 0, 0)]
    ppermute x1, waiting for transfers between devices: 0.01 us -> 5.51 us  [local(): lax.ppermute(passages, ('xh', 'xl'), both)]
    unnamed x19 -> x17, local copies, waits for them, and re-layouts: 6.47 us -> 0.99 us
    ppermute x1, waiting for transfers between devices: 0.01 us -> 3.56 us  [local(): lax.ppermute(passages, 'xl', flip)]
    pallas_call x1, Pallas kernels: 10.8 us -> 7.64 us  [local(): pl.pallas_call(functools.partial(query_kernel, scale), out_shape=jax.Shap...]
    pallas_call x1, Pallas kernels: 3.67 us -> 6.72 us  [local(): pl.pallas_call(passage_kernel, out_shape=jax.ShapeDtypeStruct((width, wid...]
  transfers between devices with their start and end apart: 8 -> 8, of which waited for: 3 -> 6; matrix products, arithmetic and copies ran while one was open for 3% -> 3% of each run, Pallas kernels for 3% -> 6%
where the time goes in v5:
time: 114 us; the launch traced here: 112 us
  starting transfers between devices  44.1 us (39%)
  waiting for transfers between devices  34.9 us (31%)
  Pallas kernels  14.4 us (13%)
  between operations  14.2 us (12%)
  local copies, waits for them, and re-layouts  3.61 us (3%)
  other arithmetic  1.22 us (1%)
    all_to_all x1, starting transfers between devices, local(): lax.all_to_all(jnp.broadcast_to(packed, (deep,) + packed.shape), 'z', 0, 0)  16 us
    all_to_all x1, waiting for transfers between devices, local(): home = lax.all_to_all(stats, 'z', 0, 0)  10.1 us
    ppermute x1, waiting for transfers between devices, local(): lax.ppermute(passages, 'xh', flip)  9.79 us
    ppermute x1, starting transfers between devices, local(): lax.ppermute(passages, 'xh', flip)  8.5 us
    pallas_call x1, Pallas kernels, local(): pl.pallas_call(functools.partial(query_kernel, scale), out_shape=jax.Shap...  7.64 us
    all_to_all x1, starting transfers between devices, local(): lax.all_to_all(jnp.broadcast_to(head, (steps,) + head.shape), 'y', 0, 0)  7.1 us
    pallas_call x1, Pallas kernels, local(): pl.pallas_call(passage_kernel, out_shape=jax.ShapeDtypeStruct((width, wid...  6.72 us
    all_to_all x1, starting transfers between devices, local(): home = lax.all_to_all(stats, 'z', 0, 0)  5.89 us
  transfers between devices with their start and end apart: 8, of which 6 were waited for; matrix products, arithmetic and copies ran while one was open for 3% of the time, Pallas kernels for 6%

profile of v5, /device:TPU:6, one launch (start us, length us, event | category | flops | bytes accessed | tf_op | source)
XLA Modules:
  0.0 112.5 jit_solution(8253070233776561712)
XLA Ops:
  6.5 0.7 all-gather.3.cloned.1.call-update
  7.3 2.0 %broadcast_in_dim.30 = bf16[8,64,1024]{2,1,0:T(8,128)(2,1)} broadcast(bf16[64,1024]{1,0:T(8,128)(2,1)} %param.8), dimensions={1,2} | broadcast | bytes 1179648 | tf_op jit(solution)/shard_map/broadcast_in_dim | solution.py:114
  9.3 7.1 %all-to-all-start.1 = ((bf16[8,64,1024]{2,1,0:T(8,128)(2,1)}), bf16[8,64,1024]{2,1,0:T(8,128)(2,1)S(1)}, u32[]{:S(2)}, u32[]{:S(2)}) async-start(bf16[8,64,1024]{2,1,0:T(8,128)(2,1)} %broadcast_in_dim.30), calls=%async_computation.1 | async-start | bytes 2097152 | tf_op jit(solution)/shard_map/all_to_all | solution.py:114
  16.4 2.7 %collective-permute-start = (bf16[256,1024]{1,0:T(8,128)(2,1)S(1)}, bf16[256,1024]{1,0:T(8,128)(2,1)S(1)}, u32[]{:S(2)}, u32[]{:S(2)}) collective-permute-start(bf16[256,1024]{1,0:T(8,128)(2,1)S(1)} %bitcast.44), channel_id=1, source_target_pairs={{0,1},{1,0},{2,3},{3,2},{4,5},{5,4},{6,7},{7,6},{8,9},{9,8},{10,11... | collective-permute-start | bytes 1572872 | tf_op jit(solution)/shard_map/ppermute | solution.py:110
  19.1 8.5 %collective-permute-start.1 = (bf16[256,1024]{1,0:T(8,128)(2,1)S(1)}, bf16[256,1024]{1,0:T(8,128)(2,1)S(1)}, u32[]{:S(2)}, u32[]{:S(2)}) collective-permute-start(bf16[256,1024]{1,0:T(8,128)(2,1)S(1)} %bitcast.45), channel_id=1, source_target_pairs={{0,384},{384,0},{1,385},{385,1},{2,386},{386,2},{3,387},{387,3},{4... | collective-permute-start | bytes 1572872 | tf_op jit(solution)/shard_map/ppermute | solution.py:111
  27.6 1.9 %collective-permute-start.2 = (bf16[256,1024]{1,0:T(8,128)(2,1)S(1)}, bf16[256,1024]{1,0:T(8,128)(2,1)S(1)}, u32[]{:S(2)}, u32[]{:S(2)}) collective-permute-start(bf16[256,1024]{1,0:T(8,128)(2,1)S(1)} %bitcast.46), channel_id=1, source_target_pairs={{0,385},{1,384},{384,1},{385,0},{2,387},{3,386},{386,3},{387,2},{4... | collective-permute-start | bytes 1572872 | tf_op jit(solution)/shard_map/ppermute | solution.py:112
  29.6 3.6 %collective-permute-done.p1 = bf16[256,1024]{1,0:T(8,128)(2,1)S(1)} collective-permute-done((bf16[256,1024]{1,0:T(8,128)(2,1)S(1)}, bf16[256,1024]{1,0:T(8,128)(2,1)S(1)}, u32[]{:S(2)}, u32[]{:S(2)}) %collective-permute-start) | collective-permute-done | bytes 524320 | tf_op jit(solution)/shard_map/ppermute | solution.py:110
  33.1 9.8 %collective-permute-done.1.p2 = bf16[256,1024]{1,0:T(8,128)(2,1)S(1)} collective-permute-done((bf16[256,1024]{1,0:T(8,128)(2,1)S(1)}, bf16[256,1024]{1,0:T(8,128)(2,1)S(1)}, u32[]{:S(2)}, u32[]{:S(2)}) %collective-permute-start.1) | collective-permute-done | bytes 524320 | tf_op jit(solution)/shard_map/ppermute | solution.py:111
  42.9 5.5 %collective-permute-done.2.p3 = bf16[256,1024]{1,0:T(8,128)(2,1)S(1)} collective-permute-done((bf16[256,1024]{1,0:T(8,128)(2,1)S(1)}, bf16[256,1024]{1,0:T(8,128)(2,1)S(1)}, u32[]{:S(2)}, u32[]{:S(2)}) %collective-permute-start.2) | collective-permute-done | bytes 524320 | tf_op jit(solution)/shard_map/ppermute | solution.py:112
  48.4 0.0 all-to-all-done.1.mine
  48.5 1.9 %collective-permute-start.3 = (bf16[8,64,1024]{2,1,0:T(8,128)(2,1)S(1)}, bf16[8,64,1024]{2,1,0:T(8,128)(2,1)S(1)}, u32[]{:S(2)}, u32[]{:S(2)}) collective-permute-start(bf16[8,64,1024]{2,1,0:T(8,128)(2,1)S(1)} %all-to-all-done.1.mine), channel_id=1, source_target_pairs={{0,2},{2,0},{1,3},{3,1},{4,6},{6,4},{5,7},{7,5},{8,10},{10,8},{9,1... | collective-permute-start | bytes 3145736 | tf_op jit(solution)/shard_map/ppermute | solution.py:116
  51.1 0.6 broadcast_in_dim.28
  51.7 16.0 %all-to-all-start = ((s32[12,2,128]{2,1,0:T(2,128)}), s32[12,2,128]{2,1,0:T(2,128)S(1)}, u32[]{:S(2)}, u32[]{:S(2)}) async-start(s32[12,2,128]{2,1,0:T(2,128)} %broadcast_in_dim.28), calls=%async_computation | async-start | bytes 24576 | tf_op jit(solution)/shard_map/all_to_all | solution.py:144
  67.8 1.0 copy-done.1
  68.8 6.7 %shard_map.64.keys = bf16[1024,1024]{1,0:T(8,128)(2,1)S(1)} custom-call(s32[1]{0:T(128)} %bitcast.2.core, bf16[8,64,1024]{2,1,0:T(8,128)(2,1)} %copy-done, bf16[8,64,1024]{2,1,0:T(8,128)(2,1)} %copy-done.1, bf16[256,1024]{1,0:T(8,128)(2,1)} %bitcast.43, bf16[256,1024]{1,0:T(8,128)(2,1)} %copy-done.3, bf16[256,1024]{1,0:T(8,128)(2,1)} %copy-done.4, ...), custom_call_target="tpu_custom_call" | custom-call | tf_op jit(solution)/shard_map/pallas_call | solution.py:129
  75.5 2.4 %all-to-all-done = s32[12,2,128]{2,1,0:T(2,128)S(1)} async-done(((s32[12,2,128]{2,1,0:T(2,128)}), s32[12,2,128]{2,1,0:T(2,128)S(1)}, u32[]{:S(2)}, u32[]{:S(2)}) %all-to-all-start) | async-done | bytes 12320 | tf_op jit(solution)/shard_map/all_to_all | solution.py:144
  78.0 0.4 compare_reduce_fusion
  78.3 0.1 and_select_fusion.3.target
  78.4 2.8 %all-gather.3.cloned.1.call-done = bf16[1,1536,1024]{2,1,0:T(8,128)(2,1)} async-done(((bf16[1,128,1024]{2,1,0:T(8,128)(2,1)}), bf16[1,1536,1024]{2,1,0:T(8,128)(2,1)}) %all-gather.3.cloned.1.call-update) | async-done | bytes 3145744 | tf_op jit(solution)/shard_map/all_gather | solution.py:106
  81.2 7.6 %shard_map.65 = f32[12,2,128]{2,1,0:T(2,128)} custom-call(s32[12,8]{1,0:T(8,128)S(1)} %convert_element_type.3.used, bf16[1536,1024]{1,0:T(8,128)(2,1)} %bitcast.42, bf16[1024,1024]{1,0:T(8,128)(2,1)S(1)} %shard_map.64.keys, s32[12,1,128]{2,1,0:T(1,128)S(1)} %and_select_fusion.3.target), custom_call_target="tpu_custom_call" | custom-call | tf_op jit(solution)/shard_map/pallas_call | solution.py:160
  88.9 5.9 %all-to-all-start.2 = ((f32[12,2,128]{2,1,0:T(2,128)}), f32[12,2,128]{2,1,0:T(2,128)S(1)}, u32[]{:S(2)}, u32[]{:S(2)}) async-start(f32[12,2,128]{2,1,0:T(2,128)} %shard_map.65), calls=%async_computation.2 | async-start | bytes 24576 | tf_op jit(solution)/shard_map/all_to_all | solution.py:173
  94.8 0.1 compare_reduce_fusion.1
  94.9 10.1 %all-to-all-done.2 = f32[12,2,128]{2,1,0:T(2,128)S(1)} async-done(((f32[12,2,128]{2,1,0:T(2,128)}), f32[12,2,128]{2,1,0:T(2,128)S(1)}, u32[]{:S(2)}, u32[]{:S(2)}) %all-to-all-start.2) | async-done | bytes 12320 | tf_op jit(solution)/shard_map/all_to_all | solution.py:173
  105.1 0.5 fusion.10
  (28 shorter events, 0.2 us)
Async XLA Ops:
  6.5 9.8 %copy-start.2 = (bf16[1,256,1024]{2,1,0:T(8,128)(2,1)S(1)}, bf16[1,256,1024]{2,1,0:T(8,128)(2,1)}, u32[]{:S(2)}) copy-start(bf16[1,256,1024]{2,1,0:T(8,128)(2,1)} %param.7) | copy-start | bytes 1572868
  6.5 44.5 %copy-start.7 = (s32[1,1,12]{2,1,0:T(1,128)S(1)}, s32[1,1,12]{2,1,0:T(1,128)}, u32[]{:S(2)}) copy-start(s32[1,1,12]{2,1,0:T(1,128)} %param.10) | copy-start | bytes 148
  6.5 44.5 %copy-start.6 = (s32[1,128]{1,0:T(1,128)S(1)}, s32[1,128]{1,0:T(1,128)}, u32[]{:S(2)}) copy-start(s32[1,128]{1,0:T(1,128)} %param.9) | copy-start | bytes 1540
  6.5 74.7 %all-gather.3.cloned.1.call-start = ((), (), s32[]{:S(2)}) async-start(), calls=%async_computation.3 | async-start | bytes 3407872 | tf_op jit(solution)/shard_map/all_gather | solution.py:106
  9.3 39.2 %all-to-all-start.1 = ((bf16[8,64,1024]{2,1,0:T(8,128)(2,1)}), bf16[8,64,1024]{2,1,0:T(8,128)(2,1)S(1)}, u32[]{:S(2)}, u32[]{:S(2)}) async-start(bf16[8,64,1024]{2,1,0:T(8,128)(2,1)} %broadcast_in_dim.30), calls=%async_computation.1 | async-start | bytes 2097152 | tf_op jit(solution)/shard_map/all_to_all | solution.py:114
  16.4 16.7 %collective-permute-start = (bf16[256,1024]{1,0:T(8,128)(2,1)S(1)}, bf16[256,1024]{1,0:T(8,128)(2,1)S(1)}, u32[]{:S(2)}, u32[]{:S(2)}) collective-permute-start(bf16[256,1024]{1,0:T(8,128)(2,1)S(1)} %bitcast.44), channel_id=1, source_target_pairs={{0,1},{1,0},{2,3},{3,2},{4,5},{5,4},{6,7},{7,6},{8,9},{9,8},{10,11... | collective-permute-start | bytes 1572872 | tf_op jit(solution)/shard_map/ppermute | solution.py:110
  19.1 23.8 %collective-permute-start.1 = (bf16[256,1024]{1,0:T(8,128)(2,1)S(1)}, bf16[256,1024]{1,0:T(8,128)(2,1)S(1)}, u32[]{:S(2)}, u32[]{:S(2)}) collective-permute-start(bf16[256,1024]{1,0:T(8,128)(2,1)S(1)} %bitcast.45), channel_id=1, source_target_pairs={{0,384},{384,0},{1,385},{385,1},{2,386},{386,2},{3,387},{387,3},{4... | collective-permute-start | bytes 1572872 | tf_op jit(solution)/shard_map/ppermute | solution.py:111
  27.6 20.8 %collective-permute-start.2 = (bf16[256,1024]{1,0:T(8,128)(2,1)S(1)}, bf16[256,1024]{1,0:T(8,128)(2,1)S(1)}, u32[]{:S(2)}, u32[]{:S(2)}) collective-permute-start(bf16[256,1024]{1,0:T(8,128)(2,1)S(1)} %bitcast.46), channel_id=1, source_target_pairs={{0,385},{1,384},{384,1},{385,0},{2,387},{3,386},{386,3},{387,2},{4... | collective-permute-start | bytes 1572872 | tf_op jit(solution)/shard_map/ppermute | solution.py:112
  33.1 15.3 %copy-start.3 = (bf16[256,1024]{1,0:T(8,128)(2,1)}, bf16[256,1024]{1,0:T(8,128)(2,1)S(1)}, u32[]{:S(2)}) copy-start(bf16[256,1024]{1,0:T(8,128)(2,1)S(1)} %collective-permute-done.p1) | copy-start | bytes 1572868
  42.9 24.9 %copy-start.4 = (bf16[256,1024]{1,0:T(8,128)(2,1)}, bf16[256,1024]{1,0:T(8,128)(2,1)S(1)}, u32[]{:S(2)}) copy-start(bf16[256,1024]{1,0:T(8,128)(2,1)S(1)} %collective-permute-done.1.p2) | copy-start | bytes 1572868
  48.4 19.4 %copy-start.5 = (bf16[256,1024]{1,0:T(8,128)(2,1)}, bf16[256,1024]{1,0:T(8,128)(2,1)S(1)}, u32[]{:S(2)}) copy-start(bf16[256,1024]{1,0:T(8,128)(2,1)S(1)} %collective-permute-done.2.p3) | copy-start | bytes 1572868
  48.4 20.4 %copy-start = (bf16[8,64,1024]{2,1,0:T(8,128)(2,1)}, bf16[8,64,1024]{2,1,0:T(8,128)(2,1)S(1)}, u32[]{:S(2)}) copy-start(bf16[8,64,1024]{2,1,0:T(8,128)(2,1)S(1)} %all-to-all-done.1.mine) | copy-start | bytes 3145732
  48.5 19.3 %collective-permute-start.3 = (bf16[8,64,1024]{2,1,0:T(8,128)(2,1)S(1)}, bf16[8,64,1024]{2,1,0:T(8,128)(2,1)S(1)}, u32[]{:S(2)}, u32[]{:S(2)}) collective-permute-start(bf16[8,64,1024]{2,1,0:T(8,128)(2,1)S(1)} %all-to-all-done.1.mine), channel_id=1, source_target_pairs={{0,2},{2,0},{1,3},{3,1},{4,6},{6,4},{5,7},{7,5},{8,10},{10,8},{9,1... | collective-permute-start | bytes 3145736 | tf_op jit(solution)/shard_map/ppermute | solution.py:116
  51.7 26.3 %all-to-all-start = ((s32[12,2,128]{2,1,0:T(2,128)}), s32[12,2,128]{2,1,0:T(2,128)S(1)}, u32[]{:S(2)}, u32[]{:S(2)}) async-start(s32[12,2,128]{2,1,0:T(2,128)} %broadcast_in_dim.28), calls=%async_computation | async-start | bytes 24576 | tf_op jit(solution)/shard_map/all_to_all | solution.py:144
  67.8 1.0 copy-start.1
  88.9 16.1 %all-to-all-start.2 = ((f32[12,2,128]{2,1,0:T(2,128)}), f32[12,2,128]{2,1,0:T(2,128)S(1)}, u32[]{:S(2)}, u32[]{:S(2)}) async-start(f32[12,2,128]{2,1,0:T(2,128)} %shard_map.65), calls=%async_computation.2 | async-start | bytes 24576 | tf_op jit(solution)/shard_map/all_to_all | solution.py:173
Sparse Core Ops, SparseCore 0:
  9.8 71.4 all-gather.2

commit v6 on v5

--- a/solution.py
+++ b/solution.py
@@ -112,15 +112,16 @@
         lax.ppermute(passages, ("xh", "xl"), both),
     ]
     mine = lax.all_to_all(jnp.broadcast_to(head, (steps,) + head.shape), "y", 0, 0)
-    mine, *pieces = lax.optimization_barrier((mine, *pieces))
-    other = lax.ppermute(mine, "core", flip)
-
     slots = negative_ids.shape[2]
     alive = lax.broadcasted_iota(jnp.int32, (1, slots), 1) < negative_count
     listed = jnp.where(alive, negative_ids[0], -1)
     packed = jnp.concatenate(
         [positives, jnp.pad(listed, ((0, 0), (0, BLOCK - slots)), constant_values=-1)], axis=0
     )
+    met_lists = lax.all_gather(packed, "z")
+    mine, met_lists, *pieces = lax.optimization_barrier((mine, met_lists, *pieces))
+    other = lax.ppermute(mine, "core", flip)
+
     vmem = pl.BlockSpec(memory_space=pltpu.VMEM)
     smem = pl.BlockSpec(memory_space=pltpu.SMEM)
     hbm = pl.BlockSpec(memory_space=pltpu.HBM)
@@ -141,8 +142,6 @@
         compiler_params=params,
     )(core[None], *map(in_hbm, (mine, other, *pieces)))
 
-    met_lists = lax.all_to_all(jnp.broadcast_to(packed, (deep,) + packed.shape), "z", 0, 0)
-    met_lists, keys = lax.optimization_barrier((met_lists, keys))
     wanted, lists = met_lists[:, 0, :], met_lists[:, 1, :slots]
 
     run = 2 * rows

time: 114 us -> 113 us (level)
  blocking collectives: 0 us -> 29.6 us
  starting transfers between devices: 44.1 us -> 28 us
  waiting for transfers between devices: 34.9 us -> 21.1 us
    all_gather x0 -> x1, blocking collectives: none -> 29.6 us  [local(): met_lists = lax.all_gather(packed, 'z')]
    all_to_all x1 -> x0, starting transfers between devices: 16 us -> none  [local(): lax.all_to_all(jnp.broadcast_to(packed, (deep,) + packed.shape), 'z', 0, 0)]
    ppermute x1, waiting for transfers between devices: 9.79 us -> 0.01 us  [local(): lax.ppermute(passages, 'xh', flip)]
    ppermute x1, waiting for transfers between devices: 5.51 us -> 0.01 us  [local(): lax.ppermute(passages, ('xh', 'xl'), both)]
    all_gather x1, waiting for transfers between devices: 2.8 us -> 8.26 us  [local(): gathered = lax.all_gather(queries, 'z', axis=0, tiled=True)]
    ppermute x1, waiting for transfers between devices: 3.56 us -> 0.01 us  [local(): lax.ppermute(passages, 'xl', flip)]
    all_to_all x1 -> x0, waiting for transfers between devices: 2.41 us -> none  [local(): lax.all_to_all(jnp.broadcast_to(packed, (deep,) + packed.shape), 'z', 0, 0)]
    ppermute x1, waiting for transfers between devices: 0.01 us -> 2.05 us  [local(): other = lax.ppermute(mine, 'core', flip)]
  transfers between devices with their start and end apart: 8 -> 7, of which waited for: 6 -> 3; matrix products, arithmetic and copies ran while one was open for 3% -> 2% of each run, Pallas kernels for 6% -> 6%
where the time goes in v6:
time: 113 us; the launch traced here: 112 us
  blocking collectives  29.6 us (26%)
  starting transfers between devices  28 us (25%)
  waiting for transfers between devices  21.1 us (19%)
  Pallas kernels  14.4 us (13%)
  between operations  14.2 us (13%)
  local copies, waits for them, and re-layouts  3.8 us (3%)
  other arithmetic  1.21 us (1%)
    all_gather x1, blocking collectives, local(): met_lists = lax.all_gather(packed, 'z')  29.6 us
    all_to_all x1, waiting for transfers between devices, local(): home = lax.all_to_all(stats, 'z', 0, 0)  10 us
    ppermute x1, starting transfers between devices, local(): lax.ppermute(passages, 'xh', flip)  8.5 us
    all_gather x1, waiting for transfers between devices, local(): gathered = lax.all_gather(queries, 'z', axis=0, tiled=True)  8.26 us
    pallas_call x1, Pallas kernels, local(): pl.pallas_call(functools.partial(query_kernel, scale), out_shape=jax.Shap...  7.64 us
    all_to_all x1, starting transfers between devices, local(): lax.all_to_all(jnp.broadcast_to(head, (steps,) + head.shape), 'y', 0, 0)  7.1 us
    pallas_call x1, Pallas kernels, local(): pl.pallas_call(passage_kernel, out_shape=jax.ShapeDtypeStruct((width, wid...  6.74 us
    all_to_all x1, starting transfers between devices, local(): home = lax.all_to_all(stats, 'z', 0, 0)  5.79 us
  transfers between devices with their start and end apart: 7, of which 3 were waited for; matrix products, arithmetic and copies ran while one was open for 2% of the time, Pallas kernels for 6%

profile of v6, /device:TPU:6, one launch (start us, length us, event | category | flops | bytes accessed | tf_op | source)
XLA Modules:
  0.0 112.2 jit_solution(17211424105823938757)
XLA Ops:
  6.5 0.7 all-gather.5.cloned.1.call-update
  7.3 2.0 %broadcast_in_dim.24 = bf16[8,64,1024]{2,1,0:T(8,128)(2,1)} broadcast(bf16[64,1024]{1,0:T(8,128)(2,1)} %param.8), dimensions={1,2} | broadcast | bytes 1179648 | tf_op jit(solution)/shard_map/broadcast_in_dim | solution.py:114
  9.3 7.1 %all-to-all-start = ((bf16[8,64,1024]{2,1,0:T(8,128)(2,1)}), bf16[8,64,1024]{2,1,0:T(8,128)(2,1)S(1)}, u32[]{:S(2)}, u32[]{:S(2)}) async-start(bf16[8,64,1024]{2,1,0:T(8,128)(2,1)} %broadcast_in_dim.24), calls=%async_computation | async-start | bytes 2097152 | tf_op jit(solution)/shard_map/all_to_all | solution.py:114
  16.4 2.7 %collective-permute-start = (bf16[256,1024]{1,0:T(8,128)(2,1)S(1)}, bf16[256,1024]{1,0:T(8,128)(2,1)S(1)}, u32[]{:S(2)}, u32[]{:S(2)}) collective-permute-start(bf16[256,1024]{1,0:T(8,128)(2,1)S(1)} %bitcast.46), channel_id=1, source_target_pairs={{0,1},{1,0},{2,3},{3,2},{4,5},{5,4},{6,7},{7,6},{8,9},{9,8},{10,11... | collective-permute-start | bytes 1572872 | tf_op jit(solution)/shard_map/ppermute | solution.py:110
  19.1 8.5 %collective-permute-start.1 = (bf16[256,1024]{1,0:T(8,128)(2,1)S(1)}, bf16[256,1024]{1,0:T(8,128)(2,1)S(1)}, u32[]{:S(2)}, u32[]{:S(2)}) collective-permute-start(bf16[256,1024]{1,0:T(8,128)(2,1)S(1)} %bitcast.47), channel_id=1, source_target_pairs={{0,384},{384,0},{1,385},{385,1},{2,386},{386,2},{3,387},{387,3},{4... | collective-permute-start | bytes 1572872 | tf_op jit(solution)/shard_map/ppermute | solution.py:111
  27.6 1.9 %collective-permute-start.2 = (bf16[256,1024]{1,0:T(8,128)(2,1)S(1)}, bf16[256,1024]{1,0:T(8,128)(2,1)S(1)}, u32[]{:S(2)}, u32[]{:S(2)}) collective-permute-start(bf16[256,1024]{1,0:T(8,128)(2,1)S(1)} %bitcast.48), channel_id=1, source_target_pairs={{0,385},{1,384},{384,1},{385,0},{2,387},{3,386},{386,3},{387,2},{4... | collective-permute-start | bytes 1572872 | tf_op jit(solution)/shard_map/ppermute | solution.py:112
  30.3 29.6 %all-gather.2 = s32[12,2,128]{2,1,0:T(2,128)S(1)} all-gather(s32[1,2,128]{2,1,0:T(2,128)S(1)} %fusion.5), channel_id=2, replica_groups=mesh['xh'=2,'z'=12,'y'=8,'core'=2,'xl'=2] {'z'}, dimensions={0}, use_global_device_ids=true | all-gather | bytes 13312 | tf_op jit(solution)/shard_map/all_gather | solution.py:121
  59.8 0.0 collective-permute-done.p1
  59.8 0.0 collective-permute-done.1.p2
  59.9 0.0 collective-permute-done.2.p3
  59.9 0.8 copy-done.3
  60.6 0.0 all-to-all-done.mine
  60.7 1.9 %collective-permute-start.3 = (bf16[8,64,1024]{2,1,0:T(8,128)(2,1)S(1)}, bf16[8,64,1024]{2,1,0:T(8,128)(2,1)S(1)}, u32[]{:S(2)}, u32[]{:S(2)}) collective-permute-start(bf16[8,64,1024]{2,1,0:T(8,128)(2,1)S(1)} %all-to-all-done.mine), channel_id=1, source_target_pairs={{0,2},{2,0},{1,3},{3,1},{4,6},{6,4},{5,7},{7,5},{8,10},{10,8},{9,1... | collective-permute-start | bytes 3145736 | tf_op jit(solution)/shard_map/ppermute | solution.py:123
  62.7 0.4 compare_reduce_fusion
  63.0 0.1 and_select_fusion.3.target
  63.1 2.1 %collective-permute-done.3.other = bf16[8,64,1024]{2,1,0:T(8,128)(2,1)S(1)} collective-permute-done((bf16[8,64,1024]{2,1,0:T(8,128)(2,1)S(1)}, bf16[8,64,1024]{2,1,0:T(8,128)(2,1)S(1)}, u32[]{:S(2)}, u32[]{:S(2)}) %collective-permute-start.3) | collective-permute-done | bytes 1048608 | tf_op jit(solution)/shard_map/ppermute | solution.py:123
  65.2 1.0 copy-done.1
  66.2 6.7 %shard_map.64.keys = bf16[1024,1024]{1,0:T(8,128)(2,1)S(1)} custom-call(s32[1]{0:T(128)} %bitcast.5.core, bf16[8,64,1024]{2,1,0:T(8,128)(2,1)} %copy-done, bf16[8,64,1024]{2,1,0:T(8,128)(2,1)} %copy-done.1, bf16[256,1024]{1,0:T(8,128)(2,1)} %bitcast.45, bf16[256,1024]{1,0:T(8,128)(2,1)} %copy-done.3, bf16[256,1024]{1,0:T(8,128)(2,1)} %copy-done.4, ...), custom_call_target="tpu_custom_call" | custom-call | tf_op jit(solution)/shard_map/pallas_call | solution.py:130
  72.9 8.3 %all-gather.5.cloned.1.call-done = bf16[1,1536,1024]{2,1,0:T(8,128)(2,1)} async-done(((bf16[1,128,1024]{2,1,0:T(8,128)(2,1)}), bf16[1,1536,1024]{2,1,0:T(8,128)(2,1)}) %all-gather.5.cloned.1.call-update) | async-done | bytes 3145744 | tf_op jit(solution)/shard_map/all_gather | solution.py:106
  81.2 7.6 %shard_map.65 = f32[12,2,128]{2,1,0:T(2,128)} custom-call(s32[12,8]{1,0:T(8,128)S(1)} %convert_element_type.3.used, bf16[1536,1024]{1,0:T(8,128)(2,1)} %bitcast.44, bf16[1024,1024]{1,0:T(8,128)(2,1)S(1)} %shard_map.64.keys, s32[12,1,128]{2,1,0:T(1,128)S(1)} %and_select_fusion.3.target), custom_call_target="tpu_custom_call" | custom-call | tf_op jit(solution)/shard_map/pallas_call | solution.py:159
  88.8 5.8 %all-to-all-start.1 = ((f32[12,2,128]{2,1,0:T(2,128)}), f32[12,2,128]{2,1,0:T(2,128)S(1)}, u32[]{:S(2)}, u32[]{:S(2)}) async-start(f32[12,2,128]{2,1,0:T(2,128)} %shard_map.65), calls=%async_computation.1 | async-start | bytes 24576 | tf_op jit(solution)/shard_map/all_to_all | solution.py:172
  94.6 0.1 compare_reduce_fusion.1
  94.7 10.0 %all-to-all-done.1 = f32[12,2,128]{2,1,0:T(2,128)S(1)} async-done(((f32[12,2,128]{2,1,0:T(2,128)}), f32[12,2,128]{2,1,0:T(2,128)S(1)}, u32[]{:S(2)}, u32[]{:S(2)}) %all-to-all-start.1) | async-done | bytes 12320 | tf_op jit(solution)/shard_map/all_to_all | solution.py:172
  104.8 0.5 fusion.11
  (26 shorter events, 0.2 us)
Async XLA Ops:
  6.5 9.8 %copy-start.2 = (bf16[1,256,1024]{2,1,0:T(8,128)(2,1)S(1)}, bf16[1,256,1024]{2,1,0:T(8,128)(2,1)}, u32[]{:S(2)}) copy-start(bf16[1,256,1024]{2,1,0:T(8,128)(2,1)} %param.7) | copy-start | bytes 1572868
  6.5 23.7 %copy-start.7 = (s32[1,1,12]{2,1,0:T(1,128)S(1)}, s32[1,1,12]{2,1,0:T(1,128)}, u32[]{:S(2)}) copy-start(s32[1,1,12]{2,1,0:T(1,128)} %param.10) | copy-start | bytes 148
  6.5 23.7 %copy-start.6 = (s32[1,128]{1,0:T(1,128)S(1)}, s32[1,128]{1,0:T(1,128)}, u32[]{:S(2)}) copy-start(s32[1,128]{1,0:T(1,128)} %param.9) | copy-start | bytes 1540
  6.5 74.7 %all-gather.5.cloned.1.call-start = ((), (), s32[]{:S(2)}) async-start(), calls=%async_computation.2 | async-start | bytes 3407872 | tf_op jit(solution)/shard_map/all_gather | solution.py:106
  9.3 51.4 %all-to-all-start = ((bf16[8,64,1024]{2,1,0:T(8,128)(2,1)}), bf16[8,64,1024]{2,1,0:T(8,128)(2,1)S(1)}, u32[]{:S(2)}, u32[]{:S(2)}) async-start(bf16[8,64,1024]{2,1,0:T(8,128)(2,1)} %broadcast_in_dim.24), calls=%async_computation | async-start | bytes 2097152 | tf_op jit(solution)/shard_map/all_to_all | solution.py:114
  16.4 43.5 %collective-permute-start = (bf16[256,1024]{1,0:T(8,128)(2,1)S(1)}, bf16[256,1024]{1,0:T(8,128)(2,1)S(1)}, u32[]{:S(2)}, u32[]{:S(2)}) collective-permute-start(bf16[256,1024]{1,0:T(8,128)(2,1)S(1)} %bitcast.46), channel_id=1, source_target_pairs={{0,1},{1,0},{2,3},{3,2},{4,5},{5,4},{6,7},{7,6},{8,9},{9,8},{10,11... | collective-permute-start | bytes 1572872 | tf_op jit(solution)/shard_map/ppermute | solution.py:110
  19.1 40.7 %collective-permute-start.1 = (bf16[256,1024]{1,0:T(8,128)(2,1)S(1)}, bf16[256,1024]{1,0:T(8,128)(2,1)S(1)}, u32[]{:S(2)}, u32[]{:S(2)}) collective-permute-start(bf16[256,1024]{1,0:T(8,128)(2,1)S(1)} %bitcast.47), channel_id=1, source_target_pairs={{0,384},{384,0},{1,385},{385,1},{2,386},{386,2},{3,387},{387,3},{4... | collective-permute-start | bytes 1572872 | tf_op jit(solution)/shard_map/ppermute | solution.py:111
  27.6 32.2 %collective-permute-start.2 = (bf16[256,1024]{1,0:T(8,128)(2,1)S(1)}, bf16[256,1024]{1,0:T(8,128)(2,1)S(1)}, u32[]{:S(2)}, u32[]{:S(2)}) collective-permute-start(bf16[256,1024]{1,0:T(8,128)(2,1)S(1)} %bitcast.48), channel_id=1, source_target_pairs={{0,385},{1,384},{384,1},{385,0},{2,387},{3,386},{386,3},{387,2},{4... | collective-permute-start | bytes 1572872 | tf_op jit(solution)/shard_map/ppermute | solution.py:112
  59.8 0.8 copy-start.3
  59.8 5.4 %copy-start.4 = (bf16[256,1024]{1,0:T(8,128)(2,1)}, bf16[256,1024]{1,0:T(8,128)(2,1)S(1)}, u32[]{:S(2)}) copy-start(bf16[256,1024]{1,0:T(8,128)(2,1)S(1)} %collective-permute-done.1.p2) | copy-start | bytes 1572868
  60.6 4.6 %copy-start.5 = (bf16[256,1024]{1,0:T(8,128)(2,1)}, bf16[256,1024]{1,0:T(8,128)(2,1)S(1)}, u32[]{:S(2)}) copy-start(bf16[256,1024]{1,0:T(8,128)(2,1)S(1)} %collective-permute-done.2.p3) | copy-start | bytes 1572868
  60.7 5.5 %copy-start = (bf16[8,64,1024]{2,1,0:T(8,128)(2,1)}, bf16[8,64,1024]{2,1,0:T(8,128)(2,1)S(1)}, u32[]{:S(2)}) copy-start(bf16[8,64,1024]{2,1,0:T(8,128)(2,1)S(1)} %all-to-all-done.mine) | copy-start | bytes 3145732
  60.7 4.5 %collective-permute-start.3 = (bf16[8,64,1024]{2,1,0:T(8,128)(2,1)S(1)}, bf16[8,64,1024]{2,1,0:T(8,128)(2,1)S(1)}, u32[]{:S(2)}, u32[]{:S(2)}) collective-permute-start(bf16[8,64,1024]{2,1,0:T(8,128)(2,1)S(1)} %all-to-all-done.mine), channel_id=1, source_target_pairs={{0,2},{2,0},{1,3},{3,1},{4,6},{6,4},{5,7},{7,5},{8,10},{10,8},{9,1... | collective-permute-start | bytes 3145736 | tf_op jit(solution)/shard_map/ppermute | solution.py:123
  65.2 1.0 copy-start.1
  88.8 15.9 %all-to-all-start.1 = ((f32[12,2,128]{2,1,0:T(2,128)}), f32[12,2,128]{2,1,0:T(2,128)S(1)}, u32[]{:S(2)}, u32[]{:S(2)}) async-start(f32[12,2,128]{2,1,0:T(2,128)} %shard_map.65), calls=%async_computation.1 | async-start | bytes 24576 | tf_op jit(solution)/shard_map/all_to_all | solution.py:172
Sparse Core Ops, SparseCore 0:
  9.8 71.3 all-gather.4

commit v7 on v6

--- a/solution.py
+++ b/solution.py
@@ -10,6 +10,7 @@
 
 BLOCK = 128
 FLOOR = -1e30
+LOG2E = 1.4426950408889634
 NT = (((1,), (1,)), ((), ()))
 VMEM_BYTES = 24 * 1024 * 1024
 PARTS = (512, 1024)
@@ -17,24 +18,21 @@
 
 def passage_kernel(core, mine, other, p0, p1, p2, p3, keys, full, proj, head_buf, piece_buf, sems):
     pieces = (p0, p1, p2, p3)
-    heads = [
-        pltpu.make_async_copy(half, head_buf.at[i], sems.at[i]) for i, half in enumerate((mine, other))
-    ]
+    near = pltpu.make_async_copy(mine, head_buf, sems.at[0])
     loads = [
-        pltpu.make_async_copy(piece, piece_buf.at[i], sems.at[2 + i])
+        pltpu.make_async_copy(piece, piece_buf.at[i], sems.at[1 + i])
         for i, piece in enumerate(pieces)
     ]
-    for copy in heads + loads:
+    for copy in [near] + loads:
         copy.start()
-    for copy in heads:
-        copy.wait()
+    near.wait()
     steps, depth, _ = mine.shape
     here = core[0]
     for y in range(steps):
         first = pl.multiple_of((2 * y + here) * depth, depth)
         second = pl.multiple_of((2 * y + 1 - here) * depth, depth)
-        full[pl.ds(first, depth), :] = head_buf[0, y]
-        full[pl.ds(second, depth), :] = head_buf[1, y]
+        full[pl.ds(first, depth), :] = head_buf[y]
+        full[pl.ds(second, depth), :] = other[y]
     for copy in loads:
         copy.wait()
     rows = p0.shape[0]
@@ -82,7 +80,7 @@
         acc = jnp.zeros((8, BLOCK), jnp.float32)
         for j in range(tiles):
             tile = logits[pl.ds(j * BLOCK, BLOCK), lanes]
-            term = jnp.exp(jnp.where(live[j], tile - top, FLOOR) * scale)
+            term = jnp.exp2((tile - jnp.where(live[j], top, -FLOOR)) * (scale * LOG2E))
             acc = acc + jnp.sum(term.reshape(BLOCK // 8, 8, BLOCK), axis=0)
         acc = jnp.sum(acc, axis=0, keepdims=True)
         some = acc > 0.0
@@ -130,17 +128,17 @@
     keys = pl.pallas_call(
         passage_kernel,
         out_shape=jax.ShapeDtypeStruct((width, width), jnp.bfloat16),
-        in_specs=[smem] + [hbm] * 6,
+        in_specs=[smem, hbm, vmem] + [hbm] * 4,
         out_specs=vmem,
         scratch_shapes=[
             pltpu.VMEM((width, width), jnp.bfloat16),
             pltpu.VMEM((width, width), jnp.bfloat16),
-            pltpu.VMEM((2,) + mine.shape, jnp.bfloat16),
+            pltpu.VMEM(mine.shape, jnp.bfloat16),
             pltpu.VMEM((4,) + passages.shape, jnp.bfloat16),
-            pltpu.SemaphoreType.DMA((6,)),
+            pltpu.SemaphoreType.DMA((5,)),
         ],
         compiler_params=params,
-    )(core[None], *map(in_hbm, (mine, other, *pieces)))
+    )(core[None], in_hbm(mine), other, *map(in_hbm, pieces))
 
     wanted, lists = met_lists[:, 0, :], met_lists[:, 1, :slots]
 
@@ -155,6 +153,8 @@
     tile_id = ((((piece // 2) ^ high) * deep + z) * 2 + ((piece % 2) ^ low)) * tiles + tile % tiles
     used = jnp.any(lists[:, :, None] == tile_id[None, None, :], axis=1).astype(jnp.int32)
 
+    also_listed = jnp.any(listed[0][:, None] == positives // BLOCK, axis=0).astype(jnp.int32)
+    used, also_listed = lax.optimization_barrier((used, also_listed))
     count = deep * queries.shape[0]
     stats = pl.pallas_call(
         functools.partial(query_kernel, scale),
@@ -171,8 +171,7 @@
 
     home = lax.all_to_all(stats, "z", 0, 0)
     logit = jnp.sum(home[:, 1, :], axis=0)
-    also_listed = jnp.any(listed[0][:, None] == positives // BLOCK, axis=0)
-    extra = jnp.where(also_listed, FLOOR, logit)
+    extra = jnp.where(also_listed > 0, FLOOR, logit)
     top = jnp.maximum(jnp.max(home[:, 0, :], axis=0), extra)
     total = jnp.sum(jnp.exp(home[:, 0, :] - top), axis=0) + jnp.exp(extra - top)
     return (top + jnp.log(total) - logit)[None, :]

time: 113 us -> 111 us (0.982)
  blocking collectives: 29.6 us -> 45.2 us
  waiting for transfers between devices: 21.1 us -> 11.5 us
  starting transfers between devices: 28 us -> 22.2 us
  Pallas kernels: 14.4 us -> 13.1 us
    all_to_all x0 -> x1, blocking collectives: none -> 15.6 us  [local(): home = lax.all_to_all(stats, 'z', 0, 0)]
    all_to_all x1 -> x0, waiting for transfers between devices: 10 us -> none  [local(): home = lax.all_to_all(stats, 'z', 0, 0)]
    all_to_all x1 -> x0, starting transfers between devices: 5.79 us -> none  [local(): home = lax.all_to_all(stats, 'z', 0, 0)]
  transfers between devices with their start and end apart: 7 -> 6, of which waited for: 3 -> 2; matrix products, arithmetic and copies ran while one was open for 2% -> 2% of each run, Pallas kernels for 6% -> 6%
where the time goes in v7:
time: 111 us
  blocking collectives  45.2 us (41%)
  starting transfers between devices  22.2 us (20%)
  between operations  14.2 us (13%)
  Pallas kernels  13.1 us (12%)
  waiting for transfers between devices  11.5 us (10%)
  local copies, waits for them, and re-layouts  3.63 us (3%)
  other arithmetic  1.22 us (1%)
    all_gather x1, blocking collectives, local(): met_lists = lax.all_gather(packed, 'z')  29.6 us
    all_to_all x1, blocking collectives, local(): home = lax.all_to_all(stats, 'z', 0, 0)  15.6 us
    all_gather x1, waiting for transfers between devices, local(): gathered = lax.all_gather(queries, 'z', axis=0, tiled=True)  8.83 us
    ppermute x1, starting transfers between devices, local(): lax.ppermute(passages, 'xh', flip)  8.5 us
    all_to_all x1, starting transfers between devices, local(): lax.all_to_all(jnp.broadcast_to(head, (steps,) + head.shape), 'y', 0, 0)  7.1 us
    pallas_call x1, Pallas kernels, local(): pl.pallas_call(functools.partial(query_kernel, scale), out_shape=jax.Shap...  6.65 us
    pallas_call x1, Pallas kernels, local(): pl.pallas_call(passage_kernel, out_shape=jax.ShapeDtypeStruct((width, wid...  6.41 us
    ppermute x1, starting transfers between devices, local(): lax.ppermute(passages, 'xl', flip)  2.74 us
  transfers between devices with their start and end apart: 6, of which 2 were waited for; matrix products, arithmetic and copies ran while one was open for 2% of the time, Pallas kernels for 6%

profile of v7, /device:TPU:6, one launch (start us, length us, event | category | flops | bytes accessed | tf_op | source)
XLA Modules:
  0.0 111.0 jit_solution(13483684207774860580)
XLA Ops:
  6.5 0.0 all-gather.5.cloned.1.call-start
  6.5 0.7 all-gather.5.cloned.1.call-update
  7.3 2.0 %broadcast_in_dim.24 = bf16[8,64,1024]{2,1,0:T(8,128)(2,1)} broadcast(bf16[64,1024]{1,0:T(8,128)(2,1)} %param.8), dimensions={1,2} | broadcast | bytes 1179648 | tf_op jit(solution)/shard_map/broadcast_in_dim | solution.py:112
  9.3 7.1 %all-to-all-start = ((bf16[8,64,1024]{2,1,0:T(8,128)(2,1)}), bf16[8,64,1024]{2,1,0:T(8,128)(2,1)S(1)}, u32[]{:S(2)}, u32[]{:S(2)}) async-start(bf16[8,64,1024]{2,1,0:T(8,128)(2,1)} %broadcast_in_dim.24), calls=%async_computation | async-start | bytes 2097152 | tf_op jit(solution)/shard_map/all_to_all | solution.py:112
  16.4 2.7 %collective-permute-start = (bf16[256,1024]{1,0:T(8,128)(2,1)S(1)}, bf16[256,1024]{1,0:T(8,128)(2,1)S(1)}, u32[]{:S(2)}, u32[]{:S(2)}) collective-permute-start(bf16[256,1024]{1,0:T(8,128)(2,1)S(1)} %bitcast.27), channel_id=1, source_target_pairs={{0,1},{1,0},{2,3},{3,2},{4,5},{5,4},{6,7},{7,6},{8,9},{9,8},{10,11... | collective-permute-start | bytes 1572872 | tf_op jit(solution)/shard_map/ppermute | solution.py:108
  19.1 8.5 %collective-permute-start.1 = (bf16[256,1024]{1,0:T(8,128)(2,1)S(1)}, bf16[256,1024]{1,0:T(8,128)(2,1)S(1)}, u32[]{:S(2)}, u32[]{:S(2)}) collective-permute-start(bf16[256,1024]{1,0:T(8,128)(2,1)S(1)} %bitcast.28), channel_id=1, source_target_pairs={{0,384},{384,0},{1,385},{385,1},{2,386},{386,2},{3,387},{387,3},{4... | collective-permute-start | bytes 1572872 | tf_op jit(solution)/shard_map/ppermute | solution.py:109
  27.6 1.9 %collective-permute-start.2 = (bf16[256,1024]{1,0:T(8,128)(2,1)S(1)}, bf16[256,1024]{1,0:T(8,128)(2,1)}, u32[]{:S(2)}, u32[]{:S(2)}) collective-permute-start(bf16[256,1024]{1,0:T(8,128)(2,1)S(1)} %bitcast.29), channel_id=1, source_target_pairs={{0,385},{1,384},{384,1},{385,0},{2,387},{3,386},{386,3},{387,2},{4... | collective-permute-start | bytes 1572872 | tf_op jit(solution)/shard_map/ppermute | solution.py:110
  30.3 29.6 %all-gather.2 = s32[12,2,128]{2,1,0:T(2,128)S(1)} all-gather(s32[1,2,128]{2,1,0:T(2,128)S(1)} %fusion.5), channel_id=2, replica_groups=mesh['xh'=2,'z'=12,'y'=8,'core'=2,'xl'=2] {'z'}, dimensions={0}, use_global_device_ids=true | all-gather | bytes 13312 | tf_op jit(solution)/shard_map/all_gather | solution.py:119
  59.8 0.0 collective-permute-done.p1
  59.8 0.0 collective-permute-done.1.p2
  59.8 0.8 copy-done.2
  60.6 0.8 copy-done.3
  61.4 0.0 collective-permute-done.2.p3
  61.4 0.0 all-to-all-done.mine
  61.5 1.9 %collective-permute-start.3 = (bf16[8,64,1024]{2,1,0:T(8,128)(2,1)S(1)}, bf16[8,64,1024]{2,1,0:T(8,128)(2,1)S(1)}, u32[]{:S(2)}, u32[]{:S(2)}) collective-permute-start(bf16[8,64,1024]{2,1,0:T(8,128)(2,1)S(1)} %all-to-all-done.mine), channel_id=1, source_target_pairs={{0,2},{2,0},{1,3},{3,1},{4,6},{6,4},{5,7},{7,5},{8,10},{10,8},{9,1... | collective-permute-start | bytes 3145736 | tf_op jit(solution)/shard_map/ppermute | solution.py:121
  63.4 0.1 compare_reduce_fusion.1
  63.6 0.4 compare_reduce_fusion
  63.9 0.1 and_select_fusion.3.target
  64.1 2.0 %collective-permute-done.3.other = bf16[8,64,1024]{2,1,0:T(8,128)(2,1)S(1)} collective-permute-done((bf16[8,64,1024]{2,1,0:T(8,128)(2,1)S(1)}, bf16[8,64,1024]{2,1,0:T(8,128)(2,1)S(1)}, u32[]{:S(2)}, u32[]{:S(2)}) %collective-permute-start.3) | collective-permute-done | bytes 1048608 | tf_op jit(solution)/shard_map/ppermute | solution.py:121
  66.0 6.4 %shard_map.64.keys = bf16[1024,1024]{1,0:T(8,128)(2,1)S(1)} custom-call(s32[1]{0:T(128)} %bitcast.7.core, bf16[8,64,1024]{2,1,0:T(8,128)(2,1)} %copy-done, bf16[8,64,1024]{2,1,0:T(8,128)(2,1)S(1)} %collective-permute-done.3.other, bf16[256,1024]{1,0:T(8,128)(2,1)} %bitcast.26, bf16[256,1024]{1,0:T(8,128)(2,1)} %copy-done.2, bf16[256,1024]{1,0:T(8,128)(2,1)} %copy-done.3, ...), custom_call_target="tpu_custom_call" | custom-call | tf_op jit(solution)/shard_map/pallas_call | solution.py:128
  72.4 8.8 %all-gather.5.cloned.1.call-done = bf16[1,1536,1024]{2,1,0:T(8,128)(2,1)} async-done(((bf16[1,128,1024]{2,1,0:T(8,128)(2,1)}), bf16[1,1536,1024]{2,1,0:T(8,128)(2,1)}) %all-gather.5.cloned.1.call-update) | async-done | bytes 3145744 | tf_op jit(solution)/shard_map/all_gather | solution.py:104
  81.3 6.7 %shard_map.65 = f32[12,2,128]{2,1,0:T(2,128)S(1)} custom-call(s32[12,8]{1,0:T(8,128)S(1)} %convert_element_type.6.used, bf16[1536,1024]{1,0:T(8,128)(2,1)} %bitcast.25, bf16[1024,1024]{1,0:T(8,128)(2,1)S(1)} %shard_map.64.keys, s32[12,1,128]{2,1,0:T(1,128)S(1)} %and_select_fusion.3.target), custom_call_target="tpu_custom_call" | custom-call | tf_op jit(solution)/shard_map/pallas_call | solution.py:159
  87.9 15.6 %all_to_all.10 = f32[12,2,128]{2,1,0:T(2,128)S(1)} all-to-all(f32[12,2,128]{2,1,0:T(2,128)S(1)} %shard_map.65), channel_id=1, replica_groups=mesh['xh'=2,'z'=12,'y'=8,'core'=2,'xl'=2] {'z'}, dimensions={0} | all-to-all | bytes 24576 | tf_op jit(solution)/shard_map/all_to_all | solution.py:172
  103.6 0.5 subtract_bitcast_fusion
  (22 shorter events, 0.1 us)
Async XLA Ops:
  6.5 9.8 %copy-start.1 = (bf16[1,256,1024]{2,1,0:T(8,128)(2,1)S(1)}, bf16[1,256,1024]{2,1,0:T(8,128)(2,1)}, u32[]{:S(2)}) copy-start(bf16[1,256,1024]{2,1,0:T(8,128)(2,1)} %param.7) | copy-start | bytes 1572868
  6.5 23.7 %copy-start.5 = (s32[1,1,12]{2,1,0:T(1,128)S(1)}, s32[1,1,12]{2,1,0:T(1,128)}, u32[]{:S(2)}) copy-start(s32[1,1,12]{2,1,0:T(1,128)} %param.10) | copy-start | bytes 148
  6.5 23.7 %copy-start.4 = (s32[1,128]{1,0:T(1,128)S(1)}, s32[1,128]{1,0:T(1,128)}, u32[]{:S(2)}) copy-start(s32[1,128]{1,0:T(1,128)} %param.9) | copy-start | bytes 1540
  6.5 74.7 %all-gather.5.cloned.1.call-start = ((), (), s32[]{:S(2)}) async-start(), calls=%async_computation.2 | async-start | bytes 3407872 | tf_op jit(solution)/shard_map/all_gather | solution.py:104
  9.3 52.2 %all-to-all-start = ((bf16[8,64,1024]{2,1,0:T(8,128)(2,1)}), bf16[8,64,1024]{2,1,0:T(8,128)(2,1)S(1)}, u32[]{:S(2)}, u32[]{:S(2)}) async-start(bf16[8,64,1024]{2,1,0:T(8,128)(2,1)} %broadcast_in_dim.24), calls=%async_computation | async-start | bytes 2097152 | tf_op jit(solution)/shard_map/all_to_all | solution.py:112
  16.4 43.5 %collective-permute-start = (bf16[256,1024]{1,0:T(8,128)(2,1)S(1)}, bf16[256,1024]{1,0:T(8,128)(2,1)S(1)}, u32[]{:S(2)}, u32[]{:S(2)}) collective-permute-start(bf16[256,1024]{1,0:T(8,128)(2,1)S(1)} %bitcast.27), channel_id=1, source_target_pairs={{0,1},{1,0},{2,3},{3,2},{4,5},{5,4},{6,7},{7,6},{8,9},{9,8},{10,11... | collective-permute-start | bytes 1572872 | tf_op jit(solution)/shard_map/ppermute | solution.py:108
  19.1 40.7 %collective-permute-start.1 = (bf16[256,1024]{1,0:T(8,128)(2,1)S(1)}, bf16[256,1024]{1,0:T(8,128)(2,1)S(1)}, u32[]{:S(2)}, u32[]{:S(2)}) collective-permute-start(bf16[256,1024]{1,0:T(8,128)(2,1)S(1)} %bitcast.28), channel_id=1, source_target_pairs={{0,384},{384,0},{1,385},{385,1},{2,386},{386,2},{3,387},{387,3},{4... | collective-permute-start | bytes 1572872 | tf_op jit(solution)/shard_map/ppermute | solution.py:109
  27.6 33.8 %collective-permute-start.2 = (bf16[256,1024]{1,0:T(8,128)(2,1)S(1)}, bf16[256,1024]{1,0:T(8,128)(2,1)}, u32[]{:S(2)}, u32[]{:S(2)}) collective-permute-start(bf16[256,1024]{1,0:T(8,128)(2,1)S(1)} %bitcast.29), channel_id=1, source_target_pairs={{0,385},{1,384},{384,1},{385,0},{2,387},{3,386},{386,3},{387,2},{4... | collective-permute-start | bytes 1572872 | tf_op jit(solution)/shard_map/ppermute | solution.py:110
  59.8 0.8 copy-start.2
  60.6 0.8 copy-start.3
  61.4 4.6 %copy-start = (bf16[8,64,1024]{2,1,0:T(8,128)(2,1)}, bf16[8,64,1024]{2,1,0:T(8,128)(2,1)S(1)}, u32[]{:S(2)}) copy-start(bf16[8,64,1024]{2,1,0:T(8,128)(2,1)S(1)} %all-to-all-done.mine) | copy-start | bytes 3145732
  61.5 4.6 %collective-permute-start.3 = (bf16[8,64,1024]{2,1,0:T(8,128)(2,1)S(1)}, bf16[8,64,1024]{2,1,0:T(8,128)(2,1)S(1)}, u32[]{:S(2)}, u32[]{:S(2)}) collective-permute-start(bf16[8,64,1024]{2,1,0:T(8,128)(2,1)S(1)} %all-to-all-done.mine), channel_id=1, source_target_pairs={{0,2},{2,0},{1,3},{3,1},{4,6},{6,4},{5,7},{7,5},{8,10},{10,8},{9,1... | collective-permute-start | bytes 3145736 | tf_op jit(solution)/shard_map/ppermute | solution.py:121
Sparse Core Ops, SparseCore 0:
  9.8 71.4 all-gather.4

commit v8 on v7

--- a/solution.py
+++ b/solution.py
@@ -35,11 +35,9 @@
         full[pl.ds(second, depth), :] = other[y]
     for copy in loads:
         copy.wait()
-    rows = p0.shape[0]
-    for i in range(len(pieces)):
-        proj[pl.ds(i * rows, rows), :] = jnp.dot(
-            piece_buf[i], full[...], preferred_element_type=jnp.float32
-        ).astype(proj.dtype)
+    proj[...] = jnp.dot(
+        piece_buf[...].reshape(proj.shape), full[...], preferred_element_type=jnp.float32
+    ).astype(proj.dtype)
     keys[...] = lax.dot_general(
         proj[...], full[...], NT, preferred_element_type=jnp.float32
     ).astype(keys.dtype)

time: 111 us -> 111 us (level)
  no operation moved by 1% of the time
where the time goes in v8:
time: 111 us
  blocking collectives  45.2 us (41%)
  starting transfers between devices  22.2 us (20%)
  between operations  14.2 us (13%)
  Pallas kernels  13.1 us (12%)
  waiting for transfers between devices  11.5 us (10%)
  local copies, waits for them, and re-layouts  3.63 us (3%)
  other arithmetic  1.22 us (1%)
    all_gather x1, blocking collectives, local(): met_lists = lax.all_gather(packed, 'z')  29.6 us
    all_to_all x1, blocking collectives, local(): home = lax.all_to_all(stats, 'z', 0, 0)  15.6 us
    all_gather x1, waiting for transfers between devices, local(): gathered = lax.all_gather(queries, 'z', axis=0, tiled=True)  8.84 us
    ppermute x1, starting transfers between devices, local(): lax.ppermute(passages, 'xh', flip)  8.5 us
    all_to_all x1, starting transfers between devices, local(): lax.all_to_all(jnp.broadcast_to(head, (steps,) + head.shape), 'y', 0, 0)  7.1 us
    pallas_call x1, Pallas kernels, local(): pl.pallas_call(functools.partial(query_kernel, scale), out_shape=jax.Shap...  6.65 us
    pallas_call x1, Pallas kernels, local(): pl.pallas_call(passage_kernel, out_shape=jax.ShapeDtypeStruct((width, wid...  6.4 us
    ppermute x1, starting transfers between devices, local(): lax.ppermute(passages, 'xl', flip)  2.74 us
  transfers between devices with their start and end apart: 6, of which 2 were waited for; matrix products, arithmetic and copies ran while one was open for 2% of the time, Pallas kernels for 6%

profile of v8, /device:TPU:6, one launch (start us, length us, event | category | flops | bytes accessed | tf_op | source)
XLA Modules:
  0.0 111.0 jit_solution(4110141985533874906)
XLA Ops:
  6.5 0.0 all-gather.5.cloned.1.call-start
  6.5 0.7 all-gather.5.cloned.1.call-update
  7.3 2.0 %broadcast_in_dim.24 = bf16[8,64,1024]{2,1,0:T(8,128)(2,1)} broadcast(bf16[64,1024]{1,0:T(8,128)(2,1)} %param.8), dimensions={1,2} | broadcast | bytes 1179648 | tf_op jit(solution)/shard_map/broadcast_in_dim | solution.py:110
  9.3 7.1 %all-to-all-start = ((bf16[8,64,1024]{2,1,0:T(8,128)(2,1)}), bf16[8,64,1024]{2,1,0:T(8,128)(2,1)S(1)}, u32[]{:S(2)}, u32[]{:S(2)}) async-start(bf16[8,64,1024]{2,1,0:T(8,128)(2,1)} %broadcast_in_dim.24), calls=%async_computation | async-start | bytes 2097152 | tf_op jit(solution)/shard_map/all_to_all | solution.py:110
  16.4 2.7 %collective-permute-start = (bf16[256,1024]{1,0:T(8,128)(2,1)S(1)}, bf16[256,1024]{1,0:T(8,128)(2,1)S(1)}, u32[]{:S(2)}, u32[]{:S(2)}) collective-permute-start(bf16[256,1024]{1,0:T(8,128)(2,1)S(1)} %bitcast.27), channel_id=1, source_target_pairs={{0,1},{1,0},{2,3},{3,2},{4,5},{5,4},{6,7},{7,6},{8,9},{9,8},{10,11... | collective-permute-start | bytes 1572872 | tf_op jit(solution)/shard_map/ppermute | solution.py:106
  19.1 8.5 %collective-permute-start.1 = (bf16[256,1024]{1,0:T(8,128)(2,1)S(1)}, bf16[256,1024]{1,0:T(8,128)(2,1)S(1)}, u32[]{:S(2)}, u32[]{:S(2)}) collective-permute-start(bf16[256,1024]{1,0:T(8,128)(2,1)S(1)} %bitcast.28), channel_id=1, source_target_pairs={{0,384},{384,0},{1,385},{385,1},{2,386},{386,2},{3,387},{387,3},{4... | collective-permute-start | bytes 1572872 | tf_op jit(solution)/shard_map/ppermute | solution.py:107
  27.6 1.9 %collective-permute-start.2 = (bf16[256,1024]{1,0:T(8,128)(2,1)S(1)}, bf16[256,1024]{1,0:T(8,128)(2,1)}, u32[]{:S(2)}, u32[]{:S(2)}) collective-permute-start(bf16[256,1024]{1,0:T(8,128)(2,1)S(1)} %bitcast.29), channel_id=1, source_target_pairs={{0,385},{1,384},{384,1},{385,0},{2,387},{3,386},{386,3},{387,2},{4... | collective-permute-start | bytes 1572872 | tf_op jit(solution)/shard_map/ppermute | solution.py:108
  30.3 29.6 %all-gather.2 = s32[12,2,128]{2,1,0:T(2,128)S(1)} all-gather(s32[1,2,128]{2,1,0:T(2,128)S(1)} %fusion.5), channel_id=2, replica_groups=mesh['xh'=2,'z'=12,'y'=8,'core'=2,'xl'=2] {'z'}, dimensions={0}, use_global_device_ids=true | all-gather | bytes 13312 | tf_op jit(solution)/shard_map/all_gather | solution.py:117
  59.8 0.0 collective-permute-done.p1
  59.8 0.0 collective-permute-done.1.p2
  59.8 0.8 copy-done.2
  60.6 0.8 copy-done.3
  61.4 0.0 collective-permute-done.2.p3
  61.4 0.0 all-to-all-done.mine
  61.5 1.9 %collective-permute-start.3 = (bf16[8,64,1024]{2,1,0:T(8,128)(2,1)S(1)}, bf16[8,64,1024]{2,1,0:T(8,128)(2,1)S(1)}, u32[]{:S(2)}, u32[]{:S(2)}) collective-permute-start(bf16[8,64,1024]{2,1,0:T(8,128)(2,1)S(1)} %all-to-all-done.mine), channel_id=1, source_target_pairs={{0,2},{2,0},{1,3},{3,1},{4,6},{6,4},{5,7},{7,5},{8,10},{10,8},{9,1... | collective-permute-start | bytes 3145736 | tf_op jit(solution)/shard_map/ppermute | solution.py:119
  63.4 0.1 compare_reduce_fusion.1
  63.6 0.4 compare_reduce_fusion
  63.9 0.1 and_select_fusion.3.target
  64.1 2.0 %collective-permute-done.3.other = bf16[8,64,1024]{2,1,0:T(8,128)(2,1)S(1)} collective-permute-done((bf16[8,64,1024]{2,1,0:T(8,128)(2,1)S(1)}, bf16[8,64,1024]{2,1,0:T(8,128)(2,1)S(1)}, u32[]{:S(2)}, u32[]{:S(2)}) %collective-permute-start.3) | collective-permute-done | bytes 1048608 | tf_op jit(solution)/shard_map/ppermute | solution.py:119
  66.0 6.4 %shard_map.64.keys = bf16[1024,1024]{1,0:T(8,128)(2,1)S(1)} custom-call(s32[1]{0:T(128)} %bitcast.7.core, bf16[8,64,1024]{2,1,0:T(8,128)(2,1)} %copy-done, bf16[8,64,1024]{2,1,0:T(8,128)(2,1)S(1)} %collective-permute-done.3.other, bf16[256,1024]{1,0:T(8,128)(2,1)} %bitcast.26, bf16[256,1024]{1,0:T(8,128)(2,1)} %copy-done.2, bf16[256,1024]{1,0:T(8,128)(2,1)} %copy-done.3, ...), custom_call_target="tpu_custom_call" | custom-call | tf_op jit(solution)/shard_map/pallas_call | solution.py:126
  72.4 8.8 %all-gather.5.cloned.1.call-done = bf16[1,1536,1024]{2,1,0:T(8,128)(2,1)} async-done(((bf16[1,128,1024]{2,1,0:T(8,128)(2,1)}), bf16[1,1536,1024]{2,1,0:T(8,128)(2,1)}) %all-gather.5.cloned.1.call-update) | async-done | bytes 3145744 | tf_op jit(solution)/shard_map/all_gather | solution.py:102
  81.3 6.7 %shard_map.65 = f32[12,2,128]{2,1,0:T(2,128)S(1)} custom-call(s32[12,8]{1,0:T(8,128)S(1)} %convert_element_type.6.used, bf16[1536,1024]{1,0:T(8,128)(2,1)} %bitcast.25, bf16[1024,1024]{1,0:T(8,128)(2,1)S(1)} %shard_map.64.keys, s32[12,1,128]{2,1,0:T(1,128)S(1)} %and_select_fusion.3.target), custom_call_target="tpu_custom_call" | custom-call | tf_op jit(solution)/shard_map/pallas_call | solution.py:157
  87.9 15.6 %all_to_all.10 = f32[12,2,128]{2,1,0:T(2,128)S(1)} all-to-all(f32[12,2,128]{2,1,0:T(2,128)S(1)} %shard_map.65), channel_id=1, replica_groups=mesh['xh'=2,'z'=12,'y'=8,'core'=2,'xl'=2] {'z'}, dimensions={0} | all-to-all | bytes 24576 | tf_op jit(solution)/shard_map/all_to_all | solution.py:170
  103.6 0.5 subtract_bitcast_fusion
  (22 shorter events, 0.1 us)
Async XLA Ops:
  6.5 9.8 %copy-start.1 = (bf16[1,256,1024]{2,1,0:T(8,128)(2,1)S(1)}, bf16[1,256,1024]{2,1,0:T(8,128)(2,1)}, u32[]{:S(2)}) copy-start(bf16[1,256,1024]{2,1,0:T(8,128)(2,1)} %param.7) | copy-start | bytes 1572868
  6.5 23.7 %copy-start.5 = (s32[1,1,12]{2,1,0:T(1,128)S(1)}, s32[1,1,12]{2,1,0:T(1,128)}, u32[]{:S(2)}) copy-start(s32[1,1,12]{2,1,0:T(1,128)} %param.10) | copy-start | bytes 148
  6.5 23.7 %copy-start.4 = (s32[1,128]{1,0:T(1,128)S(1)}, s32[1,128]{1,0:T(1,128)}, u32[]{:S(2)}) copy-start(s32[1,128]{1,0:T(1,128)} %param.9) | copy-start | bytes 1540
  6.5 74.7 %all-gather.5.cloned.1.call-start = ((), (), s32[]{:S(2)}) async-start(), calls=%async_computation.2 | async-start | bytes 3407872 | tf_op jit(solution)/shard_map/all_gather | solution.py:102
  9.3 52.2 %all-to-all-start = ((bf16[8,64,1024]{2,1,0:T(8,128)(2,1)}), bf16[8,64,1024]{2,1,0:T(8,128)(2,1)S(1)}, u32[]{:S(2)}, u32[]{:S(2)}) async-start(bf16[8,64,1024]{2,1,0:T(8,128)(2,1)} %broadcast_in_dim.24), calls=%async_computation | async-start | bytes 2097152 | tf_op jit(solution)/shard_map/all_to_all | solution.py:110
  16.4 43.5 %collective-permute-start = (bf16[256,1024]{1,0:T(8,128)(2,1)S(1)}, bf16[256,1024]{1,0:T(8,128)(2,1)S(1)}, u32[]{:S(2)}, u32[]{:S(2)}) collective-permute-start(bf16[256,1024]{1,0:T(8,128)(2,1)S(1)} %bitcast.27), channel_id=1, source_target_pairs={{0,1},{1,0},{2,3},{3,2},{4,5},{5,4},{6,7},{7,6},{8,9},{9,8},{10,11... | collective-permute-start | bytes 1572872 | tf_op jit(solution)/shard_map/ppermute | solution.py:106
  19.1 40.7 %collective-permute-start.1 = (bf16[256,1024]{1,0:T(8,128)(2,1)S(1)}, bf16[256,1024]{1,0:T(8,128)(2,1)S(1)}, u32[]{:S(2)}, u32[]{:S(2)}) collective-permute-start(bf16[256,1024]{1,0:T(8,128)(2,1)S(1)} %bitcast.28), channel_id=1, source_target_pairs={{0,384},{384,0},{1,385},{385,1},{2,386},{386,2},{3,387},{387,3},{4... | collective-permute-start | bytes 1572872 | tf_op jit(solution)/shard_map/ppermute | solution.py:107
  27.6 33.8 %collective-permute-start.2 = (bf16[256,1024]{1,0:T(8,128)(2,1)S(1)}, bf16[256,1024]{1,0:T(8,128)(2,1)}, u32[]{:S(2)}, u32[]{:S(2)}) collective-permute-start(bf16[256,1024]{1,0:T(8,128)(2,1)S(1)} %bitcast.29), channel_id=1, source_target_pairs={{0,385},{1,384},{384,1},{385,0},{2,387},{3,386},{386,3},{387,2},{4... | collective-permute-start | bytes 1572872 | tf_op jit(solution)/shard_map/ppermute | solution.py:108
  59.8 0.8 copy-start.2
  60.6 0.8 copy-start.3
  61.4 4.6 %copy-start = (bf16[8,64,1024]{2,1,0:T(8,128)(2,1)}, bf16[8,64,1024]{2,1,0:T(8,128)(2,1)S(1)}, u32[]{:S(2)}) copy-start(bf16[8,64,1024]{2,1,0:T(8,128)(2,1)S(1)} %all-to-all-done.mine) | copy-start | bytes 3145732
  61.5 4.6 %collective-permute-start.3 = (bf16[8,64,1024]{2,1,0:T(8,128)(2,1)S(1)}, bf16[8,64,1024]{2,1,0:T(8,128)(2,1)S(1)}, u32[]{:S(2)}, u32[]{:S(2)}) collective-permute-start(bf16[8,64,1024]{2,1,0:T(8,128)(2,1)S(1)} %all-to-all-done.mine), channel_id=1, source_target_pairs={{0,2},{2,0},{1,3},{3,1},{4,6},{6,4},{5,7},{7,5},{8,10},{10,8},{9,1... | collective-permute-start | bytes 3145736 | tf_op jit(solution)/shard_map/ppermute | solution.py:119
Sparse Core Ops, SparseCore 0:
  9.8 71.4 all-gather.4

commit v9 on v7

--- a/solution.py
+++ b/solution.py
@@ -14,6 +14,11 @@
 NT = (((1,), (1,)), ((), ()))
 VMEM_BYTES = 24 * 1024 * 1024
 PARTS = (512, 1024)
+
+
+def copy_kernel(head, copies):
+    for y in range(copies.shape[0]):
+        copies[y] = head[...]
 
 
 def passage_kernel(core, mine, other, p0, p1, p2, p3, keys, full, proj, head_buf, piece_buf, sems):
@@ -109,7 +114,17 @@
         lax.ppermute(passages, "xh", flip),
         lax.ppermute(passages, ("xh", "xl"), both),
     ]
-    mine = lax.all_to_all(jnp.broadcast_to(head, (steps,) + head.shape), "y", 0, 0)
+    mine = lax.all_to_all(
+        pl.pallas_call(
+            copy_kernel,
+            out_shape=jax.ShapeDtypeStruct((steps,) + head.shape, head.dtype),
+            in_specs=[pl.BlockSpec(memory_space=pltpu.VMEM)],
+            out_specs=pl.BlockSpec(memory_space=pltpu.VMEM),
+        )(head),
+        "y",
+        0,
+        0,
+    )
     slots = negative_ids.shape[2]
     alive = lax.broadcasted_iota(jnp.int32, (1, slots), 1) < negative_count
     listed = jnp.where(alive, negative_ids[0], -1)

time: 111 us -> 111 us (level)
  local copies, waits for them, and re-layouts: 3.63 us -> 1.62 us
  Pallas kernels: 13.1 us -> 15 us
    broadcast_in_dim x1 -> x0, local copies, waits for them, and re-layouts: 2.01 us -> none  [local(): jnp.broadcast_to(head, (steps,) + head.shape)]
    pallas_call x0 -> x1, Pallas kernels: none -> 1.95 us  [local(): pl.pallas_call(copy_kernel, out_shape=jax.ShapeDtypeStruct((steps,) + hea...]
  transfers between devices with their start and end apart: 6 -> 6, of which waited for: 2 -> 2; matrix products, arithmetic and copies ran while one was open for 2% -> 1% of each run, Pallas kernels for 6% -> 8%
where the time goes in v9:
time: 111 us
  blocking collectives  45.2 us (41%)
  starting transfers between devices  22.2 us (20%)
  Pallas kernels  15 us (14%)
  between operations  14.2 us (13%)
  waiting for transfers between devices  11 us (10%)
  local copies, waits for them, and re-layouts  1.62 us (1%)
  other arithmetic  1.22 us (1%)
    all_gather x1, blocking collectives, local(): met_lists = lax.all_gather(packed, 'z')  29.6 us
    all_to_all x1, blocking collectives, local(): home = lax.all_to_all(stats, 'z', 0, 0)  15.7 us
    ppermute x1, starting transfers between devices, local(): lax.ppermute(passages, 'xh', flip)  8.5 us
    all_gather x1, waiting for transfers between devices, local(): gathered = lax.all_gather(queries, 'z', axis=0, tiled=True)  8.37 us
    all_to_all x1, starting transfers between devices, local(): lax.all_to_all(pl.pallas_call(copy_kernel, out_shape=jax.ShapeDtypeStruct...  7.1 us
    pallas_call x1, Pallas kernels, local(): pl.pallas_call(functools.partial(query_kernel, scale), out_shape=jax.Shap...  6.65 us
    pallas_call x1, Pallas kernels, local(): pl.pallas_call(passage_kernel, out_shape=jax.ShapeDtypeStruct((width, wid...  6.4 us
    ppermute x1, starting transfers between devices, local(): lax.ppermute(passages, 'xl', flip)  2.74 us
  transfers between devices with their start and end apart: 6, of which 2 were waited for; matrix products, arithmetic and copies ran while one was open for 1% of the time, Pallas kernels for 8%

profile of v9, /device:TPU:6, one launch (start us, length us, event | category | flops | bytes accessed | tf_op | source)
XLA Modules:
  0.0 110.5 jit_solution(14260780654039385395)
XLA Ops:
  6.5 0.7 all-gather.5.cloned.1.call-update
  7.3 2.0 %shard_map.64 = bf16[8,64,1024]{2,1,0:T(8,128)(2,1)} custom-call(bf16[64,1024]{1,0:T(8,128)(2,1)} %head.1), custom_call_target="tpu_custom_call" | custom-call | tf_op jit(solution)/shard_map/pallas_call | solution.py:118
  9.2 7.1 %all-to-all-start = ((bf16[8,64,1024]{2,1,0:T(8,128)(2,1)}), bf16[8,64,1024]{2,1,0:T(8,128)(2,1)S(1)}, u32[]{:S(2)}, u32[]{:S(2)}) async-start(bf16[8,64,1024]{2,1,0:T(8,128)(2,1)} %shard_map.64), calls=%async_computation | async-start | bytes 2097152 | tf_op jit(solution)/shard_map/all_to_all | solution.py:117
  16.3 0.0 copy-done.1
  16.3 2.7 %collective-permute-start = (bf16[256,1024]{1,0:T(8,128)(2,1)S(1)}, bf16[256,1024]{1,0:T(8,128)(2,1)S(1)}, u32[]{:S(2)}, u32[]{:S(2)}) collective-permute-start(bf16[256,1024]{1,0:T(8,128)(2,1)S(1)} %bitcast.27), channel_id=1, source_target_pairs={{0,1},{1,0},{2,3},{3,2},{4,5},{5,4},{6,7},{7,6},{8,9},{9,8},{10,11... | collective-permute-start | bytes 1572872 | tf_op jit(solution)/shard_map/ppermute | solution.py:113
  19.1 8.5 %collective-permute-start.1 = (bf16[256,1024]{1,0:T(8,128)(2,1)S(1)}, bf16[256,1024]{1,0:T(8,128)(2,1)S(1)}, u32[]{:S(2)}, u32[]{:S(2)}) collective-permute-start(bf16[256,1024]{1,0:T(8,128)(2,1)S(1)} %bitcast.28), channel_id=1, source_target_pairs={{0,384},{384,0},{1,385},{385,1},{2,386},{386,2},{3,387},{387,3},{4... | collective-permute-start | bytes 1572872 | tf_op jit(solution)/shard_map/ppermute | solution.py:114
  27.6 1.9 %collective-permute-start.2 = (bf16[256,1024]{1,0:T(8,128)(2,1)S(1)}, bf16[256,1024]{1,0:T(8,128)(2,1)}, u32[]{:S(2)}, u32[]{:S(2)}) collective-permute-start(bf16[256,1024]{1,0:T(8,128)(2,1)S(1)} %bitcast.29), channel_id=1, source_target_pairs={{0,385},{1,384},{384,1},{385,0},{2,387},{3,386},{386,3},{387,2},{4... | collective-permute-start | bytes 1572872 | tf_op jit(solution)/shard_map/ppermute | solution.py:115
  30.2 29.6 %all-gather.2 = s32[12,2,128]{2,1,0:T(2,128)S(1)} all-gather(s32[1,2,128]{2,1,0:T(2,128)S(1)} %fusion.5), channel_id=2, replica_groups=mesh['xh'=2,'z'=12,'y'=8,'core'=2,'xl'=2] {'z'}, dimensions={0}, use_global_device_ids=true | all-gather | bytes 13312 | tf_op jit(solution)/shard_map/all_gather | solution.py:134
  59.8 0.0 collective-permute-done.p1
  59.8 0.0 collective-permute-done.1.p2
  59.8 0.8 copy-done.2
  60.6 0.8 copy-done.3
  61.4 0.0 collective-permute-done.2.p3
  61.4 0.0 all-to-all-done.mine
  61.4 1.9 %collective-permute-start.3 = (bf16[8,64,1024]{2,1,0:T(8,128)(2,1)S(1)}, bf16[8,64,1024]{2,1,0:T(8,128)(2,1)S(1)}, u32[]{:S(2)}, u32[]{:S(2)}) collective-permute-start(bf16[8,64,1024]{2,1,0:T(8,128)(2,1)S(1)} %all-to-all-done.mine), channel_id=1, source_target_pairs={{0,2},{2,0},{1,3},{3,1},{4,6},{6,4},{5,7},{7,5},{8,10},{10,8},{9,1... | collective-permute-start | bytes 3145736 | tf_op jit(solution)/shard_map/ppermute | solution.py:136
  63.4 0.1 compare_reduce_fusion.1
  63.5 0.4 compare_reduce_fusion
  63.9 0.1 and_select_fusion.3.target
  64.0 2.0 %collective-permute-done.3.other = bf16[8,64,1024]{2,1,0:T(8,128)(2,1)S(1)} collective-permute-done((bf16[8,64,1024]{2,1,0:T(8,128)(2,1)S(1)}, bf16[8,64,1024]{2,1,0:T(8,128)(2,1)S(1)}, u32[]{:S(2)}, u32[]{:S(2)}) %collective-permute-start.3) | collective-permute-done | bytes 1048608 | tf_op jit(solution)/shard_map/ppermute | solution.py:136
  65.9 6.4 %shard_map.65.keys = bf16[1024,1024]{1,0:T(8,128)(2,1)S(1)} custom-call(s32[1]{0:T(128)} %bitcast.7.core, bf16[8,64,1024]{2,1,0:T(8,128)(2,1)} %copy-done, bf16[8,64,1024]{2,1,0:T(8,128)(2,1)S(1)} %collective-permute-done.3.other, bf16[256,1024]{1,0:T(8,128)(2,1)} %bitcast.26, bf16[256,1024]{1,0:T(8,128)(2,1)} %copy-done.2, bf16[256,1024]{1,0:T(8,128)(2,1)} %copy-done.3, ...), custom_call_target="tpu_custom_call" | custom-call | tf_op jit(solution)/shard_map/pallas_call | solution.py:143
  72.4 8.4 %all-gather.5.cloned.1.call-done = bf16[1,1536,1024]{2,1,0:T(8,128)(2,1)} async-done(((bf16[1,128,1024]{2,1,0:T(8,128)(2,1)}), bf16[1,1536,1024]{2,1,0:T(8,128)(2,1)}) %all-gather.5.cloned.1.call-update) | async-done | bytes 3145744 | tf_op jit(solution)/shard_map/all_gather | solution.py:109
  80.7 6.7 %shard_map.66 = f32[12,2,128]{2,1,0:T(2,128)S(1)} custom-call(s32[12,8]{1,0:T(8,128)S(1)} %convert_element_type.6.used, bf16[1536,1024]{1,0:T(8,128)(2,1)} %bitcast.25, bf16[1024,1024]{1,0:T(8,128)(2,1)S(1)} %shard_map.65.keys, s32[12,1,128]{2,1,0:T(1,128)S(1)} %and_select_fusion.3.target), custom_call_target="tpu_custom_call" | custom-call | tf_op jit(solution)/shard_map/pallas_call | solution.py:174
  87.4 15.7 %all_to_all.10 = f32[12,2,128]{2,1,0:T(2,128)S(1)} all-to-all(f32[12,2,128]{2,1,0:T(2,128)S(1)} %shard_map.66), channel_id=1, replica_groups=mesh['xh'=2,'z'=12,'y'=8,'core'=2,'xl'=2] {'z'}, dimensions={0} | all-to-all | bytes 24576 | tf_op jit(solution)/shard_map/all_to_all | solution.py:187
  103.1 0.5 subtract_bitcast_fusion
  (22 shorter events, 0.1 us)
Async XLA Ops:
  6.5 9.8 %copy-start.1 = (bf16[1,256,1024]{2,1,0:T(8,128)(2,1)S(1)}, bf16[1,256,1024]{2,1,0:T(8,128)(2,1)}, u32[]{:S(2)}) copy-start(bf16[1,256,1024]{2,1,0:T(8,128)(2,1)} %param.7) | copy-start | bytes 1572868
  6.5 23.6 %copy-start.5 = (s32[1,1,12]{2,1,0:T(1,128)S(1)}, s32[1,1,12]{2,1,0:T(1,128)}, u32[]{:S(2)}) copy-start(s32[1,1,12]{2,1,0:T(1,128)} %param.10) | copy-start | bytes 148
  6.5 23.6 %copy-start.4 = (s32[1,128]{1,0:T(1,128)S(1)}, s32[1,128]{1,0:T(1,128)}, u32[]{:S(2)}) copy-start(s32[1,128]{1,0:T(1,128)} %param.9) | copy-start | bytes 1540
  6.5 74.2 %all-gather.5.cloned.1.call-start = ((), (), s32[]{:S(2)}) async-start(), calls=%async_computation.2 | async-start | bytes 3407872 | tf_op jit(solution)/shard_map/all_gather | solution.py:109
  9.2 52.2 %all-to-all-start = ((bf16[8,64,1024]{2,1,0:T(8,128)(2,1)}), bf16[8,64,1024]{2,1,0:T(8,128)(2,1)S(1)}, u32[]{:S(2)}, u32[]{:S(2)}) async-start(bf16[8,64,1024]{2,1,0:T(8,128)(2,1)} %shard_map.64), calls=%async_computation | async-start | bytes 2097152 | tf_op jit(solution)/shard_map/all_to_all | solution.py:117
  16.3 43.5 %collective-permute-start = (bf16[256,1024]{1,0:T(8,128)(2,1)S(1)}, bf16[256,1024]{1,0:T(8,128)(2,1)S(1)}, u32[]{:S(2)}, u32[]{:S(2)}) collective-permute-start(bf16[256,1024]{1,0:T(8,128)(2,1)S(1)} %bitcast.27), channel_id=1, source_target_pairs={{0,1},{1,0},{2,3},{3,2},{4,5},{5,4},{6,7},{7,6},{8,9},{9,8},{10,11... | collective-permute-start | bytes 1572872 | tf_op jit(solution)/shard_map/ppermute | solution.py:113
  19.1 40.7 %collective-permute-start.1 = (bf16[256,1024]{1,0:T(8,128)(2,1)S(1)}, bf16[256,1024]{1,0:T(8,128)(2,1)S(1)}, u32[]{:S(2)}, u32[]{:S(2)}) collective-permute-start(bf16[256,1024]{1,0:T(8,128)(2,1)S(1)} %bitcast.28), channel_id=1, source_target_pairs={{0,384},{384,0},{1,385},{385,1},{2,386},{386,2},{3,387},{387,3},{4... | collective-permute-start | bytes 1572872 | tf_op jit(solution)/shard_map/ppermute | solution.py:114
  27.6 33.8 %collective-permute-start.2 = (bf16[256,1024]{1,0:T(8,128)(2,1)S(1)}, bf16[256,1024]{1,0:T(8,128)(2,1)}, u32[]{:S(2)}, u32[]{:S(2)}) collective-permute-start(bf16[256,1024]{1,0:T(8,128)(2,1)S(1)} %bitcast.29), channel_id=1, source_target_pairs={{0,385},{1,384},{384,1},{385,0},{2,387},{3,386},{386,3},{387,2},{4... | collective-permute-start | bytes 1572872 | tf_op jit(solution)/shard_map/ppermute | solution.py:115
  59.8 0.8 copy-start.2
  60.6 0.8 copy-start.3
  61.4 4.6 %copy-start = (bf16[8,64,1024]{2,1,0:T(8,128)(2,1)}, bf16[8,64,1024]{2,1,0:T(8,128)(2,1)S(1)}, u32[]{:S(2)}) copy-start(bf16[8,64,1024]{2,1,0:T(8,128)(2,1)S(1)} %all-to-all-done.mine) | copy-start | bytes 3145732
  61.4 4.6 %collective-permute-start.3 = (bf16[8,64,1024]{2,1,0:T(8,128)(2,1)S(1)}, bf16[8,64,1024]{2,1,0:T(8,128)(2,1)S(1)}, u32[]{:S(2)}, u32[]{:S(2)}) collective-permute-start(bf16[8,64,1024]{2,1,0:T(8,128)(2,1)S(1)} %all-to-all-done.mine), channel_id=1, source_target_pairs={{0,2},{2,0},{1,3},{3,1},{4,6},{6,4},{5,7},{7,5},{8,10},{10,8},{9,1... | collective-permute-start | bytes 3145736 | tf_op jit(solution)/shard_map/ppermute | solution.py:136
Sparse Core Ops, SparseCore 0:
  9.8 70.9 all-gather.4
